TPU v7x, 32 devices: a whole 2x2x4 slice. The times are simulated.
32 devices in a mesh: fsdp: 4 (over y, x), ctx: 4 (over z), tp: 2 (over core).
Axes of the slice: x: 2, y: 2, z: 4, core: 2. Of those that a mesh axis runs over, the one named last changes fastest.
Arguments:
- tokens: bfloat16 [8, 2048, 896], P('fsdp', 'ctx'), may hold values from -6 to 6
- cotangent: bfloat16 [8, 2048, 896], P('fsdp', 'ctx'), may hold values from -6 to 6
- segments: int32 [8, 2048], P('fsdp'), may hold values from 0 to 3, as said below
- positions: int32 [8, 2048], P('fsdp', 'ctx'), may hold values from 0 to 2044, as said below
- norm_one: bfloat16 [896], replicated, may hold values from 0.5 to 1.5
- qkv_weight: bfloat16 [896, 2, 576], P(('fsdp', 'ctx'), 'tp'), may hold values from -0.1875 to 0.1875
- qkv_bias: bfloat16 [2, 576], P('tp'), may hold values from -3 to 3
- out_weight: bfloat16 [896, 896], P(('fsdp', 'ctx'), 'tp'), may hold values from -0.75 to 0.75
- norm_two: bfloat16 [896], replicated, may hold values from 0.5 to 1.5
- gate_weight: bfloat16 [896, 4864], P(('fsdp', 'ctx'), 'tp'), may hold values from -0.1875 to 0.1875
- up_weight: bfloat16 [896, 4864], P(('fsdp', 'ctx'), 'tp'), may hold values from -0.1875 to 0.1875
- down_weight: bfloat16 [896, 4864], P(('fsdp', 'ctx'), 'tp'), may hold values from -0.078125 to 0.078125
Outputs:
- block_out: bfloat16 [8, 2048, 896], P('fsdp', ('ctx', 'tp'))
- input_grad: float32 [8, 2048, 896], P('fsdp', 'ctx')
- norm_one_grad: float32 [896], replicated
- qkv_weight_grad: float32 [896, 2, 576], P(('fsdp', 'ctx'), 'tp')
- qkv_bias_grad: float32 [2, 576], P('tp')
- out_weight_grad: float32 [896, 896], P(('fsdp', 'ctx'), 'tp')
- norm_two_grad: float32 [896], replicated
- gate_weight_grad: float32 [896, 4864], P(('fsdp', 'ctx'), 'tp')
- up_weight_grad: float32 [896, 4864], P(('fsdp', 'ctx'), 'tp')
- down_weight_grad: float32 [896, 4864], P(('fsdp', 'ctx'), 'tp')
Inputs may be any that keep to these rules, and one draw needn't show every extreme that they name: `segments`: each sequence holds exactly 4 documents, numbered from 0 in order, each a contiguous run; the first token is document 0. `positions`: each token's offset from the first token of its document; the largest is reached in every draw.
All inputs are finite; a program needn't handle non-finite values.
Results may differ from a plain program's by a relative error of at most 0.02.
Values may be sent and summed in bfloat16 or wider, within the bound.
No kernel may reach another device: no remote copies, remote signals or barrier semaphores. Data moves between devices by JAX's collectives and lax.ppermute only.
A program may use at most 256 MiB of HBM per device.

v0:
```python
import jax
import jax.numpy as jnp
from jax import lax
from jax.sharding import PartitionSpec as P

HD = 64
GROUP = 7


epsilon = 1e-06
rope_base = 1000000.0
masked_value = -1e30
contract_rows = (((0,), (0,)), ((), ()))
contract_last = (((1,), (1,)), ((), ()))


def rotary_tables(positions):
    half_dim = HD // 2
    frequency = rope_base ** (-(jnp.arange(half_dim, dtype=jnp.float32) * 2.0) / HD)
    angles = positions.astype(jnp.float32)[..., None] * frequency
    cosine = jnp.cos(angles)
    sine_table = jnp.sin(angles)
    return (jnp.concatenate([cosine, cosine], -1), jnp.concatenate([sine_table, sine_table], -1))


def rotate(values, cosine, sine_table):
    half_dim = values.shape[-1] // 2
    turned = jnp.concatenate([-values[..., half_dim:], values[..., :half_dim]], -1)
    return values * cosine + turned * sine_table


def masked_scores(query_one, key_one, own_segment, all_segments, first_row):
    raw_scores = jnp.einsum(
        "qhgd,khd->hgqk", query_one, key_one, preferred_element_type=jnp.float32
    ) * HD ** (-0.5)
    query_index = first_row + jnp.arange(own_segment.shape[0], dtype=jnp.int32)
    key_index = jnp.arange(all_segments.shape[0], dtype=jnp.int32)
    allowed = (own_segment[:, None] == all_segments[None, :]) & (
        key_index[None, :] <= query_index[:, None]
    )
    return jnp.where(allowed, raw_scores, masked_value)


def shards(
    tokens,
    cotangent,
    segments,
    positions,
    norm_one,
    qkv_weight,
    qkv_bias,
    out_weight,
    norm_two,
    gate_weight,
    up_weight,
    down_weight,
):
    seq_count, block_len, model_width = tokens.shape
    row_count = seq_count * block_len
    kv_local = qkv_weight.shape[1]
    per_group = qkv_weight.shape[2]
    q_width = out_weight.shape[1]
    first_row = lax.axis_index("ctx") * block_len
    half_len = block_len // lax.axis_size("tp")
    half_start = lax.axis_index("tp") * half_len

    def own_rows(values):
        return lax.dynamic_slice_in_dim(values, half_start, half_len, 1)

    attention_full = (
        lax.all_gather(qkv_weight, ("fsdp", "ctx"), axis=0, tiled=True),
        lax.all_gather(out_weight, ("fsdp", "ctx"), axis=0, tiled=True),
    )
    qkv_full = attention_full[0].reshape(model_width, kv_local * per_group)
    out_full = attention_full[1]
    inputs_block = tokens.astype(jnp.float32)
    inputs = inputs_block.reshape(row_count, model_width)
    gain_one = norm_one.astype(jnp.float32)
    scale_one = lax.rsqrt(jnp.mean(inputs * inputs, -1, keepdims=True) + epsilon)
    unit_one = inputs * scale_one
    normed = (unit_one * gain_one).astype(jnp.bfloat16)
    projected = jnp.dot(normed, qkv_full, preferred_element_type=jnp.float32) + qkv_bias.astype(
        jnp.float32
    )
    grouped = projected.reshape(seq_count, block_len, kv_local, GROUP + 2, HD)
    cosine, sine_table = rotary_tables(positions)
    queries = rotate(
        grouped[:, :, :, :GROUP], cosine[:, :, None, None], sine_table[:, :, None, None]
    ).astype(jnp.bfloat16)
    key_rows = rotate(grouped[:, :, :, GROUP], cosine[:, :, None], sine_table[:, :, None]).astype(
        jnp.bfloat16
    )
    values = grouped[:, :, :, GROUP + 1].astype(jnp.bfloat16)
    kv_pack = jnp.concatenate([key_rows, values], -1)
    kv_all = lax.all_gather(kv_pack, "ctx", axis=1, tiled=True)
    own_segments = lax.dynamic_slice_in_dim(segments, first_row, block_len, 1)

    def attend(pieces):
        query_one, pack_one, own_segment, all_segments = pieces
        masked = masked_scores(query_one, pack_one[..., :HD], own_segment, all_segments, first_row)
        row_max = jnp.max(masked, -1, keepdims=True)
        exponent = jnp.exp(masked - row_max)
        row_total = jnp.sum(exponent, -1, keepdims=True)
        probability = (exponent / row_total).astype(jnp.bfloat16)
        result = jnp.einsum(
            "hgqk,khd->qhgd", probability, pack_one[..., HD:], preferred_element_type=jnp.float32
        )
        return (result, row_max + jnp.log(row_total))

    attended, log_totals = lax.map(attend, (queries, kv_all, own_segments, segments))
    mixed = attended.reshape(row_count, q_width).astype(jnp.bfloat16)
    branch_part = lax.dot_general(
        mixed, out_full, contract_last, preferred_element_type=jnp.float32
    )
    attention_sum = lax.psum_scatter(
        branch_part.reshape(seq_count, block_len, model_width).astype(jnp.bfloat16),
        "tp",
        scatter_dimension=1,
        tiled=True,
    ).astype(jnp.float32)
    middle = own_rows(inputs_block) + attention_sum
    feed_full = (
        lax.all_gather(gate_weight, ("fsdp", "ctx"), axis=0, tiled=True),
        lax.all_gather(up_weight, ("fsdp", "ctx"), axis=0, tiled=True),
        lax.all_gather(down_weight, ("fsdp", "ctx"), axis=0, tiled=True),
    )
    gate_full, up_full, down_full = feed_full
    gain_two = norm_two.astype(jnp.float32)
    scale_two = lax.rsqrt(jnp.mean(middle * middle, -1, keepdims=True) + epsilon)
    unit_two = middle * scale_two
    normed_two_half = (unit_two * gain_two).astype(jnp.bfloat16)
    normed_two = lax.all_gather(normed_two_half, "tp", axis=1, tiled=True).reshape(
        row_count, model_width
    )
    gate_act = jnp.dot(normed_two, gate_full, preferred_element_type=jnp.float32)
    up_act = jnp.dot(normed_two, up_full, preferred_element_type=jnp.float32)
    silu_gate = jax.nn.silu(gate_act)
    hidden = (silu_gate * up_act).astype(jnp.bfloat16)
    feed_part = lax.dot_general(
        hidden, down_full, contract_last, preferred_element_type=jnp.float32
    )
    feed_sum = lax.psum_scatter(
        feed_part.reshape(seq_count, block_len, model_width).astype(jnp.bfloat16),
        "tp",
        scatter_dimension=1,
        tiled=True,
    ).astype(jnp.float32)
    block_out = (middle + feed_sum).astype(jnp.bfloat16)
    attention_back = (
        lax.all_gather(qkv_weight, ("fsdp", "ctx"), axis=0, tiled=True),
        lax.all_gather(out_weight, ("fsdp", "ctx"), axis=0, tiled=True),
    )
    feed_back = (
        lax.all_gather(gate_weight, ("fsdp", "ctx"), axis=0, tiled=True),
        lax.all_gather(up_weight, ("fsdp", "ctx"), axis=0, tiled=True),
        lax.all_gather(down_weight, ("fsdp", "ctx"), axis=0, tiled=True),
    )
    qkv_back = attention_back[0].reshape(model_width, kv_local * per_group)
    out_back = attention_back[1]
    gate_back, up_back, down_back = feed_back
    upstream_low = cotangent.reshape(row_count, model_width)
    upstream_half = own_rows(cotangent).astype(jnp.float32)
    hidden_grad = jnp.dot(upstream_low, down_back, preferred_element_type=jnp.float32)
    down_weight_grad = lax.dot_general(
        upstream_low, hidden, contract_rows, preferred_element_type=jnp.float32
    )
    sigmoid = jax.nn.sigmoid(gate_act)
    gate_grad = (hidden_grad * up_act * (sigmoid * (1.0 + gate_act * (1.0 - sigmoid)))).astype(
        jnp.bfloat16
    )
    up_grad = (hidden_grad * silu_gate).astype(jnp.bfloat16)
    normed_two_part = lax.dot_general(
        gate_grad, gate_back, contract_last, preferred_element_type=jnp.float32
    )
    normed_two_part = normed_two_part + lax.dot_general(
        up_grad, up_back, contract_last, preferred_element_type=jnp.float32
    )
    gate_weight_grad = lax.dot_general(
        normed_two, gate_grad, contract_rows, preferred_element_type=jnp.float32
    )
    up_weight_grad = lax.dot_general(
        normed_two, up_grad, contract_rows, preferred_element_type=jnp.float32
    )
    feed_grads = (
        lax.psum_scatter(gate_weight_grad, ("fsdp", "ctx"), scatter_dimension=0, tiled=True),
        lax.psum_scatter(up_weight_grad, ("fsdp", "ctx"), scatter_dimension=0, tiled=True),
        lax.psum_scatter(down_weight_grad, ("fsdp", "ctx"), scatter_dimension=0, tiled=True),
    )
    normed_two_grad = lax.psum_scatter(
        normed_two_part.reshape(seq_count, block_len, model_width).astype(jnp.bfloat16),
        "tp",
        scatter_dimension=1,
        tiled=True,
    ).astype(jnp.float32)
    gain_two_grad = jnp.sum(normed_two_grad * unit_two, (0, 1))
    scaled_two = normed_two_grad * gain_two
    middle_grad = upstream_half + scale_two * (
        scaled_two - unit_two * jnp.mean(scaled_two * unit_two, -1, keepdims=True)
    )
    branch_half = middle_grad.astype(jnp.bfloat16)
    branch_low = lax.all_gather(branch_half, "tp", axis=1, tiled=True).reshape(
        row_count, model_width
    )
    mixed_grad = jnp.dot(branch_low, out_back, preferred_element_type=jnp.float32).astype(
        jnp.bfloat16
    )
    out_weight_grad = lax.dot_general(
        branch_low, mixed, contract_rows, preferred_element_type=jnp.float32
    )
    mixed_heads = mixed_grad.reshape(seq_count, block_len, kv_local, GROUP, HD)

    def attend_back(pieces):
        query_one, pack_one, own_segment, all_segments, log_one, grad_one = pieces
        key_one = pack_one[..., :HD]
        value_one = pack_one[..., HD:]
        masked = masked_scores(query_one, key_one, own_segment, all_segments, first_row)
        probability = jnp.exp(masked - log_one)
        value_grad = jnp.einsum(
            "hgqk,qhgd->khd",
            probability.astype(jnp.bfloat16),
            grad_one,
            preferred_element_type=jnp.float32,
        )
        prob_grad = jnp.einsum(
            "qhgd,khd->hgqk", grad_one, value_one, preferred_element_type=jnp.float32
        )
        centre = jnp.sum(probability * prob_grad, -1, keepdims=True)
        score_grad = (probability * (prob_grad - centre)).astype(jnp.bfloat16)
        query_grad = jnp.einsum(
            "hgqk,khd->qhgd", score_grad, key_one, preferred_element_type=jnp.float32
        ) * HD ** (-0.5)
        key_grad = jnp.einsum(
            "hgqk,qhgd->khd", score_grad, query_one, preferred_element_type=jnp.float32
        ) * HD ** (-0.5)
        return (query_grad, jnp.concatenate([key_grad, value_grad], -1))

    query_grads, pack_grads = lax.map(
        attend_back, (queries, kv_all, own_segments, segments, log_totals, mixed_heads)
    )
    pack_sum = lax.psum_scatter(
        pack_grads.astype(jnp.bfloat16), "ctx", scatter_dimension=1, tiled=True
    ).astype(jnp.float32)
    query_turned = rotate(query_grads, cosine[:, :, None, None], -sine_table[:, :, None, None])
    key_turned = rotate(pack_sum[..., :HD], cosine[:, :, None], -sine_table[:, :, None])
    grouped_grad = jnp.concatenate(
        [query_turned, key_turned[:, :, :, None], pack_sum[:, :, :, None, HD:]], 3
    )
    projected_grad = grouped_grad.reshape(row_count, kv_local * per_group).astype(jnp.bfloat16)
    bias_grad = jnp.sum(projected_grad.astype(jnp.float32), 0).reshape(kv_local, per_group)
    normed_one_part = lax.dot_general(
        projected_grad, qkv_back, contract_last, preferred_element_type=jnp.float32
    )
    qkv_weight_grad = lax.dot_general(
        normed, projected_grad, contract_rows, preferred_element_type=jnp.float32
    )
    qkv_shaped = qkv_weight_grad.reshape(model_width, kv_local, per_group)
    attention_grads = (
        lax.psum_scatter(qkv_shaped, ("fsdp", "ctx"), scatter_dimension=0, tiled=True),
        lax.psum_scatter(out_weight_grad, ("fsdp", "ctx"), scatter_dimension=0, tiled=True),
    )
    normed_one_grad = lax.psum_scatter(
        normed_one_part.reshape(seq_count, block_len, model_width).astype(jnp.bfloat16),
        "tp",
        scatter_dimension=1,
        tiled=True,
    ).astype(jnp.float32)
    unit_one_half = own_rows(unit_one.reshape(seq_count, block_len, model_width))
    scale_one_half = own_rows(scale_one.reshape(seq_count, block_len, 1))
    gain_one_grad = jnp.sum(normed_one_grad * unit_one_half, (0, 1))
    scaled_one = normed_one_grad * gain_one
    input_half = middle_grad + scale_one_half * (
        scaled_one - unit_one_half * jnp.mean(scaled_one * unit_one_half, -1, keepdims=True)
    )
    gain_pair = jnp.stack([gain_one_grad, gain_two_grad])[None]
    gathered = (
        lax.all_gather(input_half.astype(jnp.bfloat16), "tp", axis=1, tiled=True).astype(
            input_half.dtype
        ),
        lax.all_gather(gain_pair.astype(jnp.bfloat16), "tp", axis=0, tiled=True).astype(
            gain_pair.dtype
        ),
    )
    input_grad = gathered[0]
    gain_total = jnp.sum(gathered[1], 0)
    small_grads = lax.psum((gain_total, bias_grad), ("fsdp", "ctx"))
    return (
        block_out,
        input_grad,
        small_grads[0][0],
        attention_grads[0],
        small_grads[1],
        attention_grads[1],
        small_grads[0][1],
        feed_grads[0],
        feed_grads[1],
        feed_grads[2],
    )


def solution(mesh):
    return jax.shard_map(
        shards,
        mesh=mesh,
        in_specs=(
            P("fsdp", "ctx", None),
            P("fsdp", "ctx", None),
            P("fsdp", None),
            P("fsdp", "ctx"),
            P(),
            P(("fsdp", "ctx"), "tp", None),
            P("tp", None),
            P(("fsdp", "ctx"), "tp"),
            P(),
            P(("fsdp", "ctx"), "tp"),
            P(("fsdp", "ctx"), "tp"),
            P(("fsdp", "ctx"), "tp"),
        ),
        out_specs=(
            P("fsdp", ("ctx", "tp"), None),
            P("fsdp", "ctx", None),
            P(),
            P(("fsdp", "ctx"), "tp", None),
            P("tp", None),
            P(("fsdp", "ctx"), "tp"),
            P(),
            P(("fsdp", "ctx"), "tp"),
            P(("fsdp", "ctx"), "tp"),
            P(("fsdp", "ctx"), "tp"),
        ),
        check_vma=False,
    )
```

profile of v0, /device:TPU:0, one launch (start us, length us, event | category | flops | bytes accessed | tf_op | source)
XLA Modules:
  0.0 1616.2 jit_solution(670635166496155173)
XLA Ops:
  10.7 54.7 %all_gather.35 = bf16[896,1,576]{2,0,1:T(8,128)(2,1)S(1)} all-gather(bf16[56,1,576]{2,0,1:T(8,128)(2,1)} %param.21), channel_id=1, replica_groups=mesh['fsdp'=4,'ctx'=4,'tp'=2] {'fsdp','ctx'}, dimensions={0}, use_global_device_ids=true | all-gather | bytes 1096704 | tf_op jit(solution)/shard_map/all_gather | solution.py:71
  84.3 54.7 %all_gather.37 = bf16[896,448]{1,0:T(8,128)(2,1)} all-gather(bf16[56,448]{1,0:T(8,128)(2,1)S(1)} %copy-done.37), channel_id=1, replica_groups=mesh['fsdp'=4,'ctx'=4,'tp'=2] {'fsdp','ctx'}, dimensions={0}, use_global_device_ids=true | all-gather | bytes 852992 | tf_op jit(solution)/shard_map/all_gather | solution.py:72
  139.0 81.7 %while.26 = (s32[]{:T(128)}, bf16[2,512,1,7,64]{1,4,3,2,0:T(8,128)(2,1)}, f32[2,1,7,512,1]{3,2,4,1,0:T(8,128)S(1)}, bf16[2,2048,1,128]{1,3,2,0:T(8,128)(2,1)}, s...) while((s32[]{:T(128)}, ...), condition=%wide.region_4.5_spmd.clone, body=%wide.region_1.4_spmd.sunk.clone | while | flops 1970271232 | bytes 102723752 | solution.py:110
  141.1 11.9 fusion.158
  153.0 12.8 fusion.159
  165.9 13.0 fusion.160
  181.9 11.9 fusion.158
  193.9 12.8 fusion.159
  206.7 13.0 fusion.160
  220.7 4.1 convolution_convert_fusion.2
  227.0 4.4 reduce-scatter.16.cloned.1.call-done
  236.9 9.5 all-gather.10.cloned.1.call-done
  246.4 81.2 %all-gather.14.cloned.1.call-done = bf16[896,2432]{1,0:T(8,128)(2,1)} async-done(((bf16[56,2432]{1,0:T(8,128)(2,1)}), bf16[896,2432]{1,0:T(8,128)(2,1)}) %all-gather.14.cloned.1.call-update) | async-done | bytes 4358160 | tf_op jit(solution)/shard_map/all_gather | solution.py:124
  327.6 10.4 fusion.84
  338.0 68.3 %all-gather.12.cloned.1.call-done = bf16[896,2432]{1,0:T(8,128)(2,1)} async-done(((bf16[56,2432]{1,0:T(8,128)(2,1)}), bf16[896,2432]{1,0:T(8,128)(2,1)}) %all-gather.12.cloned.1.call-update) | async-done | bytes 4358160 | tf_op jit(solution)/shard_map/all_gather | solution.py:123
  406.3 10.5 fusion.83
  416.8 68.2 %all-gather.16.cloned.1.call-done = bf16[896,2432]{1,0:T(8,128)(2,1)} async-done(((bf16[56,2432]{1,0:T(8,128)(2,1)}), bf16[896,2432]{1,0:T(8,128)(2,1)}) %all-gather.16.cloned.1.call-update) | async-done | bytes 4358160 | tf_op jit(solution)/shard_map/all_gather | solution.py:125
  485.0 17.8 %multiply_convert_fusion = (bf16[1024,2432]{1,0:T(8,128)(2,1)}, bf16[1024,2432]{1,0:T(8,128)(2,1)}, bf16[1024,2432]{1,0:T(8,128)(2,1)}) fusion(f32[1024,2432]{1,0:T(8,128)} %fusion.83, f32[1024,2432]{1,0:T(8,128)} %fusion.84, bf16[1024,896]{1,0:T(8,128)(2,1)} %bitcast.347, bf16[896,2432]{1,0:T(8,128)(2,1)} %all-gather.16.cloned.1.call-done), kind=kOutput, calls=%fused_computation.67 | convolution fusion | flops 4500094976 | bytes 41058304 | tf_op jit(solution)/shard_map/dot_general | solution.py:163
  502.8 7.6 fusion.85
  510.4 8.9 add_convert_fusion
  519.4 8.1 reduce-scatter.20.cloned.1.call-done
  531.7 11.5 all-gather.18.cloned.1.call-done
  549.0 188.7 %while.27 = (s32[]{:T(128)}, f32[2,512,1,7,64]{1,4,3,2,0:T(8,128)}, bf16[2,2048,1,128]{1,3,2,0:T(8,128)(2,1)}, bf16[2,2048,1,128]{1,3,2,0:T(8,128)(2,1)}, s32[2,...) while((s32[]{:T(128)}, f32[2,512,1,7,64]{1,4,3,2,0:T(8,128)}, ...), condition=%wide.region_12.13_spmd.clone, body=%wide.region_10.12_spmd.sunk.clone | while | flops 4768363520 | bytes 251635968 | solution.py:237
  551.6 11.8 fusion.167
  563.4 21.3 %fusion.169 = (f32[7,512]{1,0:T(8,128)S(1)}, f32[1,7,512,2048]{2,3,1,0:T(8,128)}) fusion(f32[2048,512,7]{1,0,2:T(8,128)} %fusion.167, f32[7,512]{1,0:T(8,128)S(1)} %dynamic-slice_bitcast_fusion.11, bf16[2,512,1,7,64]{1,4,3,2,0:T(8,128)(2,1)S(1)} %get-tuple-element.480, s32[]{:T(128)S(6)} %copy.121, ...), kind=kOutput, calls=%fused_computation.29.clone.1.clone | convolution fusion | flops 976220672 | bytes 60520452 | tf_op jit(solution)/shard_map/while/body/eval_jaxpr/qhgd,khd->hgqk/dot_general | solution.py:33
  584.7 25.0 %fusion.170 = bf16[7,512,2048]{1,2,0:T(8,128)(2,1)} fusion(f32[1,7,512,2048]{2,3,1,0:T(8,128)} %get-tuple-element.416, f32[2048,512,7]{1,0,2:T(8,128)} %fusion.167, f32[7,512]{1,0:T(8,128)S(1)} %get-tuple-element.417), kind=kLoop, calls=%fused_computation.32.clone.1.clone | loop fusion | flops 22020096 | bytes 73414656 | tf_op jit(solution)/shard_map/reshape.37
  609.7 13.9 fusion.172
  623.6 9.8 fusion.173
  633.4 7.9 fusion.171
  645.6 11.8 fusion.167
  657.4 21.3 %fusion.169 = (f32[7,512]{1,0:T(8,128)S(1)}, f32[1,7,512,2048]{2,3,1,0:T(8,128)}) fusion(f32[2048,512,7]{1,0,2:T(8,128)} %fusion.167, f32[7,512]{1,0:T(8,128)S(1)} %dynamic-slice_bitcast_fusion.11, bf16[2,512,1,7,64]{1,4,3,2,0:T(8,128)(2,1)S(1)} %get-tuple-element.480, s32[]{:T(128)S(6)} %copy.121, ...), kind=kOutput, calls=%fused_computation.29.clone.1.clone | convolution fusion | flops 976220672 | bytes 60520452 | tf_op jit(solution)/shard_map/while/body/eval_jaxpr/qhgd,khd->hgqk/dot_general | solution.py:33
  678.7 25.0 %fusion.170 = bf16[7,512,2048]{1,2,0:T(8,128)(2,1)} fusion(f32[1,7,512,2048]{2,3,1,0:T(8,128)} %get-tuple-element.416, f32[2048,512,7]{1,0,2:T(8,128)} %fusion.167, f32[7,512]{1,0:T(8,128)S(1)} %get-tuple-element.417), kind=kLoop, calls=%fused_computation.32.clone.1.clone | loop fusion | flops 22020096 | bytes 73414656 | tf_op jit(solution)/shard_map/reshape.37
  703.7 13.9 fusion.172
  717.6 9.8 fusion.173
  727.4 7.9 fusion.171
  740.4 25.8 %reduce-scatter.22.cloned.1.call-done = bf16[2,512,1,128]{1,3,2,0:T(8,128)(2,1)} async-done(((bf16[2,2048,1,128]{1,3,2,0:T(8,128)(2,1)}), bf16[2,512,1,128]{1,3,2,0:T(8,128)(2,1)}) %reduce-scatter.22.cloned.1.call-update) | async-done | bytes 262160 | tf_op jit(solution)/shard_map/reduce_scatter | solution.py:240
  773.6 9.6 convolution_convert_fusion.1
  785.9 8.6 reduce-scatter.18.cloned.1.call-done
  794.5 3.8 fusion.56
  798.3 11.9 convolution_bitcast_fusion.1
  813.1 3.7 copy.77
  822.2 11.4 fusion.88
  833.7 10.7 fusion.87
  848.3 48.3 %all-reduce.4 = (f32[2,896]{1,0:T(2,128)S(1)}, f32[1,576]{1,0:T(1,128)}) all-reduce(f32[2,896]{1,0:T(2,128)S(1)} %convert_reduce_fusion.1, f32[1,576]{1,0:T(1,128)S(1)} %reshape.576), channel_id=1, replica_groups=mesh['fsdp'=4,'ctx'=4,'tp'=2] {'fsdp','ctx'}, use_global_device_ids=true, to_apply=%region_19.20 | all-reduce | flops 2368 | bytes 18944 | tf_op jit(solution)/shard_map/psum | solution.py:285
  900.7 243.7 %all-reduce.8.cloned.1.call-done = (f32[896,1,576]{2,1,0:T(1,128)}, f32[896,2432]{0,1:T(8,128)}) async-done(((f32[896,1,576]{2,1,0:T(1,128)}, f32[896,2432]{0,1:T(8,128)}), (f32[896,1,576]{2,1,0:T(1,128)}, f32[896,2432]{0,1:T(8,128)})) %all-reduce.8.cloned.1.call-update) | async-done | bytes 10780688
  1149.3 79.3 %reduce-scatter.26.cloned.1.call-done = f32[56,448]{1,0:T(8,128)} async-done(((f32[896,448]{1,0:T(8,128)}), f32[56,448]{1,0:T(8,128)}) %reduce-scatter.26.cloned.1.call-update) | async-done | bytes 100368 | tf_op jit(solution)/shard_map/reduce_scatter | solution.py:259
  1228.6 190.1 %reduce-scatter.30.cloned.1.call-done = f32[56,2432]{1,0:T(8,128)} async-done(((f32[896,2432]{1,0:T(8,128)}), f32[56,2432]{1,0:T(8,128)}) %reduce-scatter.30.cloned.1.call-update) | async-done | bytes 544784
  1418.8 190.7 %reduce-scatter.28.cloned.1.call-done = f32[56,2432]{1,0:T(8,128)} async-done(((f32[896,2432]{1,0:T(8,128)}), f32[56,2432]{1,0:T(8,128)}) %reduce-scatter.28.cloned.1.call-update) | async-done | bytes 544784
  (248 shorter events, 87.4 us)
Async XLA Ops:
  7.2 58.2 %copy-start.3 = (bf16[2,512,896]{2,1,0:T(8,128)(2,1)S(1)}, bf16[2,512,896]{2,1,0:T(8,128)(2,1)}, u32[]{:S(2)}) copy-start(bf16[2,512,896]{2,1,0:T(8,128)(2,1)} %param.16) | copy-start | bytes 5505028
  7.2 131.8 %all-gather.8.cloned.1.call-start = ((), (), s32[]{:S(2)}) async-start(), calls=%async_computation.8 | async-start | bytes 1310720 | tf_op jit(solution)/shard_map/all_gather | solution.py:95
  8.1 59.7 %copy-start.35 = (f32[896]{0:T(1024)}, f32[896]{0:T(1024)S(1)}, u32[]{:S(2)}) copy-start(f32[896]{0:T(1024)S(1)} %convert_element_type.184) | copy-start | bytes 10756
  10.7 57.0 %copy-start.40 = (f32[2,512]{1,0:T(2,128)}, f32[2,512]{1,0:T(2,128)S(1)}, u32[]{:S(2)}) copy-start(f32[2,512]{1,0:T(2,128)S(1)} %add_rsqrt_fusion) | copy-start | bytes 12292
  71.8 3.5 copy-start.45
  75.2 3.4 copy-start.2
  76.0 5.4 copy-start.21
  76.9 154.5 %reduce-scatter.16.cloned.1.call-start = ((), (), s32[]{:S(2)}) async-start(), calls=%async_computation.9 | async-start | bytes 2752512 | tf_op jit(solution)/shard_map/reduce_scatter | solution.py:115
  83.5 55.5 %copy-start.31 = (f32[2,1,7,512,1]{3,2,4,1,0:T(8,128)S(1)}, f32[2,1,7,512,1]{3,2,4,1,0:T(8,128)}, u32[]{:S(2)}) copy-start(f32[2,1,7,512,1]{3,2,4,1,0:T(8,128)} %custom-call) | copy-start | bytes 86020
  83.5 55.5 %copy-start.32 = (s32[2,512]{1,0:T(2,128)S(1)}, s32[2,512]{1,0:T(2,128)}, u32[]{:S(2)}) copy-start(s32[2,512]{1,0:T(2,128)} %constant_dynamic-slice_fusion.5) | copy-start | bytes 12292
  153.0 12.9 copy-start.13
  193.9 12.9 copy-start.13
  220.7 4.2 copy-start.4
  224.9 21.5 %all-gather.10.cloned.1.call-start = ((), (), s32[]{:S(2)}) async-start(), calls=%async_computation.10 | async-start | bytes 2752512 | tf_op jit(solution)/shard_map/all_gather | solution.py:132
  227.0 303.1 %copy-start.33 = (f32[896]{0:T(1024)}, f32[896]{0:T(1024)S(1)}, u32[]{:S(2)}) copy-start(f32[896]{0:T(1024)S(1)} %convert_element_type.195) | copy-start | bytes 10756
  233.5 296.6 %copy-start = (f32[2,256,896]{2,1,0:T(8,128)}, f32[2,256,896]{2,1,0:T(8,128)S(1)}, u32[]{:S(2)}) copy-start(f32[2,256,896]{2,1,0:T(8,128)S(1)} %get-tuple-element.243) | copy-start | bytes 5505028
  233.5 296.6 %copy-start.38 = (f32[2,256]{1,0:T(2,128)}, f32[2,256]{1,0:T(2,128)S(1)}, u32[]{:S(2)}) copy-start(f32[2,256]{1,0:T(2,128)S(1)} %add_rsqrt_fusion.1) | copy-start | bytes 6148
  234.8 92.8 %all-gather.14.cloned.1.call-start = ((), (), s32[]{:S(2)}) async-start(), calls=%async_computation.12 | async-start | bytes 4630528 | tf_op jit(solution)/shard_map/all_gather | solution.py:124
  235.4 170.9 %all-gather.12.cloned.1.call-start = ((), (), s32[]{:S(2)}) async-start(), calls=%async_computation.11 | async-start | bytes 4630528 | tf_op jit(solution)/shard_map/all_gather | solution.py:123
  236.0 249.0 %all-gather.16.cloned.1.call-start = ((), (), s32[]{:S(2)}) async-start(), calls=%async_computation.13 | async-start | bytes 4630528 | tf_op jit(solution)/shard_map/all_gather | solution.py:125
  236.6 290.9 %reduce-scatter.20.cloned.1.call-start = ((), (), s32[]{:S(2)}) async-start(), calls=%async_computation.15 | async-start | bytes 2752512 | tf_op jit(solution)/shard_map/reduce_scatter | solution.py:189
  485.0 17.8 %copy-start.47 = (bf16[896,2432]{1,0:T(8,128)(2,1)S(1)}, bf16[896,2432]{1,0:T(8,128)(2,1)}, u32[]{:S(2)}) copy-start(bf16[896,2432]{1,0:T(8,128)(2,1)} %all-gather.12.cloned.1.call-done) | copy-start | bytes 13074436
  502.8 7.6 copy-start.51
  519.3 23.8 %all-gather.18.cloned.1.call-start = ((), (), s32[]{:S(2)}) async-start(), calls=%async_computation.16 | async-start | bytes 2752512 | tf_op jit(solution)/shard_map/all_gather | solution.py:201
  531.6 234.6 %reduce-scatter.22.cloned.1.call-start = ((), (), s32[]{:S(2)}) async-start(), calls=%async_computation.17 | async-start | bytes 1310720 | tf_op jit(solution)/shard_map/reduce_scatter | solution.py:240
  623.6 9.8 copy-start.7
  633.4 7.9 copy-start.28
  717.6 9.8 copy-start.7
  727.4 7.9 copy-start.28
  737.8 45.6 %reduce-scatter.24.cloned.1.call-start = ((), (), s32[]{:S(2)}) async-start(), calls=%async_computation.18 | async-start | bytes 2752512 | tf_op jit(solution)/shard_map/reduce_scatter | solution.py:261
  739.8 28.3 %copy-start.22 = (f32[2,512,32]{1,2,0:T(8,128)S(1)}, f32[2,512,32]{1,2,0:T(8,128)}, u32[]{:S(2)}) copy-start(f32[2,512,32]{1,2,0:T(8,128)} %copy-done.21) | copy-start | bytes 393220
  739.8 28.3 %copy-start.24 = (f32[2,512,1,32]{1,3,0,2:T(8,128)S(1)}, f32[2,512,1,32]{1,3,0,2:T(8,128)}, u32[]{:S(2)}) copy-start(f32[2,512,1,32]{1,3,0,2:T(8,128)} %copy-done.23) | copy-start | bytes 393220
  740.4 30.0 %copy-start.26 = (bf16[896,1,576]{2,0,1:T(8,128)(2,1)S(1)}, bf16[896,1,576]{2,0,1:T(8,128)(2,1)}, u32[]{:S(2)}) copy-start(bf16[896,1,576]{2,0,1:T(8,128)(2,1)} %copy-done.25) | copy-start | bytes 3096580
  773.5 21.0 %reduce-scatter.18.cloned.1.call-start = ((), (), s32[]{:S(2)}) async-start(), calls=%async_computation.14 | async-start | bytes 2752512 | tf_op jit(solution)/shard_map/reduce_scatter | solution.py:142
  773.5 9.8 copy-start.41
  773.6 9.8 copy-start.36
  783.2 11.3 copy-start.1
  783.2 11.3 copy-start.6
  783.2 11.3 copy-start.34
  783.2 11.3 copy-start.39
  783.2 11.2 copy-start.43
  783.3 113.9 %all-gather.20.cloned.1.call-start = ((), (), s32[]{:S(2)}) async-start(), calls=%async_computation.19 | async-start | bytes 2752512 | tf_op jit(solution)/shard_map/all_gather | solution.py:276
  798.3 11.9 copy-start.11
  798.3 346.2 %all-reduce.8.cloned.1.call-start = ((), (), s32[]{:S(2)}) async-start(), calls=%async_computation.23 | async-start | bytes 22020096
  816.8 411.8 %reduce-scatter.26.cloned.1.call-start = ((), (), s32[]{:S(2)}) async-start(), calls=%async_computation.20 | async-start | bytes 1949696 | tf_op jit(solution)/shard_map/reduce_scatter | solution.py:259
  819.5 2.7 copy-start.48
  821.9 596.8 %reduce-scatter.30.cloned.1.call-start = ((), (), s32[]{:S(2)}) async-start(), calls=%async_computation.22 | async-start | bytes 9261056
  833.6 775.8 %reduce-scatter.28.cloned.1.call-start = ((), (), s32[]{:S(2)}) async-start(), calls=%async_computation.21 | async-start | bytes 9261056
  (27 other events, 44.6 us)
Sparse Core Ops, SparseCore 0:
  77.0 32.6 all-gather.7
  225.0 6.3 reduce-scatter.15
  235.0 11.3 all-gather.9
  249.3 78.2 all-gather.13
  330.5 75.7 all-gather.11
  409.2 75.7 all-gather.15
  519.4 7.9 reduce-scatter.19
  531.8 11.3 all-gather.17
  737.9 28.3 reduce-scatter.21
  773.6 7.9 reduce-scatter.23
  783.9 10.5 reduce-scatter.17
  798.4 11.3 all-gather.19
  817.3 327.0 all-reduce.7
  1147.3 81.2 reduce-scatter.25
  1231.4 187.3 reduce-scatter.29
  1421.5 187.9 reduce-scatter.27
where the time goes:
time: 1620 us
  waiting for transfers between devices  991 us (61%)
  matrix products  295 us (18%)
  blocking collectives  159 us (10%)
  other arithmetic  113 us (7%)
  local copies, waits for them, and re-layouts  40.6 us (3%)
    unnamed x19, waiting for transfers between devices  626 us
    all_gather x1, waiting for transfers between devices, shards(): lax.all_gather(up_weight, ('fsdp', 'ctx'), axis=0, tiled=True)  81.2 us
    reduce_scatter x1, waiting for transfers between devices, shards(): lax.psum_scatter(out_weight_grad, ('fsdp', 'ctx'), scatter_dimension=0, t...  79.3 us
    all_gather x1, waiting for transfers between devices, shards(): lax.all_gather(gate_weight, ('fsdp', 'ctx'), axis=0, tiled=True)  68.3 us
    all_gather x1, waiting for transfers between devices, shards(): lax.all_gather(down_weight, ('fsdp', 'ctx'), axis=0, tiled=True)  68.2 us
    dot_general x4, matrix products, masked_scores(): jnp.einsum('qhgd,khd->hgqk', query_one, key_one, preferred_element_type=j...  66.4 us
    all_gather x1, blocking collectives, shards(): lax.all_gather(qkv_weight, ('fsdp', 'ctx'), axis=0, tiled=True)  54.7 us
    all_gather x1, blocking collectives, shards(): lax.all_gather(out_weight, ('fsdp', 'ctx'), axis=0, tiled=True)  54.7 us
  transfers between devices with their start and end apart: 16, of which 13 were waited for; matrix products, arithmetic and copies ran while one was open for 6% of the time, Pallas kernels for 0%

commit v1 on v0

v1 whole, which is shorter than its diff:
```python
import functools

import jax
import jax.numpy as jnp
from jax import lax
from jax.experimental import pallas as pl
from jax.experimental.pallas import tpu as pltpu
from jax.sharding import PartitionSpec as P

HD = 64
GROUP = 7

epsilon = 1e-06
rope_base = 1000000.0
masked_value = -1e30
contract_rows = (((0,), (0,)), ((), ()))
contract_last = (((1,), (1,)), ((), ()))
contract_first_last = (((0,), (1,)), ((), ()))
f32 = jnp.float32
bf16 = jnp.bfloat16


def mm(a, b, dims=(((1,), (0,)), ((), ()))):
    return lax.dot_general(a, b, dims, preferred_element_type=f32)


def swap_tp(v):
    n = lax.axis_size("tp")
    return lax.ppermute(v, "tp", [(i, (i + 1) % n) for i in range(n)])


def sum_tp(part):
    low = part.astype(bf16)
    return low.astype(f32) + swap_tp(low).astype(f32)


def swap_x(v):
    return lax.ppermute(v, "fsdp", [(i, i ^ 1) for i in range(4)])


def swap_y(v):
    return lax.ppermute(v, "fsdp", [(i, i ^ 2) for i in range(4)])


def ring_up(v):
    n = lax.axis_size("ctx")
    return lax.ppermute(v, "ctx", [(i, (i + 1) % n) for i in range(n)])


def ring_down(v):
    n = lax.axis_size("ctx")
    return lax.ppermute(v, "ctx", [((i + 1) % n, i) for i in range(n)])


def relative_order():
    return lax.axis_size("fsdp") == 4 and lax.axis_size("ctx") % 2 == 0


def gather_rows(w, plane_first=False):
    if not relative_order():
        return lax.all_gather(w, ("fsdp", "ctx"), axis=0, tiled=True)
    steps = lax.axis_size("ctx") - 1
    rows, cols = w.shape
    if plane_first:
        cut = cols // 256 * 128
        x1, y1 = swap_x(w), swap_y(w)
        d1 = jnp.concatenate([swap_y(x1[:, :cut]), swap_x(y1[:, cut:])], 1)
        current = jnp.stack([w, x1, y1, d1])
        pieces = [current]
        for _ in range(steps):
            current = ring_up(current)
            pieces.append(current)
        return jnp.stack(pieces, 1).reshape(-1, cols)
    current = w
    pieces = [w]
    for _ in range(steps):
        current = ring_up(current)
        pieces.append(current)
    own = jnp.concatenate(pieces, 0)
    half = own.shape[0] // 2
    xs, ys = swap_x(own), swap_y(own)
    d1, d2 = swap_y(xs[:half]), swap_x(ys[half:])
    return jnp.concatenate([own, xs, ys, d1, d2], 0)


def add_low(a, b):
    return (a.astype(f32) + b.astype(f32)).astype(bf16)


def scatter_rows(g, plane_first=False):
    if not relative_order():
        return lax.psum_scatter(g, ("fsdp", "ctx"), scatter_dimension=0, tiled=True).astype(f32)
    count = lax.axis_size("ctx")
    cols = g.shape[1]
    g = g.reshape(4, count, -1, cols)
    if plane_first:
        cut = cols // 256 * 128
        total = g[:, count - 1]
        for s in range(count - 2, -1, -1):
            total = add_low(ring_down(total), g[:, s])
        own, gx, gy, gd = (total[i] for i in range(4))
        r1, r2 = swap_y(gd[:, :cut]), swap_x(gd[:, cut:])
        gx = jnp.concatenate([add_low(gx[:, :cut], r1), gx[:, cut:]], 1)
        gy = jnp.concatenate([gy[:, :cut], add_low(gy[:, cut:], r2)], 1)
        return own.astype(f32) + swap_x(gx).astype(f32) + swap_y(gy).astype(f32)
    half = count // 2
    own, gx, gy, gd = (g[i] for i in range(4))
    r1, r2 = swap_y(gd[:half]), swap_x(gd[half:])
    gx = jnp.concatenate([add_low(gx[:half], r1), gx[half:]], 0)
    gy = jnp.concatenate([gy[:half], add_low(gy[half:], r2)], 0)
    plane = (own.astype(f32) + swap_x(gx).astype(f32) + swap_y(gy).astype(f32)).astype(bf16)
    total = plane[count - 1]
    for s in range(count - 2, 0, -1):
        total = add_low(ring_down(total), plane[s])
    return ring_down(total).astype(f32) + plane[0].astype(f32)


def order_matrix(model_width):
    if not relative_order():
        return None
    count = lax.axis_size("ctx")
    rows = model_width // (4 * count)
    place = jnp.arange(model_width, dtype=jnp.int32)
    block = place // rows
    fsdp = lax.axis_index("fsdp") ^ (block // count)
    ctx = (lax.axis_index("ctx") - block % count + count) % count
    source = (fsdp * count + ctx) * rows + place % rows
    return (jnp.arange(model_width, dtype=jnp.int32)[:, None] == source[None, :]).astype(bf16)


def to_relative(v, order):
    return v if order is None else mm(v, order).astype(v.dtype)


def to_canonical(v, order):
    return v if order is None else mm(v, order, contract_last).astype(v.dtype)


def allowed_pairs(pos, offset, keys, block):
    gap = (
        lax.broadcasted_iota(jnp.int32, (keys, block), 1)
        - lax.broadcasted_iota(jnp.int32, (keys, block), 0)
        + offset
    )
    return (gap >= 0) & (gap <= pos)


def attend_kernel(count_ref, q_ref, pos_ref, kv_ref, vt_ref, o_ref, lse_ref, m_ref, l_ref, acc_ref):
    block = q_ref.shape[1]
    pos = pos_ref[0]
    m_ref[...] = jnp.full(m_ref.shape, masked_value, f32)
    l_ref[...] = jnp.zeros(l_ref.shape, f32)
    acc_ref[...] = jnp.zeros(acc_ref.shape, f32)

    def step(s, carry):
        keep = allowed_pairs(pos, s * block, block, block)
        keys = kv_ref[0, s, :, :HD]
        values_t = vt_ref[0, s]
        for g in range(GROUP):
            rows = slice(g * HD, (g + 1) * HD)
            scores = jnp.where(keep, mm(keys, q_ref[rows, :]), masked_value)
            old = m_ref[g : g + 1, :]
            top = jnp.maximum(old, jnp.max(scores, 0, keepdims=True))
            weight = jnp.exp(scores - top)
            shrink = jnp.exp(old - top)
            m_ref[g : g + 1, :] = top
            l_ref[g : g + 1, :] = l_ref[g : g + 1, :] * shrink + jnp.sum(weight, 0, keepdims=True)
            acc_ref[rows, :] = acc_ref[rows, :] * shrink + mm(values_t, weight.astype(bf16))
        return carry

    lax.fori_loop(0, count_ref[pl.program_id(0)], step, 0)
    for g in range(GROUP):
        rows = slice(g * HD, (g + 1) * HD)
        total = l_ref[g : g + 1, :]
        o_ref[rows, :] = (acc_ref[rows, :] / total).astype(bf16)
        lse_ref[0, g : g + 1, :] = m_ref[g : g + 1, :] + jnp.log(total)
    lse_ref[0, GROUP : GROUP + 1, :] = jnp.zeros((1, block), f32)


def attend_back_kernel(
    count_ref, q_ref, pos_ref, kv_ref, kt_ref, o_ref, lse_ref, do_ref, dq_ref, dkv_ref, dq_acc
):
    block = q_ref.shape[1]
    pos = pos_ref[0]
    dkv_ref[...] = jnp.zeros(dkv_ref.shape, bf16)
    dq_acc[...] = jnp.zeros(dq_acc.shape, f32)

    def step(s, carry):
        keep = allowed_pairs(pos, s * block, block, block)
        keys = kv_ref[0, s, :, :HD]
        values = kv_ref[0, s, :, HD:]
        keys_t = kt_ref[0, s]
        key_grad = jnp.zeros((block, HD), f32)
        value_grad = jnp.zeros((block, HD), f32)
        for g in range(GROUP):
            rows = slice(g * HD, (g + 1) * HD)
            query = q_ref[rows, :]
            grad = do_ref[rows, :]
            centre = jnp.sum(grad.astype(f32) * o_ref[rows, :].astype(f32), 0, keepdims=True)
            scores = mm(keys, query) - lse_ref[0, g : g + 1, :]
            probs = jnp.exp(jnp.where(keep, scores, masked_value))
            prob_grad = mm(values, grad)
            score_grad = (probs * (prob_grad - centre)).astype(bf16)
            value_grad = value_grad + mm(probs.astype(bf16), grad, contract_last)
            key_grad = key_grad + mm(score_grad, query, contract_last)
            dq_acc[rows, :] += mm(keys_t, score_grad)
        dkv_ref[0, s, :, :HD] = key_grad.astype(bf16)
        dkv_ref[0, s, :, HD:] = value_grad.astype(bf16)
        return carry

    lax.fori_loop(0, count_ref[pl.program_id(0)], step, 0)
    dq_ref[...] = dq_acc[...] * HD ** (-0.5)


def attention_specs(block, count):
    return dict(
        wide=pl.BlockSpec((GROUP * HD, block), lambda i, *_: (0, i)),
        pos=pl.BlockSpec((1, 1, block), lambda i, *_: (i, 0, 0)),
        kv=pl.BlockSpec((1, count, block, 2 * HD), lambda i, *_: (i, 0, 0, 0)),
        half=pl.BlockSpec((1, count, HD, block), lambda i, *_: (i, 0, 0, 0)),
        lse=pl.BlockSpec((1, GROUP + 1, block), lambda i, *_: (i, 0, 0)),
    )


VMEM_BYTES = 48 * 1024 * 1024


def attend(counts, queries, pos, kv, values_t, block):
    seqs, count = kv.shape[:2]
    spec = attention_specs(block, count)
    work = seqs * GROUP * block * block * count
    return pl.pallas_call(
        attend_kernel,
        grid_spec=pltpu.PrefetchScalarGridSpec(
            num_scalar_prefetch=1,
            grid=(seqs,),
            in_specs=[spec["wide"], spec["pos"], spec["kv"], spec["half"]],
            out_specs=[spec["wide"], spec["lse"]],
            scratch_shapes=[
                pltpu.VMEM((GROUP + 1, block), f32),
                pltpu.VMEM((GROUP + 1, block), f32),
                pltpu.VMEM((GROUP * HD, block), f32),
            ],
        ),
        out_shape=[
            jax.ShapeDtypeStruct((GROUP * HD, seqs * block), bf16),
            jax.ShapeDtypeStruct((seqs, GROUP + 1, block), f32),
        ],
        compiler_params=pltpu.CompilerParams(vmem_limit_bytes=VMEM_BYTES),
        cost_estimate=pl.CostEstimate(
            flops=4 * HD * work * 4, bytes_accessed=4 * 1024 * 1024, transcendentals=work
        ),
        name="attend",
    )(counts, queries, pos, kv, values_t)


def attend_back(counts, queries, pos, kv, keys_t, mixed, lse, mixed_grad, block):
    seqs, count = kv.shape[:2]
    spec = attention_specs(block, count)
    work = seqs * GROUP * block * block * count
    return pl.pallas_call(
        attend_back_kernel,
        grid_spec=pltpu.PrefetchScalarGridSpec(
            num_scalar_prefetch=1,
            grid=(seqs,),
            in_specs=[
                spec["wide"], spec["pos"], spec["kv"], spec["half"],
                spec["wide"], spec["lse"], spec["wide"],
            ],
            out_specs=[spec["wide"], spec["kv"]],
            scratch_shapes=[pltpu.VMEM((GROUP * HD, block), f32)],
        ),
        out_shape=[
            jax.ShapeDtypeStruct((GROUP * HD, seqs * block), f32),
            jax.ShapeDtypeStruct((seqs, count, block, 2 * HD), bf16),
        ],
        compiler_params=pltpu.CompilerParams(vmem_limit_bytes=VMEM_BYTES),
        cost_estimate=pl.CostEstimate(
            flops=10 * HD * work * 4, bytes_accessed=8 * 1024 * 1024, transcendentals=work
        ),
        name="attend_back",
    )(counts, queries, pos, kv, keys_t, mixed, lse, mixed_grad)


def rotate_rows(v, cosine, sine):
    half = HD // 2
    low, high = v[:, :half], v[:, half:]
    return jnp.concatenate([low * cosine - high * sine, high * cosine + low * sine], 1)


def feed_parts(width):
    tiles = width // 128
    if width % 128 or tiles < 4:
        return [(0, width)]
    each = -(-tiles // 4)
    ends = [0, each * 128, 2 * each * 128, 3 * each * 128, width]
    return [(a, b) for a, b in zip(ends[:-1], ends[1:]) if b > a]


def shards(
    tokens,
    cotangent,
    segments,
    positions,
    norm_one,
    qkv_weight,
    qkv_bias,
    out_weight,
    norm_two,
    gate_weight,
    up_weight,
    down_weight,
):
    del segments
    seqs, block, width = tokens.shape
    rows = seqs * block
    per_group = qkv_weight.shape[2]
    q_width = out_weight.shape[1]
    count = lax.axis_size("ctx")
    tp = lax.axis_size("tp")
    half_len = block // tp
    half_start = lax.axis_index("tp") * half_len

    pack_low = jnp.concatenate([qkv_weight[:, 0], out_weight], 1)
    attention_full = gather_rows(pack_low)
    qkv_full = attention_full[:, :per_group]
    out_full = attention_full[:, per_group:]
    parts = feed_parts(gate_weight.shape[1])
    feed_full = []
    for i, (a, b) in enumerate(parts):
        own = jnp.concatenate([gate_weight[:, a:b], up_weight[:, a:b], down_weight[:, a:b]], 1)
        feed_full.append(gather_rows(own, i == len(parts) - 1 and len(parts) > 1))

    order = order_matrix(width)
    x_low = to_relative(tokens.reshape(rows, width), order)
    upstream_low = to_relative(cotangent.reshape(rows, width), order)
    gains = to_relative(jnp.stack([norm_one, norm_two]), order).astype(f32)
    gain_one, gain_two = gains[0:1], gains[1:2]

    inputs = x_low.astype(f32)
    scale_one = lax.rsqrt(jnp.mean(inputs * inputs, -1, keepdims=True) + epsilon)
    unit_one = inputs * scale_one
    normed = (unit_one * gain_one).astype(bf16)

    projected = mm(qkv_full, normed, contract_first_last) + qkv_bias[0].astype(f32)[:, None]
    frequency = rope_base ** (-(jnp.arange(HD // 2, dtype=f32) * 2.0) / HD)
    angles = positions.reshape(1, rows).astype(f32) * frequency[:, None]
    cosine, sine = jnp.cos(angles), jnp.sin(angles)
    turned = rotate_rows(
        projected[: (GROUP + 1) * HD].reshape(GROUP + 1, HD, rows), cosine, sine
    )
    queries = (turned[:GROUP] * HD ** (-0.5)).astype(bf16).reshape(GROUP * HD, rows)
    kv_t = jnp.concatenate([turned[GROUP], projected[(GROUP + 1) * HD :]], 0).astype(bf16)
    kv_own = kv_t.T.reshape(seqs, block, 2 * HD)
    kv_blocks = [kv_own]
    for s in range(1, count):
        kv_blocks.append(lax.ppermute(kv_own, "ctx", [(i, i + s) for i in range(count - s)]))
    kv = jnp.stack(kv_blocks, 1)
    kv_turned = jnp.swapaxes(kv, 2, 3)
    keys_t, values_t = kv_turned[:, :, :HD], kv_turned[:, :, HD:]
    place = jnp.arange(block, dtype=jnp.int32)
    reach = jnp.max(positions - place[None], 1)
    counts = 1 + jnp.minimum((jnp.maximum(reach, 0) + block - 1) // block, lax.axis_index("ctx"))
    counts = counts.astype(jnp.int32)
    pos = positions.reshape(seqs, 1, block)

    mixed, lse = attend(counts, queries, pos, kv, values_t, block)
    branch = sum_tp(mm(mixed, out_full, contract_first_last))
    middle = inputs + branch
    scale_two = lax.rsqrt(jnp.mean(middle * middle, -1, keepdims=True) + epsilon)
    unit_two = middle * scale_two
    normed_two = (unit_two * gain_two).astype(bf16)

    feed_out = jnp.zeros((rows, width), f32)
    normed_two_part = jnp.zeros((rows, width), f32)
    feed_grads = []
    for i, ((a, b), full) in enumerate(zip(parts, feed_full)):
        c = b - a
        gate_w, up_w, down_w = full[:, :c], full[:, c : 2 * c], full[:, 2 * c :]
        gate_act = mm(normed_two, gate_w)
        up_act = mm(normed_two, up_w)
        hidden_grad = mm(upstream_low, down_w)
        sigmoid = jax.nn.sigmoid(gate_act)
        silu_gate = gate_act * sigmoid
        hidden = (silu_gate * up_act).astype(bf16)
        gate_grad = (hidden_grad * up_act * (sigmoid * (1.0 + gate_act * (1.0 - sigmoid)))).astype(bf16)
        up_grad = (hidden_grad * silu_gate).astype(bf16)
        feed_out = feed_out + mm(hidden, down_w, contract_last)
        normed_two_part = (
            normed_two_part + mm(gate_grad, gate_w, contract_last) + mm(up_grad, up_w, contract_last)
        )
        grads = jnp.concatenate(
            [
                mm(normed_two, gate_grad, contract_rows).astype(bf16),
                mm(normed_two, up_grad, contract_rows).astype(bf16),
                mm(upstream_low, hidden, contract_rows).astype(bf16),
            ],
            1,
        )
        total = scatter_rows(grads, i == len(parts) - 1 and len(parts) > 1)
        feed_grads.append((total[:, :c], total[:, c : 2 * c], total[:, 2 * c :]))
    feed_grads = [jnp.concatenate([p[j] for p in feed_grads], 1) for j in range(3)]

    feed_low = feed_out.astype(bf16).reshape(seqs, block, width)

    def own_rows(v, start):
        return lax.dynamic_slice_in_dim(v, start, half_len, 1)

    other_start = (half_len * (tp - 1) - half_start) if tp == 2 else None
    feed_other = swap_tp(own_rows(feed_low, other_start))
    feed_sum = own_rows(feed_low, half_start).astype(f32) + feed_other.astype(f32)
    block_low = (own_rows(middle.reshape(seqs, block, width), half_start) + feed_sum).astype(bf16)
    block_out = to_canonical(block_low.reshape(-1, width), order).reshape(seqs, half_len, width)

    normed_two_grad = sum_tp(normed_two_part)
    gain_two_grad = jnp.sum(normed_two_grad * unit_two, 0, keepdims=True)
    scaled_two = normed_two_grad * gain_two
    middle_grad = upstream_low.astype(f32) + scale_two * (
        scaled_two - unit_two * jnp.mean(scaled_two * unit_two, -1, keepdims=True)
    )
    branch_low = middle_grad.astype(bf16)
    mixed_grad = mm(out_full, branch_low, contract_first_last).astype(bf16)
    out_weight_grad = mm(branch_low, mixed, contract_first_last_rows).astype(bf16)

    query_grads, pack_grads = attend_back(
        counts, queries, pos, kv, keys_t, mixed, lse, mixed_grad, block
    )
    pack_sum = pack_grads[:, 0].astype(f32)
    for s in range(1, count):
        pack_sum = pack_sum + lax.ppermute(
            pack_grads[:, s], "ctx", [(i + s, i) for i in range(count - s)]
        ).astype(f32)
    pack_t = pack_sum.reshape(rows, 2 * HD).T
    grouped = jnp.concatenate([query_grads, pack_t[:HD]], 0).reshape(GROUP + 1, HD, rows)
    turned_back = rotate_rows(grouped, cosine, -sine).reshape((GROUP + 1) * HD, rows)
    projected_grad = jnp.concatenate([turned_back, pack_t[HD:]], 0).astype(bf16)
    bias_grad = jnp.sum(projected_grad.astype(f32), 1)[None]
    qkv_weight_grad = mm(normed, projected_grad, contract_first_last_rows).astype(bf16)
    attention_total = scatter_rows(jnp.concatenate([qkv_weight_grad, out_weight_grad], 1))

    normed_one_grad = sum_tp(mm(projected_grad, qkv_full, contract_first_last))
    gain_one_grad = jnp.sum(normed_one_grad * unit_one, 0, keepdims=True)
    scaled_one = normed_one_grad * gain_one
    input_grad = middle_grad + scale_one * (
        scaled_one - unit_one * jnp.mean(scaled_one * unit_one, -1, keepdims=True)
    )
    input_grad = to_canonical(input_grad.astype(bf16), order).astype(f32)
    gain_grads = jnp.concatenate([gain_one_grad, gain_two_grad], 0)
    if order is not None:
        gain_grads = lax.dot_general(
            gain_grads, order.astype(f32), contract_last, precision=lax.Precision.HIGHEST
        )
    gain_total, bias_total = lax.psum((gain_grads, bias_grad), ("fsdp", "ctx"))
    return (
        block_out,
        input_grad.reshape(seqs, block, width),
        gain_total[0],
        attention_total[:, :per_group][:, None, :],
        bias_total,
        attention_total[:, per_group:],
        gain_total[1],
        feed_grads[0],
        feed_grads[1],
        feed_grads[2],
    )


contract_first_last_rows = (((0,), (1,)), ((), ()))


def solution(mesh):
    weight = P(("fsdp", "ctx"), "tp")
    return jax.shard_map(
        shards,
        mesh=mesh,
        in_specs=(
            P("fsdp", "ctx", None),
            P("fsdp", "ctx", None),
            P("fsdp", None),
            P("fsdp", "ctx"),
            P(),
            P(("fsdp", "ctx"), "tp", None),
            P("tp", None),
            weight,
            P(),
            weight,
            weight,
            weight,
        ),
        out_specs=(
            P("fsdp", ("ctx", "tp"), None),
            P("fsdp", "ctx", None),
            P(),
            P(("fsdp", "ctx"), "tp", None),
            P("tp", None),
            weight,
            P(),
            weight,
            weight,
            weight,
        ),
        check_vma=False,
    )
```

time: 1620 us -> 647 us (0.40)
  waiting for transfers between devices: 991 us -> 185 us
  matrix products: 295 us -> 128 us
  starting transfers between devices: 1.08 us -> 132 us
  blocking collectives: 159 us -> 44.2 us
  other arithmetic: 113 us -> 60.5 us
  local copies, waits for them, and re-layouts: 40.6 us -> 63.7 us
  Pallas kernels: 0 us -> 21.1 us
    unnamed x19 -> x0, waiting for transfers between devices: 626 us -> none
    all_gather x7 -> x0, waiting for transfers between devices: 239 us -> none  [the longest x1 81.2 us: shards(): lax.all_gather(up_weight, ('fsdp', 'ctx'), axis=0, tiled=True)]
    ppermute x0 -> x80, waiting for transfers between devices: none -> 185 us  [the longest x20 59.9 us: swap_x(): return lax.ppermute(v, 'fsdp', [(i, i ^ 1) for i in range(4)])]
    dot_general x29 -> x48, matrix products: 295 us -> 128 us  [the longest x47 127 us: mm(): return lax.dot_general(a, b, dims, preferred_element_type=f32)]
    ppermute x0 -> x80, starting transfers between devices: none -> 132 us  [the longest x15 40.7 us: ring_down(): return lax.ppermute(v, 'ctx', [((i + 1) % n, i) for i in range(n)])]
    reduce_scatter x6 -> x0, waiting for transfers between devices: 126 us -> none  [the longest x1 79.3 us: shards(): lax.psum_scatter(out_weight_grad, ('fsdp', 'ctx'), scatter_dimension=0, t...]
    all_gather x3 -> x0, blocking collectives: 111 us -> none  [the longest x1 54.7 us: shards(): lax.all_gather(qkv_weight, ('fsdp', 'ctx'), axis=0, tiled=True)]
    another operation x5, other arithmetic: 50.5 us -> 5.14 us  [the longest x2 4.1 us: gather_rows(): return jnp.stack(pieces, 1).reshape(-1, cols)]
  transfers between devices with their start and end apart: 16 -> 80, of which waited for: 13 -> 35; matrix products, arithmetic and copies ran while one was open for 6% -> 20% of each run, Pallas kernels for 0% -> 3%
where the time goes in v1:
time: 647 us; the launch traced here: 637 us
  waiting for transfers between devices  185 us (29%)
  starting transfers between devices  132 us (20%)
  matrix products  128 us (20%)
  local copies, waits for them, and re-layouts  63.7 us (10%)
  other arithmetic  60.5 us (9%)
  blocking collectives  44.2 us (7%)
  Pallas kernels  21.1 us (3%)
    dot_general x47, matrix products, mm(): return lax.dot_general(a, b, dims, preferred_element_type=f32)  127 us
    ppermute x20, waiting for transfers between devices, swap_x(): return lax.ppermute(v, 'fsdp', [(i, i ^ 1) for i in range(4)])  59.9 us
    psum x1, blocking collectives, shards(): gain_total, bias_total = lax.psum((gain_grads, bias_grad), ('fsdp', 'ctx'))  44.2 us
    ppermute x15, starting transfers between devices, ring_down(): return lax.ppermute(v, 'ctx', [((i + 1) % n, i) for i in range(n)])  40.7 us
    ppermute x15, waiting for transfers between devices, ring_up(): return lax.ppermute(v, 'ctx', [(i, (i + 1) % n) for i in range(n)])  40.4 us
    ppermute x15, starting transfers between devices, ring_up(): return lax.ppermute(v, 'ctx', [(i, (i + 1) % n) for i in range(n)])  36.2 us
    ppermute x20, waiting for transfers between devices, swap_y(): return lax.ppermute(v, 'fsdp', [(i, i ^ 2) for i in range(4)])  31.6 us
    unnamed x187, local copies, waits for them, and re-layouts  29.6 us
  transfers between devices with their start and end apart: 80, of which 35 were waited for; matrix products, arithmetic and copies ran while one was open for 20% of the time, Pallas kernels for 3%

profile of v1, /device:TPU:0, one launch (start us, length us, event | category | flops | bytes accessed | tf_op | source)
XLA Modules:
  0.0 637.5 jit_solution(725049538741186868)
XLA Ops:
  18.8 4.9 fusion.37
  23.7 3.4 fusion.11
  48.5 10.1 %collective-permute-done.2 = bf16[56,1024]{1,0:T(8,128)(2,1)S(1)} collective-permute-done((bf16[56,1024]{1,0:T(8,128)(2,1)S(1)}, bf16[56,1024]{1,0:T(8,128)(2,1)S(1)}, u32[]{:S(2)}, u32[]{:S(2)}) %collective-permute-start.2) | collective-permute-done | bytes 114720 | tf_op jit(solution)/shard_map/ppermute | solution.py:47
  63.6 14.3 %collective-permute-done.20 = bf16[56,1920]{1,0:T(8,128)(2,1)S(1)} collective-permute-done((bf16[56,1920]{1,0:T(8,128)(2,1)S(1)}, bf16[56,1920]{1,0:T(8,128)(2,1)S(1)}, u32[]{:S(2)}, u32[]{:S(2)}) %collective-permute-start.20) | collective-permute-done | bytes 215072 | tf_op jit(solution)/shard_map/ppermute | solution.py:47
  88.0 15.6 %collective-permute-done.5 = bf16[112,1024]{1,0:T(8,128)(2,1)S(1)} collective-permute-done((bf16[112,1024]{1,0:T(8,128)(2,1)S(1)}, bf16[112,1024]{1,0:T(8,128)(2,1)S(1)}, u32[]{:S(2)}, u32[]{:S(2)}) %collective-permute-start.5) | collective-permute-done | bytes 229408 | tf_op jit(solution)/shard_map/ppermute | solution.py:42
  111.6 3.3 collective-permute-start.7
  129.2 9.0 %attend.1 = (bf16[448,1024]{1,0:T(8,128)(2,1)S(1)}, f32[2,8,512]{2,1,0:T(8,128)S(1)}) custom-call(s32[2]{0:T(128)S(1)} %minimum_add_fusion.count_ref, bf16[448,1024]{1,0:T(8,128)(2,1)S(1)} %bitcast.299, s32[2,1,512]{2,1,0:T(1,128)S(1)} %reshape.383.pos_ref, bf16[2,4,512,128]{3,2,1,0:T(8,128)(2,1)S(1)} %copy.140.kv_ref, ...), custom_call_target="tpu_custom_call" | custom-call | flops 15032385536 | bytes 4194304 | tf_op jit(solution)/shard_map/attend/pallas_call | solution.py:232
  143.6 15.2 %collective-permute-start.37 = (bf16[4,56,1536]{2,1,0:T(8,128)(2,1)}, bf16[4,56,1536]{2,1,0:T(8,128)(2,1)S(1)}, u32[]{:S(2)}, u32[]{:S(2)}) collective-permute-start(bf16[4,56,1536]{2,1,0:T(8,128)(2,1)} %collective-permute-done.36), channel_id=1, source_target_pairs={{0,2},{2,4},{4,6},{6,0},{1,3},{3,5},{5,7},{7,1},{8,10},{10,12},{12... | collective-permute-start | bytes 2064392 | tf_op jit(solution)/shard_map/ppermute | solution.py:47
  168.6 6.4 %collective-permute-done.28 = bf16[224,1920]{1,0:T(8,128)(2,1)S(1)} collective-permute-done((bf16[224,1920]{1,0:T(8,128)(2,1)S(1)}, bf16[224,1920]{1,0:T(8,128)(2,1)S(1)}, u32[]{:S(2)}, u32[]{:S(2)}) %collective-permute-start.28) | collective-permute-done | bytes 860192 | tf_op jit(solution)/shard_map/ppermute | solution.py:38
  177.9 6.4 collective-permute-done.24
  189.3 8.5 %collective-permute-start.38 = (bf16[4,56,1536]{2,1,0:T(8,128)(2,1)S(1)}, bf16[4,56,1536]{2,1,0:T(8,128)(2,1)S(1)}, u32[]{:S(2)}, u32[]{:S(2)}) collective-permute-start(bf16[4,56,1536]{2,1,0:T(8,128)(2,1)S(1)} %collective-permute-done.37), channel_id=1, source_target_pairs={{0,2},{2,4},{4,6},{6,0},{1,3},{3,5},{5,7},{7,1},{8,10},{10,12},{12... | collective-permute-start | bytes 2064392 | tf_op jit(solution)/shard_map/ppermute | solution.py:47
  201.6 7.5 %collective-permute-done.38 = bf16[4,56,1536]{2,1,0:T(8,128)(2,1)S(1)} collective-permute-done((bf16[4,56,1536]{2,1,0:T(8,128)(2,1)S(1)}, bf16[4,56,1536]{2,1,0:T(8,128)(2,1)S(1)}, u32[]{:S(2)}, u32[]{:S(2)}) %collective-permute-start.38) | collective-permute-done | bytes 688160 | tf_op jit(solution)/shard_map/ppermute | solution.py:47
  216.6 3.4 multiply_convert_fusion.10
  231.9 3.6 fusion.75
  237.0 3.4 fusion.77
  242.0 3.4 fusion.81
  256.7 3.5 fusion.87
  261.8 3.6 fusion.93
  267.4 3.5 fusion.89
  281.5 3.6 fusion.63
  287.7 3.4 fusion.65
  293.8 3.5 fusion.69
  297.2 6.1 reshape.385
  303.3 3.2 convolution_convert_fusion.13
  309.6 4.6 copy.172
  316.3 6.7 %collective-permute-start.73 = (bf16[4,56,1536]{2,1,0:T(8,128)(2,1)}, bf16[4,56,1536]{2,1,0:T(8,128)(2,1)}, u32[]{:S(2)}, u32[]{:S(2)}) collective-permute-start(bf16[4,56,1536]{2,1,0:T(8,128)(2,1)} %slice_bitcast_fusion.3), channel_id=1, source_target_pairs={{2,0},{4,2},{6,4},{0,6},{3,1},{5,3},{7,5},{1,7},{10,8},{12,10},{14... | collective-permute-start | bytes 2064392 | tf_op jit(solution)/shard_map/ppermute | solution.py:52
  327.1 5.6 add_convert_fusion.1
  336.4 9.8 %add_convert_fusion = bf16[1024,896]{0,1:T(8,128)(2,1)} fusion(f32[1024,896]{0,1:T(8,128)S(1)} %copy-done.6, f32[1024,896]{0,1:T(8,128)} %fusion.65, f32[1024,896]{0,1:T(8,128)} %fusion.69, f32[1024,896]{0,1:T(8,128)S(1)} %copy-done.20, f32[1024,896]{0,1:T(8,128)} %fusion.81, f32[1024,896]{0,1:T(8,128)} %fusion.93, f32[1024,896]{0,1:T(8,128)} %fusion.89, ...), kind=kOutput, calls=%fused_computation.20 | convolution fusion | flops 946864128 | bytes 29491200 | tf_op jit(solution)/shard_map/dot_general | solution.py:24
  347.6 3.5 copy.199
  351.1 3.6 copy.200
  365.4 7.6 %collective-permute-done.68 = bf16[2,56,1920]{2,1,0:T(8,128)(2,1)S(1)} collective-permute-done((bf16[2,56,1920]{2,1,0:T(8,128)(2,1)S(1)}, bf16[2,56,1920]{2,1,0:T(8,128)(2,1)S(1)}, u32[]{:S(2)}, u32[]{:S(2)}) %collective-permute-start.68) | collective-permute-done | bytes 430112 | tf_op jit(solution)/shard_map/ppermute | solution.py:38
  385.3 9.8 %collective-permute-done.60 = bf16[4,56,1920]{2,1,0:T(8,128)(2,1)S(1)} collective-permute-done((bf16[4,56,1920]{2,1,0:T(8,128)(2,1)S(1)}, bf16[4,56,1920]{2,1,0:T(8,128)(2,1)S(1)}, u32[]{:S(2)}, u32[]{:S(2)}) %collective-permute-start.60) | collective-permute-done | bytes 860192 | tf_op jit(solution)/shard_map/ppermute | solution.py:38
  398.7 14.8 %collective-permute-done.53 = bf16[4,56,1920]{2,1,0:T(8,128)(2,1)S(1)} collective-permute-done((bf16[4,56,1920]{2,1,0:T(8,128)(2,1)S(1)}, bf16[4,56,1920]{2,1,0:T(8,128)(2,1)S(1)}, u32[]{:S(2)}, u32[]{:S(2)}) %collective-permute-start.53) | collective-permute-done | bytes 860192 | tf_op jit(solution)/shard_map/ppermute | solution.py:38
  417.5 12.7 %collective-permute-done.67 = bf16[4,56,1920]{2,1,0:T(8,128)(2,1)S(1)} collective-permute-done((bf16[4,56,1920]{2,1,0:T(8,128)(2,1)S(1)}, bf16[4,56,1920]{2,1,0:T(8,128)(2,1)S(1)}, u32[]{:S(2)}, u32[]{:S(2)}) %collective-permute-start.67) | collective-permute-done | bytes 860192 | tf_op jit(solution)/shard_map/ppermute | solution.py:38
  438.6 4.0 collective-permute-start.57
  443.2 4.0 collective-permute-start.71
  447.2 15.3 %collective-permute-done.64 = bf16[56,1920]{1,0:T(8,128)(2,1)S(1)} collective-permute-done((bf16[56,1920]{1,0:T(8,128)(2,1)S(1)}, bf16[56,1920]{1,0:T(8,128)(2,1)S(1)}, u32[]{:S(2)}, u32[]{:S(2)}) %collective-permute-start.64) | collective-permute-done | bytes 215072 | tf_op jit(solution)/shard_map/ppermute | solution.py:52
  462.5 4.0 collective-permute-start.65
  467.1 4.0 collective-permute-start.58
  471.8 4.2 collective-permute-start.72
  482.8 12.1 %attend_back.1 = (f32[448,1024]{1,0:T(8,128)}, bf16[2,4,512,128]{3,2,1,0:T(8,128)(2,1)S(1)}) custom-call(s32[2]{0:T(128)S(1)} %minimum_add_fusion.count_ref, bf16[448,1024]{1,0:T(8,128)(2,1)S(1)} %bitcast.300, s32[2,1,512]{2,1,0:T(1,128)S(1)} %reshape.383.pos_ref, bf16[2,4,512,128]{3,2,1,0:T(8,128)(2,1)S(1)} %copy.140.kv_ref, ...), custom_call_target="tpu_custom_call" | custom-call | flops 37580963840 | bytes 8388608 | tf_op jit(solution)/shard_map/attend_back/pallas_call | solution.py:261
  507.7 15.6 %collective-permute-done.43 = bf16[2,512,128]{2,1,0:T(8,128)(2,1)S(1)} collective-permute-done((bf16[2,512,128]{2,1,0:T(8,128)(2,1)S(1)}, bf16[2,512,128]{2,1,0:T(8,128)(2,1)S(1)}, u32[]{:S(2)}, u32[]{:S(2)}) %collective-permute-start.43) | collective-permute-done | bytes 262176 | tf_op jit(solution)/shard_map/ppermute | solution.py:430
  523.3 11.5 %collective-permute-done.42 = bf16[2,512,128]{2,1,0:T(8,128)(2,1)S(1)} collective-permute-done((bf16[2,512,128]{2,1,0:T(8,128)(2,1)S(1)}, bf16[2,512,128]{2,1,0:T(8,128)(2,1)S(1)}, u32[]{:S(2)}, u32[]{:S(2)}) %collective-permute-start.42) | collective-permute-done | bytes 262176 | tf_op jit(solution)/shard_map/ppermute | solution.py:430
  553.9 8.1 %collective-permute-done.48 = bf16[4,56,1024]{2,1,0:T(8,128)(2,1)S(1)} collective-permute-done((bf16[4,56,1024]{2,1,0:T(8,128)(2,1)S(1)}, bf16[4,56,1024]{2,1,0:T(8,128)(2,1)S(1)}, u32[]{:S(2)}, u32[]{:S(2)}) %collective-permute-start.48) | collective-permute-done | bytes 458784 | tf_op jit(solution)/shard_map/ppermute | solution.py:42
  564.6 3.7 collective-permute-done.49
  573.6 3.6 collective-permute-start.51
  584.0 44.2 %all-reduce = (f32[2,896]{1,0:T(2,128)S(1)}, f32[1,576]{1,0:T(1,128)}) all-reduce(f32[2,896]{1,0:T(2,128)S(1)} %fusion.15, f32[1,576]{1,0:T(1,128)S(1)} %broadcast_in_dim.11), channel_id=1, replica_groups=mesh['fsdp'=4,'ctx'=4,'tp'=2] {'fsdp','ctx'}, use_global_device_ids=true, to_apply=%region_7.8 | all-reduce | flops 2368 | bytes 18944 | tf_op jit(solution)/shard_map/psum | solution.py:453
  628.8 6.3 fusion.40
  (504 shorter events, 266.7 us)
Async XLA Ops:
  4.0 26.8 %collective-permute-start.32 = (bf16[56,1536]{1,0:T(8,128)(2,1)}, bf16[56,1536]{1,0:T(8,128)(2,1)S(1)}, u32[]{:S(2)}, u32[]{:S(2)}) collective-permute-start(bf16[56,1536]{1,0:T(8,128)(2,1)} %get-tuple-element.135), channel_id=1, source_target_pairs={{0,8},{8,0},{16,24},{24,16},{1,9},{9,1},{17,25},{25,17},{2,10},{10... | collective-permute-start | bytes 516104 | tf_op jit(solution)/shard_map/ppermute | solution.py:38
  6.9 25.4 %collective-permute-start.33 = (bf16[56,1536]{1,0:T(8,128)(2,1)}, bf16[56,1536]{1,0:T(8,128)(2,1)}, u32[]{:S(2)}, u32[]{:S(2)}) collective-permute-start(bf16[56,1536]{1,0:T(8,128)(2,1)} %get-tuple-element.135), channel_id=1, source_target_pairs={{0,16},{8,24},{16,0},{24,8},{1,17},{9,25},{17,1},{25,9},{2,18},{10... | collective-permute-start | bytes 516104 | tf_op jit(solution)/shard_map/ppermute | solution.py:42
  10.1 19.6 %collective-permute-start = (bf16[56,1024]{1,0:T(8,128)(2,1)}, bf16[56,1024]{1,0:T(8,128)(2,1)S(1)}, u32[]{:S(2)}, u32[]{:S(2)}) collective-permute-start(bf16[56,1024]{1,0:T(8,128)(2,1)} %get-tuple-element.51), channel_id=1, source_target_pairs={{0,2},{2,4},{4,6},{6,0},{1,3},{3,5},{5,7},{7,1},{8,10},{10,12},{12... | collective-permute-start | bytes 344072 | tf_op jit(solution)/shard_map/ppermute | solution.py:47
  35.1 23.7 %collective-permute-start.19 = (bf16[56,1920]{1,0:T(8,128)(2,1)S(1)}, bf16[56,1920]{1,0:T(8,128)(2,1)S(1)}, u32[]{:S(2)}, u32[]{:S(2)}) collective-permute-start(bf16[56,1920]{1,0:T(8,128)(2,1)S(1)} %collective-permute-done.18), channel_id=1, source_target_pairs={{0,2},{2,4},{4,6},{6,0},{1,3},{3,5},{5,7},{7,1},{8,10},{10,12},{12... | collective-permute-start | bytes 645128 | tf_op jit(solution)/shard_map/ppermute | solution.py:47
  39.9 20.9 %collective-permute-start.12 = (bf16[56,1920]{1,0:T(8,128)(2,1)S(1)}, bf16[56,1920]{1,0:T(8,128)(2,1)S(1)}, u32[]{:S(2)}, u32[]{:S(2)}) collective-permute-start(bf16[56,1920]{1,0:T(8,128)(2,1)S(1)} %collective-permute-done.11), channel_id=1, source_target_pairs={{0,2},{2,4},{4,6},{6,0},{1,3},{3,5},{5,7},{7,1},{8,10},{10,12},{12... | collective-permute-start | bytes 645128 | tf_op jit(solution)/shard_map/ppermute | solution.py:47
  42.3 19.2 %collective-permute-start.26 = (bf16[56,1920]{1,0:T(8,128)(2,1)S(1)}, bf16[56,1920]{1,0:T(8,128)(2,1)S(1)}, u32[]{:S(2)}, u32[]{:S(2)}) collective-permute-start(bf16[56,1920]{1,0:T(8,128)(2,1)S(1)} %collective-permute-done.25), channel_id=1, source_target_pairs={{0,2},{2,4},{4,6},{6,0},{1,3},{3,5},{5,7},{7,1},{8,10},{10,12},{12... | collective-permute-start | bytes 645128 | tf_op jit(solution)/shard_map/ppermute | solution.py:47
  45.4 83.6 %collective-permute-start.36 = (bf16[4,56,1536]{2,1,0:T(8,128)(2,1)}, bf16[4,56,1536]{2,1,0:T(8,128)(2,1)}, u32[]{:S(2)}, u32[]{:S(2)}) collective-permute-start(bf16[4,56,1536]{2,1,0:T(8,128)(2,1)} %get-tuple-element.104), channel_id=1, source_target_pairs={{0,2},{2,4},{4,6},{6,0},{1,3},{3,5},{5,7},{7,1},{8,10},{10,12},{12... | collective-permute-start | bytes 2064392 | tf_op jit(solution)/shard_map/ppermute | solution.py:47
  58.7 27.8 %collective-permute-start.4 = (bf16[224,1024]{1,0:T(8,128)(2,1)S(1)}, bf16[224,1024]{1,0:T(8,128)(2,1)S(1)}, u32[]{:S(2)}, u32[]{:S(2)}) collective-permute-start(bf16[224,1024]{1,0:T(8,128)(2,1)S(1)} %pad_maximum_fusion.22), channel_id=1, source_target_pairs={{0,16},{8,24},{16,0},{24,8},{1,17},{9,25},{17,1},{25,9},{2,18},{10... | collective-permute-start | bytes 1376264 | tf_op jit(solution)/shard_map/ppermute | solution.py:42
  58.8 27.8 %collective-permute-start.3 = (bf16[224,1024]{1,0:T(8,128)(2,1)S(1)}, bf16[224,1024]{1,0:T(8,128)(2,1)S(1)}, u32[]{:S(2)}, u32[]{:S(2)}) collective-permute-start(bf16[224,1024]{1,0:T(8,128)(2,1)S(1)} %pad_maximum_fusion.22), channel_id=1, source_target_pairs={{0,8},{8,0},{16,24},{24,16},{1,9},{9,1},{17,25},{25,17},{2,10},{10... | collective-permute-start | bytes 1376264 | tf_op jit(solution)/shard_map/ppermute | solution.py:38
  61.5 20.8 %collective-permute-start.13 = (bf16[56,1920]{1,0:T(8,128)(2,1)S(1)}, bf16[56,1920]{1,0:T(8,128)(2,1)S(1)}, u32[]{:S(2)}, u32[]{:S(2)}) collective-permute-start(bf16[56,1920]{1,0:T(8,128)(2,1)S(1)} %collective-permute-done.12), channel_id=1, source_target_pairs={{0,2},{2,4},{4,6},{6,0},{1,3},{3,5},{5,7},{7,1},{8,10},{10,12},{12... | collective-permute-start | bytes 645128 | tf_op jit(solution)/shard_map/ppermute | solution.py:47
  82.3 61.3 %collective-permute-start.22 = (bf16[224,1920]{1,0:T(8,128)(2,1)}, bf16[224,1920]{1,0:T(8,128)(2,1)}, u32[]{:S(2)}, u32[]{:S(2)}) collective-permute-start(bf16[224,1920]{1,0:T(8,128)(2,1)} %pad_maximum_fusion.10), channel_id=1, source_target_pairs={{0,16},{8,24},{16,0},{24,8},{1,17},{9,25},{17,1},{25,9},{2,18},{10... | collective-permute-start | bytes 2580488 | tf_op jit(solution)/shard_map/ppermute | solution.py:42
  117.2 22.4 %collective-permute-start.21 = (bf16[224,1920]{1,0:T(8,128)(2,1)}, bf16[224,1920]{1,0:T(8,128)(2,1)}, u32[]{:S(2)}, u32[]{:S(2)}) collective-permute-start(bf16[224,1920]{1,0:T(8,128)(2,1)} %pad_maximum_fusion.10), channel_id=1, source_target_pairs={{0,8},{8,0},{16,24},{24,16},{1,9},{9,1},{17,25},{25,17},{2,10},{10... | collective-permute-start | bytes 2580488 | tf_op jit(solution)/shard_map/ppermute | solution.py:38
  118.5 41.4 %collective-permute-start.15 = (bf16[224,1920]{1,0:T(8,128)(2,1)}, bf16[224,1920]{1,0:T(8,128)(2,1)}, u32[]{:S(2)}, u32[]{:S(2)}) collective-permute-start(bf16[224,1920]{1,0:T(8,128)(2,1)} %pad_maximum_fusion.9), channel_id=1, source_target_pairs={{0,16},{8,24},{16,0},{24,8},{1,17},{9,25},{17,1},{25,9},{2,18},{10... | collective-permute-start | bytes 2580488 | tf_op jit(solution)/shard_map/ppermute | solution.py:42
  121.0 40.1 %collective-permute-start.14 = (bf16[224,1920]{1,0:T(8,128)(2,1)}, bf16[224,1920]{1,0:T(8,128)(2,1)}, u32[]{:S(2)}, u32[]{:S(2)}) collective-permute-start(bf16[224,1920]{1,0:T(8,128)(2,1)} %pad_maximum_fusion.9), channel_id=1, source_target_pairs={{0,8},{8,0},{16,24},{24,16},{1,9},{9,1},{17,25},{25,17},{2,10},{10... | collective-permute-start | bytes 2580488 | tf_op jit(solution)/shard_map/ppermute | solution.py:38
  129.2 34.1 %collective-permute-start.29 = (bf16[224,1920]{1,0:T(8,128)(2,1)S(1)}, bf16[224,1920]{1,0:T(8,128)(2,1)S(1)}, u32[]{:S(2)}, u32[]{:S(2)}) collective-permute-start(bf16[224,1920]{1,0:T(8,128)(2,1)S(1)} %copy-done.48), channel_id=1, source_target_pairs={{0,16},{8,24},{16,0},{24,8},{1,17},{9,25},{17,1},{25,9},{2,18},{10... | collective-permute-start | bytes 2580488 | tf_op jit(solution)/shard_map/ppermute | solution.py:42
  139.6 35.4 %collective-permute-start.28 = (bf16[224,1920]{1,0:T(8,128)(2,1)S(1)}, bf16[224,1920]{1,0:T(8,128)(2,1)S(1)}, u32[]{:S(2)}, u32[]{:S(2)}) collective-permute-start(bf16[224,1920]{1,0:T(8,128)(2,1)S(1)} %copy-done.48), channel_id=1, source_target_pairs={{0,8},{8,0},{16,24},{24,16},{1,9},{9,1},{17,25},{25,17},{2,10},{10... | collective-permute-start | bytes 2580488 | tf_op jit(solution)/shard_map/ppermute | solution.py:38
  143.6 43.1 %collective-permute-start.37 = (bf16[4,56,1536]{2,1,0:T(8,128)(2,1)}, bf16[4,56,1536]{2,1,0:T(8,128)(2,1)S(1)}, u32[]{:S(2)}, u32[]{:S(2)}) collective-permute-start(bf16[4,56,1536]{2,1,0:T(8,128)(2,1)} %collective-permute-done.36), channel_id=1, source_target_pairs={{0,2},{2,4},{4,6},{6,0},{1,3},{3,5},{5,7},{7,1},{8,10},{10,12},{12... | collective-permute-start | bytes 2064392 | tf_op jit(solution)/shard_map/ppermute | solution.py:47
  159.8 51.0 %collective-permute-start.10 = (bf16[1024,896]{0,1:T(8,128)(2,1)S(1)}, bf16[1024,896]{0,1:T(8,128)(2,1)S(1)}, u32[]{:S(2)}, u32[]{:S(2)}) collective-permute-start(bf16[1024,896]{0,1:T(8,128)(2,1)S(1)} %convolution_convert_fusion.1), channel_id=1, source_target_pairs={{0,1},{1,0},{2,3},{3,2},{4,5},{5,4},{6,7},{7,6},{8,9},{9,8},{10,11... | collective-permute-start | bytes 5505032 | tf_op jit(solution)/shard_map/ppermute | solution.py:29
  161.1 23.1 %collective-permute-start.24 = (bf16[112,1920]{1,0:T(8,128)(2,1)S(1)}, bf16[112,1920]{1,0:T(8,128)(2,1)S(1)}, u32[]{:S(2)}, u32[]{:S(2)}) collective-permute-start(bf16[112,1920]{1,0:T(8,128)(2,1)S(1)} %slice.658), channel_id=1, source_target_pairs={{0,8},{8,0},{16,24},{24,16},{1,9},{9,1},{17,25},{25,17},{2,10},{10... | collective-permute-start | bytes 1290248 | tf_op jit(solution)/shard_map/ppermute | solution.py:38
  175.0 22.8 %collective-permute-start.17 = (bf16[112,1920]{1,0:T(8,128)(2,1)S(1)}, bf16[112,1920]{1,0:T(8,128)(2,1)S(1)}, u32[]{:S(2)}, u32[]{:S(2)}) collective-permute-start(bf16[112,1920]{1,0:T(8,128)(2,1)S(1)} %slice.653), channel_id=1, source_target_pairs={{0,8},{8,0},{16,24},{24,16},{1,9},{9,1},{17,25},{25,17},{2,10},{10... | collective-permute-start | bytes 1290248 | tf_op jit(solution)/shard_map/ppermute | solution.py:38
  189.3 19.8 %collective-permute-start.38 = (bf16[4,56,1536]{2,1,0:T(8,128)(2,1)S(1)}, bf16[4,56,1536]{2,1,0:T(8,128)(2,1)S(1)}, u32[]{:S(2)}, u32[]{:S(2)}) collective-permute-start(bf16[4,56,1536]{2,1,0:T(8,128)(2,1)S(1)} %collective-permute-done.37), channel_id=1, source_target_pairs={{0,2},{2,4},{4,6},{6,0},{1,3},{3,5},{5,7},{7,1},{8,10},{10,12},{12... | collective-permute-start | bytes 2064392 | tf_op jit(solution)/shard_map/ppermute | solution.py:47
  316.3 60.3 %collective-permute-start.73 = (bf16[4,56,1536]{2,1,0:T(8,128)(2,1)}, bf16[4,56,1536]{2,1,0:T(8,128)(2,1)}, u32[]{:S(2)}, u32[]{:S(2)}) collective-permute-start(bf16[4,56,1536]{2,1,0:T(8,128)(2,1)} %slice_bitcast_fusion.3), channel_id=1, source_target_pairs={{2,0},{4,2},{6,4},{0,6},{3,1},{5,3},{7,5},{1,7},{10,8},{12,10},{14... | collective-permute-start | bytes 2064392 | tf_op jit(solution)/shard_map/ppermute | solution.py:52
  323.0 34.7 %collective-permute-start.61 = (bf16[2,56,1920]{2,1,0:T(8,128)(2,1)}, bf16[2,56,1920]{2,1,0:T(8,128)(2,1)}, u32[]{:S(2)}, u32[]{:S(2)}) collective-permute-start(bf16[2,56,1920]{2,1,0:T(8,128)(2,1)} %bitcast.67), channel_id=1, source_target_pairs={{0,8},{8,0},{16,24},{24,16},{1,9},{9,1},{17,25},{25,17},{2,10},{10... | collective-permute-start | bytes 1290248 | tf_op jit(solution)/shard_map/ppermute | solution.py:38
  324.8 34.4 %collective-permute-start.59 = (bf16[2,56,1920]{2,1,0:T(8,128)(2,1)}, bf16[2,56,1920]{2,1,0:T(8,128)(2,1)}, u32[]{:S(2)}, u32[]{:S(2)}) collective-permute-start(bf16[2,56,1920]{2,1,0:T(8,128)(2,1)} %bitcast.63), channel_id=1, source_target_pairs={{0,16},{8,24},{16,0},{24,8},{1,17},{9,25},{17,1},{25,9},{2,18},{10... | collective-permute-start | bytes 1290248 | tf_op jit(solution)/shard_map/ppermute | solution.py:42
  324.8 36.1 %collective-permute-start.54 = (bf16[2,56,1920]{2,1,0:T(8,128)(2,1)}, bf16[2,56,1920]{2,1,0:T(8,128)(2,1)}, u32[]{:S(2)}, u32[]{:S(2)}) collective-permute-start(bf16[2,56,1920]{2,1,0:T(8,128)(2,1)} %bitcast.56), channel_id=1, source_target_pairs={{0,8},{8,0},{16,24},{24,16},{1,9},{9,1},{17,25},{25,17},{2,10},{10... | collective-permute-start | bytes 1290248 | tf_op jit(solution)/shard_map/ppermute | solution.py:38
  325.1 39.0 %collective-permute-start.52 = (bf16[2,56,1920]{2,1,0:T(8,128)(2,1)}, bf16[2,56,1920]{2,1,0:T(8,128)(2,1)}, u32[]{:S(2)}, u32[]{:S(2)}) collective-permute-start(bf16[2,56,1920]{2,1,0:T(8,128)(2,1)} %bitcast.52), channel_id=1, source_target_pairs={{0,16},{8,24},{16,0},{24,8},{1,17},{9,25},{17,1},{25,9},{2,18},{10... | collective-permute-start | bytes 1290248 | tf_op jit(solution)/shard_map/ppermute | solution.py:42
  357.8 21.9 %collective-permute-start.39 = (bf16[2,256,896]{1,0,2:T(2,128)(2,1)S(1)}, bf16[2,256,896]{1,0,2:T(2,128)(2,1)S(1)}, u32[]{:S(2)}, u32[]{:S(2)}) collective-permute-start(bf16[2,256,896]{1,0,2:T(2,128)(2,1)S(1)} %copy-done.46), channel_id=1, source_target_pairs={{0,1},{1,0},{2,3},{3,2},{4,5},{5,4},{6,7},{7,6},{8,9},{9,8},{10,11... | collective-permute-start | bytes 2752520 | tf_op jit(solution)/shard_map/ppermute | solution.py:29
  359.4 116.6 %collective-permute-start.40 = (bf16[1024,896]{0,1:T(8,128)(2,1)S(1)}, bf16[1024,896]{0,1:T(8,128)(2,1)S(1)}, u32[]{:S(2)}, u32[]{:S(2)}) collective-permute-start(bf16[1024,896]{0,1:T(8,128)(2,1)S(1)} %copy-done.7), channel_id=1, source_target_pairs={{0,1},{1,0},{2,3},{3,2},{4,5},{5,4},{6,7},{7,6},{8,9},{9,8},{10,11... | collective-permute-start | bytes 5505032 | tf_op jit(solution)/shard_map/ppermute | solution.py:29
  373.0 22.1 %collective-permute-start.60 = (bf16[4,56,1920]{2,1,0:T(8,128)(2,1)S(1)}, bf16[4,56,1920]{2,1,0:T(8,128)(2,1)S(1)}, u32[]{:S(2)}, u32[]{:S(2)}) collective-permute-start(bf16[4,56,1920]{2,1,0:T(8,128)(2,1)S(1)} %pad_maximum_fusion.14), channel_id=1, source_target_pairs={{0,8},{8,0},{16,24},{24,16},{1,9},{9,1},{17,25},{25,17},{2,10},{10... | collective-permute-start | bytes 2580488 | tf_op jit(solution)/shard_map/ppermute | solution.py:38
  375.9 22.1 %collective-permute-start.62 = (bf16[4,56,1920]{2,1,0:T(8,128)(2,1)S(1)}, bf16[4,56,1920]{2,1,0:T(8,128)(2,1)S(1)}, u32[]{:S(2)}, u32[]{:S(2)}) collective-permute-start(bf16[4,56,1920]{2,1,0:T(8,128)(2,1)S(1)} %pad_maximum_fusion.15), channel_id=1, source_target_pairs={{0,16},{8,24},{16,0},{24,8},{1,17},{9,25},{17,1},{25,9},{2,18},{10... | collective-permute-start | bytes 2580488 | tf_op jit(solution)/shard_map/ppermute | solution.py:42
  376.7 36.8 %collective-permute-start.53 = (bf16[4,56,1920]{2,1,0:T(8,128)(2,1)S(1)}, bf16[4,56,1920]{2,1,0:T(8,128)(2,1)S(1)}, u32[]{:S(2)}, u32[]{:S(2)}) collective-permute-start(bf16[4,56,1920]{2,1,0:T(8,128)(2,1)S(1)} %pad_maximum_fusion.12), channel_id=1, source_target_pairs={{0,8},{8,0},{16,24},{24,16},{1,9},{9,1},{17,25},{25,17},{2,10},{10... | collective-permute-start | bytes 2580488 | tf_op jit(solution)/shard_map/ppermute | solution.py:38
  379.7 36.7 %collective-permute-start.55 = (bf16[4,56,1920]{2,1,0:T(8,128)(2,1)S(1)}, bf16[4,56,1920]{2,1,0:T(8,128)(2,1)S(1)}, u32[]{:S(2)}, u32[]{:S(2)}) collective-permute-start(bf16[4,56,1920]{2,1,0:T(8,128)(2,1)S(1)} %pad_maximum_fusion.13), channel_id=1, source_target_pairs={{0,16},{8,24},{16,0},{24,8},{1,17},{9,25},{17,1},{25,9},{2,18},{10... | collective-permute-start | bytes 2580488 | tf_op jit(solution)/shard_map/ppermute | solution.py:42
  395.0 35.2 %collective-permute-start.67 = (bf16[4,56,1920]{2,1,0:T(8,128)(2,1)S(1)}, bf16[4,56,1920]{2,1,0:T(8,128)(2,1)S(1)}, u32[]{:S(2)}, u32[]{:S(2)}) collective-permute-start(bf16[4,56,1920]{2,1,0:T(8,128)(2,1)S(1)} %pad_maximum_fusion.16), channel_id=1, source_target_pairs={{0,8},{8,0},{16,24},{24,16},{1,9},{9,1},{17,25},{25,17},{2,10},{10... | collective-permute-start | bytes 2580488 | tf_op jit(solution)/shard_map/ppermute | solution.py:38
  398.0 34.9 %collective-permute-start.69 = (bf16[4,56,1920]{2,1,0:T(8,128)(2,1)S(1)}, bf16[4,56,1920]{2,1,0:T(8,128)(2,1)S(1)}, u32[]{:S(2)}, u32[]{:S(2)}) collective-permute-start(bf16[4,56,1920]{2,1,0:T(8,128)(2,1)S(1)} %pad_maximum_fusion.17), channel_id=1, source_target_pairs={{0,16},{8,24},{16,0},{24,8},{1,17},{9,25},{17,1},{25,9},{2,18},{10... | collective-permute-start | bytes 2580488 | tf_op jit(solution)/shard_map/ppermute | solution.py:42
  413.5 20.6 %collective-permute-start.74 = (bf16[4,56,1536]{2,1,0:T(8,128)(2,1)S(1)}, bf16[4,56,1536]{2,1,0:T(8,128)(2,1)S(1)}, u32[]{:S(2)}, u32[]{:S(2)}) collective-permute-start(bf16[4,56,1536]{2,1,0:T(8,128)(2,1)S(1)} %fusion.58), channel_id=1, source_target_pairs={{2,0},{4,2},{6,4},{0,6},{3,1},{5,3},{7,5},{1,7},{10,8},{12,10},{14... | collective-permute-start | bytes 2064392 | tf_op jit(solution)/shard_map/ppermute | solution.py:52
  435.2 69.5 %collective-permute-start.75 = (bf16[4,56,1536]{2,1,0:T(8,128)(2,1)}, bf16[4,56,1536]{2,1,0:T(8,128)(2,1)}, u32[]{:S(2)}, u32[]{:S(2)}) collective-permute-start(bf16[4,56,1536]{2,1,0:T(8,128)(2,1)} %fusion.57), channel_id=1, source_target_pairs={{2,0},{4,2},{6,4},{0,6},{3,1},{5,3},{7,5},{1,7},{10,8},{12,10},{14... | collective-permute-start | bytes 2064392 | tf_op jit(solution)/shard_map/ppermute | solution.py:52
  435.3 27.2 %collective-permute-start.64 = (bf16[56,1920]{1,0:T(8,128)(2,1)S(1)}, bf16[56,1920]{1,0:T(8,128)(2,1)S(1)}, u32[]{:S(2)}, u32[]{:S(2)}) collective-permute-start(bf16[56,1920]{1,0:T(8,128)(2,1)S(1)} %fusion.134), channel_id=1, source_target_pairs={{2,0},{4,2},{6,4},{0,6},{3,1},{5,3},{7,5},{1,7},{10,8},{12,10},{14... | collective-permute-start | bytes 645128 | tf_op jit(solution)/shard_map/ppermute | solution.py:52
  438.6 28.5 %collective-permute-start.57 = (bf16[56,1920]{1,0:T(8,128)(2,1)S(1)}, bf16[56,1920]{1,0:T(8,128)(2,1)S(1)}, u32[]{:S(2)}, u32[]{:S(2)}) collective-permute-start(bf16[56,1920]{1,0:T(8,128)(2,1)S(1)} %fusion.136), channel_id=1, source_target_pairs={{2,0},{4,2},{6,4},{0,6},{3,1},{5,3},{7,5},{1,7},{10,8},{12,10},{14... | collective-permute-start | bytes 645128 | tf_op jit(solution)/shard_map/ppermute | solution.py:52
  443.2 28.5 %collective-permute-start.71 = (bf16[56,1920]{1,0:T(8,128)(2,1)S(1)}, bf16[56,1920]{1,0:T(8,128)(2,1)S(1)}, u32[]{:S(2)}, u32[]{:S(2)}) collective-permute-start(bf16[56,1920]{1,0:T(8,128)(2,1)S(1)} %fusion.132), channel_id=1, source_target_pairs={{2,0},{4,2},{6,4},{0,6},{3,1},{5,3},{7,5},{1,7},{10,8},{12,10},{14... | collective-permute-start | bytes 645128 | tf_op jit(solution)/shard_map/ppermute | solution.py:52
  462.5 33.7 %collective-permute-start.65 = (bf16[56,1920]{1,0:T(8,128)(2,1)S(1)}, bf16[56,1920]{1,0:T(8,128)(2,1)}, u32[]{:S(2)}, u32[]{:S(2)}) collective-permute-start(bf16[56,1920]{1,0:T(8,128)(2,1)S(1)} %fusion.133), channel_id=1, source_target_pairs={{2,0},{4,2},{6,4},{0,6},{3,1},{5,3},{7,5},{1,7},{10,8},{12,10},{14... | collective-permute-start | bytes 645128 | tf_op jit(solution)/shard_map/ppermute | solution.py:52
  467.1 32.2 %collective-permute-start.58 = (bf16[56,1920]{1,0:T(8,128)(2,1)S(1)}, bf16[56,1920]{1,0:T(8,128)(2,1)}, u32[]{:S(2)}, u32[]{:S(2)}) collective-permute-start(bf16[56,1920]{1,0:T(8,128)(2,1)S(1)} %fusion.135), channel_id=1, source_target_pairs={{2,0},{4,2},{6,4},{0,6},{3,1},{5,3},{7,5},{1,7},{10,8},{12,10},{14... | collective-permute-start | bytes 645128 | tf_op jit(solution)/shard_map/ppermute | solution.py:52
  471.8 31.1 %collective-permute-start.72 = (bf16[56,1920]{1,0:T(8,128)(2,1)S(1)}, bf16[56,1920]{1,0:T(8,128)(2,1)}, u32[]{:S(2)}, u32[]{:S(2)}) collective-permute-start(bf16[56,1920]{1,0:T(8,128)(2,1)S(1)} %fusion.131), channel_id=1, source_target_pairs={{2,0},{4,2},{6,4},{0,6},{3,1},{5,3},{7,5},{1,7},{10,8},{12,10},{14... | collective-permute-start | bytes 645128 | tf_op jit(solution)/shard_map/ppermute | solution.py:52
  494.9 28.4 %collective-permute-start.43 = (bf16[2,512,128]{2,1,0:T(8,128)(2,1)S(1)}, bf16[2,512,128]{2,1,0:T(8,128)(2,1)S(1)}, u32[]{:S(2)}, u32[]{:S(2)}) collective-permute-start(bf16[2,512,128]{2,1,0:T(8,128)(2,1)S(1)} %slice_bitcast_fusion.7), channel_id=1, source_target_pairs={{6,0},{7,1},{14,8},{15,9},{22,16},{23,17},{30,24},{31,25}} | collective-permute-start | bytes 786440 | tf_op jit(solution)/shard_map/ppermute | solution.py:430
  496.3 27.0 %collective-permute-start.41 = (bf16[2,512,128]{2,1,0:T(8,128)(2,1)S(1)}, bf16[2,512,128]{2,1,0:T(8,128)(2,1)S(1)}, u32[]{:S(2)}, u32[]{:S(2)}) collective-permute-start(bf16[2,512,128]{2,1,0:T(8,128)(2,1)S(1)} %get-tuple-element.94), channel_id=1, source_target_pairs={{2,0},{4,2},{6,4},{3,1},{5,3},{7,5},{10,8},{12,10},{14,12},{11,9},... | collective-permute-start | bytes 786440 | tf_op jit(solution)/shard_map/ppermute | solution.py:430
  499.3 35.4 %collective-permute-start.42 = (bf16[2,512,128]{2,1,0:T(8,128)(2,1)S(1)}, bf16[2,512,128]{2,1,0:T(8,128)(2,1)S(1)}, u32[]{:S(2)}, u32[]{:S(2)}) collective-permute-start(bf16[2,512,128]{2,1,0:T(8,128)(2,1)S(1)} %get-tuple-element.95), channel_id=1, source_target_pairs={{4,0},{6,2},{5,1},{7,3},{12,8},{14,10},{13,9},{15,11},{20,16},{22,... | collective-permute-start | bytes 786440 | tf_op jit(solution)/shard_map/ppermute | solution.py:430
  507.3 38.3 %collective-permute-start.76 = (bf16[56,768]{1,0:T(8,128)(2,1)}, bf16[56,768]{1,0:T(8,128)(2,1)}, u32[]{:S(2)}, u32[]{:S(2)}) collective-permute-start(bf16[56,768]{1,0:T(8,128)(2,1)} %get-tuple-element.132), channel_id=1, source_target_pairs={{0,16},{8,24},{16,0},{24,8},{1,17},{9,25},{17,1},{25,9},{2,18},{10... | collective-permute-start | bytes 258056 | tf_op jit(solution)/shard_map/ppermute | solution.py:42
  507.4 35.3 %collective-permute-start.78 = (bf16[56,768]{1,0:T(8,128)(2,1)}, bf16[56,768]{1,0:T(8,128)(2,1)}, u32[]{:S(2)}, u32[]{:S(2)}) collective-permute-start(bf16[56,768]{1,0:T(8,128)(2,1)} %get-tuple-element.133), channel_id=1, source_target_pairs={{0,8},{8,0},{16,24},{24,16},{1,9},{9,1},{17,25},{25,17},{2,10},{10... | collective-permute-start | bytes 258056 | tf_op jit(solution)/shard_map/ppermute | solution.py:38
  542.5 38.6 %collective-permute-start.44 = (bf16[1024,896]{0,1:T(8,128)(2,1)S(1)}, bf16[1024,896]{0,1:T(8,128)(2,1)S(1)}, u32[]{:S(2)}, u32[]{:S(2)}) collective-permute-start(bf16[1024,896]{0,1:T(8,128)(2,1)S(1)} %convolution_convert_fusion), channel_id=1, source_target_pairs={{0,1},{1,0},{2,3},{3,2},{4,5},{5,4},{6,7},{7,6},{8,9},{9,8},{10,11... | collective-permute-start | bytes 5505032 | tf_op jit(solution)/shard_map/ppermute | solution.py:29
  (114 other events, 1524.5 us)

commit v2 on v1

--- a/solution.py
+++ b/solution.py
@@ -52,67 +52,99 @@
     return lax.ppermute(v, "ctx", [((i + 1) % n, i) for i in range(n)])
 
 
+def swap_xy(v):
+    return lax.ppermute(v, "fsdp", [(i, i ^ 3) for i in range(4)])
+
+
+def sum_all(v):
+    for axis in ("fsdp", "ctx"):
+        n = lax.axis_size(axis)
+        if n & (n - 1):
+            v = lax.psum(v, axis)
+            continue
+        step = 1
+        while step < n:
+            v = v + lax.ppermute(v, axis, [(i, i ^ step) for i in range(n)])
+            step *= 2
+    return v
+
+
 def relative_order():
     return lax.axis_size("fsdp") == 4 and lax.axis_size("ctx") % 2 == 0
 
 
-def gather_rows(w, plane_first=False):
+def ring_pieces(w):
+    pieces = [w]
+    for _ in range(lax.axis_size("ctx") - 1):
+        pieces.append(ring_up(pieces[-1]))
+    return pieces
+
+
+def gather_plane(w):
     if not relative_order():
-        return lax.all_gather(w, ("fsdp", "ctx"), axis=0, tiled=True)
-    steps = lax.axis_size("ctx") - 1
-    rows, cols = w.shape
-    if plane_first:
-        cut = cols // 256 * 128
-        x1, y1 = swap_x(w), swap_y(w)
-        d1 = jnp.concatenate([swap_y(x1[:, :cut]), swap_x(y1[:, cut:])], 1)
-        current = jnp.stack([w, x1, y1, d1])
-        pieces = [current]
-        for _ in range(steps):
-            current = ring_up(current)
-            pieces.append(current)
-        return jnp.stack(pieces, 1).reshape(-1, cols)
-    current = w
-    pieces = [w]
-    for _ in range(steps):
-        current = ring_up(current)
-        pieces.append(current)
-    own = jnp.concatenate(pieces, 0)
+        return [lax.all_gather(w, ("fsdp", "ctx"), axis=0, tiled=True)]
+    own = jnp.concatenate(ring_pieces(w), 0)
     half = own.shape[0] // 2
     xs, ys = swap_x(own), swap_y(own)
-    d1, d2 = swap_y(xs[:half]), swap_x(ys[half:])
-    return jnp.concatenate([own, xs, ys, d1, d2], 0)
-
-
-def add_low(a, b):
-    return (a.astype(f32) + b.astype(f32)).astype(bf16)
-
-
-def scatter_rows(g, plane_first=False):
+    return [own, xs, ys, swap_y(xs[:half]), swap_x(ys[half:])]
+
+
+def gather_line(w):
     if not relative_order():
-        return lax.psum_scatter(g, ("fsdp", "ctx"), scatter_dimension=0, tiled=True).astype(f32)
+        return [lax.all_gather(w, ("fsdp", "ctx"), axis=0, tiled=True)]
+    cols = w.shape[1]
+    pieces = ring_pieces(jnp.concatenate([w, swap_xy(w)], 1))
+    own = jnp.concatenate([p[:, :cols] for p in pieces], 0)
+    far = jnp.concatenate([p[:, cols:] for p in pieces], 0)
+    return [own, swap_x(own), swap_y(own), far]
+
+
+def add_low(*terms):
+    return sum(t.astype(f32) for t in terms).astype(bf16)
+
+
+def ring_sum(v, last=f32):
+    total = v[-1]
+    for s in range(v.shape[0] - 2, 0, -1):
+        total = add_low(ring_down(total), v[s])
+    return ring_down(total).astype(f32) + v[0].astype(f32)
+
+
+def scatter_plane(pieces):
+    if not relative_order():
+        return lax.psum_scatter(
+            pieces[0], ("fsdp", "ctx"), scatter_dimension=0, tiled=True
+        ).astype(f32)
     count = lax.axis_size("ctx")
-    cols = g.shape[1]
-    g = g.reshape(4, count, -1, cols)
-    if plane_first:
-        cut = cols // 256 * 128
-        total = g[:, count - 1]
-        for s in range(count - 2, -1, -1):
-            total = add_low(ring_down(total), g[:, s])
-        own, gx, gy, gd = (total[i] for i in range(4))
-        r1, r2 = swap_y(gd[:, :cut]), swap_x(gd[:, cut:])
-        gx = jnp.concatenate([add_low(gx[:, :cut], r1), gx[:, cut:]], 1)
-        gy = jnp.concatenate([gy[:, :cut], add_low(gy[:, cut:], r2)], 1)
-        return own.astype(f32) + swap_x(gx).astype(f32) + swap_y(gy).astype(f32)
-    half = count // 2
-    own, gx, gy, gd = (g[i] for i in range(4))
-    r1, r2 = swap_y(gd[:half]), swap_x(gd[half:])
+    own, gx, gy, g1, g2 = pieces
+    half = own.shape[0] // 2
+    r1, r2 = swap_y(g1), swap_x(g2)
     gx = jnp.concatenate([add_low(gx[:half], r1), gx[half:]], 0)
     gy = jnp.concatenate([gy[:half], add_low(gy[half:], r2)], 0)
-    plane = (own.astype(f32) + swap_x(gx).astype(f32) + swap_y(gy).astype(f32)).astype(bf16)
-    total = plane[count - 1]
-    for s in range(count - 2, 0, -1):
-        total = add_low(ring_down(total), plane[s])
-    return ring_down(total).astype(f32) + plane[0].astype(f32)
+    plane = add_low(own, swap_x(gx), swap_y(gy))
+    return ring_sum(plane.reshape(count, -1, own.shape[1]))
+
+
+def scatter_line(pieces):
+    if not relative_order():
+        return lax.psum_scatter(
+            pieces[0], ("fsdp", "ctx"), scatter_dimension=0, tiled=True
+        ).astype(f32)
+    count = lax.axis_size("ctx")
+    own, gx, gy, far = pieces
+    cols = own.shape[1]
+    plane = add_low(own, swap_x(gx), swap_y(gy))
+    both = jnp.concatenate([plane, far], 1).reshape(count, -1, 2 * cols)
+    total = ring_sum(both)
+    return total[:, :cols] + swap_xy(total[:, cols:].astype(bf16)).astype(f32)
+
+
+def row_pieces(g):
+    if not relative_order():
+        return [g]
+    part = g.shape[0] // 8
+    ends = [0, 2 * part, 4 * part, 6 * part, 7 * part, 8 * part]
+    return [g[a:b] for a, b in zip(ends[:-1], ends[1:])]
 
 
 def order_matrix(model_width):
@@ -282,19 +314,118 @@
     )(counts, queries, pos, kv, keys_t, mixed, lse, mixed_grad)
 
 
+def feed_kernel(starts, width, tile, *refs):
+    k = len(starts)
+    n_ref, c_ref = refs[:2]
+    w_refs = refs[2 : 2 + k]
+    out_ref, dn_ref = refs[2 + k : 4 + k]
+    g_refs = refs[4 + k : 4 + 2 * k]
+    gate_up, down, n_t, c_t, hidden_s, pair_s, out_acc, dn_acc = refs[4 + 2 * k :]
+    step = pl.program_id(0)
+
+    @pl.when(step == 0)
+    def _():
+        n_t[...] = n_ref[...].T
+        c_t[...] = c_ref[...].T
+        out_acc[...] = jnp.zeros(out_acc.shape, f32)
+        dn_acc[...] = jnp.zeros(dn_acc.shape, f32)
+
+    for start, w_ref in zip(starts, w_refs):
+        rows = slice(start, start + w_ref.shape[0])
+        gate_up[rows, :] = w_ref[:, : 2 * width]
+        down[rows, :] = w_ref[:, 2 * width :]
+
+    def token_tile(t, carry):
+        rows = pl.ds(pl.multiple_of(t * tile, tile), tile)
+        both = mm(n_ref[rows, :], gate_up[...])
+        hidden_grad = mm(c_ref[rows, :], down[...])
+        gate, up = both[:, :width], both[:, width:]
+        sigmoid = jax.nn.sigmoid(gate)
+        silu = gate * sigmoid
+        hidden = (silu * up).astype(bf16)
+        gate_grad = hidden_grad * up * (sigmoid * (1.0 + gate * (1.0 - sigmoid)))
+        pair = jnp.concatenate([gate_grad.astype(bf16), (hidden_grad * silu).astype(bf16)], 1)
+        hidden_s[rows, :] = hidden
+        pair_s[rows, :] = pair
+        out_acc[rows, :] += mm(hidden, down[...], contract_last)
+        dn_acc[rows, :] += mm(pair, gate_up[...], contract_last)
+        return carry
+
+    lax.fori_loop(0, n_ref.shape[0] // tile, token_tile, 0)
+    pair_grad = mm(n_t[...], pair_s[...]).astype(bf16)
+    down_grad = mm(c_t[...], hidden_s[...]).astype(bf16)
+    for start, g_ref in zip(starts, g_refs):
+        rows = slice(start, start + g_ref.shape[0])
+        g_ref[:, : 2 * width] = pair_grad[rows]
+        g_ref[:, 2 * width :] = down_grad[rows]
+
+    @pl.when(step == pl.num_programs(0) - 1)
+    def _():
+        out_ref[...] = out_acc[...].astype(bf16)
+        dn_ref[...] = dn_acc[...].astype(bf16)
+
+
+def feed_group(normed, upstream, pieces, width):
+    rows, model = normed.shape
+    chunks = pieces[0].shape[1] // (3 * width)
+    starts, start = [], 0
+    for p in pieces:
+        starts.append(start)
+        start += p.shape[0]
+    tile = min(rows, 256)
+    whole = pl.BlockSpec((rows, model), lambda j: (0, 0))
+    blocks = [pl.BlockSpec((p.shape[0], 3 * width), lambda j: (0, j)) for p in pieces]
+    hidden = chunks * width
+    return pl.pallas_call(
+        functools.partial(feed_kernel, starts, width, tile),
+        grid=(chunks,),
+        in_specs=[whole, whole] + blocks,
+        out_specs=[whole, whole] + blocks,
+        out_shape=[jax.ShapeDtypeStruct((rows, model), bf16)] * 2
+        + [jax.ShapeDtypeStruct(p.shape, bf16) for p in pieces],
+        scratch_shapes=[
+            pltpu.VMEM((model, 2 * width), bf16),
+            pltpu.VMEM((model, width), bf16),
+            pltpu.VMEM((model, rows), bf16),
+            pltpu.VMEM((model, rows), bf16),
+            pltpu.VMEM((rows, width), bf16),
+            pltpu.VMEM((rows, 2 * width), bf16),
+            pltpu.VMEM((rows, model), f32),
+            pltpu.VMEM((rows, model), f32),
+        ],
+        compiler_params=pltpu.CompilerParams(vmem_limit_bytes=VMEM_BYTES),
+        cost_estimate=pl.CostEstimate(
+            flops=18 * rows * model * hidden,
+            bytes_accessed=12 * model * hidden + 8 * rows * model,
+            transcendentals=rows * hidden,
+        ),
+        name="feed",
+    )(normed, upstream, *pieces)
+
+
 def rotate_rows(v, cosine, sine):
     half = HD // 2
     low, high = v[:, :half], v[:, half:]
     return jnp.concatenate([low * cosine - high * sine, high * cosine + low * sine], 1)
 
 
-def feed_parts(width):
-    tiles = width // 128
-    if width % 128 or tiles < 4:
-        return [(0, width)]
-    each = -(-tiles // 4)
-    ends = [0, each * 128, 2 * each * 128, 3 * each * 128, width]
-    return [(a, b) for a, b in zip(ends[:-1], ends[1:]) if b > a]
+def feed_plan(hidden):
+    tiles = hidden // 128
+    threes = next((b for b in range(tiles // 6, 0, -1) if (tiles - 3 * b) % 2 == 0), 0)
+    twos = (tiles - 3 * threes) // 2
+    if hidden % 128 or not threes or not twos:
+        return [(0, hidden, 1)]
+    return [(0, 256, twos), (256 * twos, 384, threes)]
+
+
+def pack_columns(arrays, first, width, chunks):
+    cut = [v[:, first : first + width * chunks].reshape(v.shape[0], chunks, width) for v in arrays]
+    return jnp.concatenate(cut, 2).reshape(arrays[0].shape[0], -1)
+
+
+def unpack_columns(v, width, chunks):
+    v = v.reshape(v.shape[0], chunks, 3, width)
+    return [v[:, :, i].reshape(v.shape[0], -1) for i in range(3)]
 
 
 def shards(
@@ -321,15 +452,15 @@
     half_len = block // tp
     half_start = lax.axis_index("tp") * half_len
 
-    pack_low = jnp.concatenate([qkv_weight[:, 0], out_weight], 1)
-    attention_full = gather_rows(pack_low)
+    attention_full = jnp.concatenate(gather_plane(jnp.concatenate([qkv_weight[:, 0], out_weight], 1)), 0)
     qkv_full = attention_full[:, :per_group]
     out_full = attention_full[:, per_group:]
-    parts = feed_parts(gate_weight.shape[1])
-    feed_full = []
-    for i, (a, b) in enumerate(parts):
-        own = jnp.concatenate([gate_weight[:, a:b], up_weight[:, a:b], down_weight[:, a:b]], 1)
-        feed_full.append(gather_rows(own, i == len(parts) - 1 and len(parts) > 1))
+    plan = feed_plan(gate_weight.shape[1])
+    routes = [(gather_line, scatter_line), (gather_plane, scatter_plane)]
+    feed_pieces = [
+        gather(pack_columns([gate_weight, up_weight, down_weight], *group))
+        for group, (gather, _) in zip(plan, routes)
+    ]
 
     order = order_matrix(width)
     x_low = to_relative(tokens.reshape(rows, width), order)
@@ -371,34 +502,14 @@
     unit_two = middle * scale_two
     normed_two = (unit_two * gain_two).astype(bf16)
 
-    feed_out = jnp.zeros((rows, width), f32)
-    normed_two_part = jnp.zeros((rows, width), f32)
-    feed_grads = []
-    for i, ((a, b), full) in enumerate(zip(parts, feed_full)):
-        c = b - a
-        gate_w, up_w, down_w = full[:, :c], full[:, c : 2 * c], full[:, 2 * c :]
-        gate_act = mm(normed_two, gate_w)
-        up_act = mm(normed_two, up_w)
-        hidden_grad = mm(upstream_low, down_w)
-        sigmoid = jax.nn.sigmoid(gate_act)
-        silu_gate = gate_act * sigmoid
-        hidden = (silu_gate * up_act).astype(bf16)
-        gate_grad = (hidden_grad * up_act * (sigmoid * (1.0 + gate_act * (1.0 - sigmoid)))).astype(bf16)
-        up_grad = (hidden_grad * silu_gate).astype(bf16)
-        feed_out = feed_out + mm(hidden, down_w, contract_last)
-        normed_two_part = (
-            normed_two_part + mm(gate_grad, gate_w, contract_last) + mm(up_grad, up_w, contract_last)
-        )
-        grads = jnp.concatenate(
-            [
-                mm(normed_two, gate_grad, contract_rows).astype(bf16),
-                mm(normed_two, up_grad, contract_rows).astype(bf16),
-                mm(upstream_low, hidden, contract_rows).astype(bf16),
-            ],
-            1,
-        )
-        total = scatter_rows(grads, i == len(parts) - 1 and len(parts) > 1)
-        feed_grads.append((total[:, :c], total[:, c : 2 * c], total[:, 2 * c :]))
+    feed_out, normed_two_part, feed_grads = [], [], []
+    for (first, chunk, chunks), pieces, (_, scatter) in zip(plan, feed_pieces, routes):
+        out_low, part_low, *grads = feed_group(normed_two, upstream_low, pieces, chunk)
+        feed_out.append(out_low)
+        normed_two_part.append(part_low)
+        feed_grads.append(unpack_columns(scatter(grads), chunk, chunks))
+    feed_out = sum(v.astype(f32) for v in feed_out)
+    normed_two_part = sum(v.astype(f32) for v in normed_two_part)
     feed_grads = [jnp.concatenate([p[j] for p in feed_grads], 1) for j in range(3)]
 
     feed_low = feed_out.astype(bf16).reshape(seqs, block, width)
@@ -436,7 +547,7 @@
     projected_grad = jnp.concatenate([turned_back, pack_t[HD:]], 0).astype(bf16)
     bias_grad = jnp.sum(projected_grad.astype(f32), 1)[None]
     qkv_weight_grad = mm(normed, projected_grad, contract_first_last_rows).astype(bf16)
-    attention_total = scatter_rows(jnp.concatenate([qkv_weight_grad, out_weight_grad], 1))
+    attention_total = scatter_plane(row_pieces(jnp.concatenate([qkv_weight_grad, out_weight_grad], 1)))
 
     normed_one_grad = sum_tp(mm(projected_grad, qkv_full, contract_first_last))
     gain_one_grad = jnp.sum(normed_one_grad * unit_one, 0, keepdims=True)
@@ -450,7 +561,9 @@
         gain_grads = lax.dot_general(
             gain_grads, order.astype(f32), contract_last, precision=lax.Precision.HIGHEST
         )
-    gain_total, bias_total = lax.psum((gain_grads, bias_grad), ("fsdp", "ctx"))
+    small = sum_all(jnp.concatenate([gain_grads.reshape(1, -1), bias_grad], 1))
+    gain_total = small[:, : 2 * width].reshape(2, width)
+    bias_total = small[:, 2 * width :]
     return (
         block_out,
         input_grad.reshape(seqs, block, width),

time: 647 us -> 500 us (0.77)
  matrix products: 128 us -> 27.5 us
  Pallas kernels: 21.1 us -> 92.6 us
  blocking collectives: 44.2 us -> 0 us
  waiting for transfers between devices: 185 us -> 147 us
  starting transfers between devices: 132 us -> 114 us
  other arithmetic: 60.5 us -> 52.5 us
    dot_general x47 -> x11, matrix products: 127 us -> 26 us  [mm(): return lax.dot_general(a, b, dims, preferred_element_type=f32)]
    pallas_call x0 -> x2, Pallas kernels: none -> 71.6 us  [feed_group(): pl.pallas_call(functools.partial(feed_kernel, starts, width, tile), grid=...]
    psum x1 -> x0, blocking collectives: 44.2 us -> none  [shards(): gain_total, bias_total = lax.psum((gain_grads, bias_grad), ('fsdp', 'ctx'))]
    ppermute x20 -> x10, waiting for transfers between devices: 31.6 us -> 13.9 us  [swap_y(): return lax.ppermute(v, 'fsdp', [(i, i ^ 2) for i in range(4)])]
    ppermute x3, waiting for transfers between devices: 27.1 us -> 9.95 us  [shards(): lax.ppermute(pack_grads[:, s], 'ctx', [(i + s, i) for i in range(count -...]
    ppermute x15 -> x9, starting transfers between devices: 36.2 us -> 22.9 us  [ring_up(): return lax.ppermute(v, 'ctx', [(i, (i + 1) % n) for i in range(n)])]
    ppermute x15 -> x9, starting transfers between devices: 40.7 us -> 31.1 us  [ring_down(): return lax.ppermute(v, 'ctx', [((i + 1) % n, i) for i in range(n)])]
    ppermute x15 -> x9, waiting for transfers between devices: 25.7 us -> 16.3 us  [ring_down(): return lax.ppermute(v, 'ctx', [((i + 1) % n, i) for i in range(n)])]
  transfers between devices with their start and end apart: 80 -> 54, of which waited for: 35 -> 20; matrix products, arithmetic and copies ran while one was open for 20% -> 25% of each run, Pallas kernels for 3% -> 12%
where the time goes in v2:
time: 500 us; the launch traced here: 494 us
  waiting for transfers between devices  147 us (29%)
  starting transfers between devices  114 us (23%)
  Pallas kernels  92.6 us (19%)
  local copies, waits for them, and re-layouts  58 us (12%)
  other arithmetic  52.5 us (10%)
  matrix products  27.5 us (6%)
    pallas_call x2, Pallas kernels, feed_group(): pl.pallas_call(functools.partial(feed_kernel, starts, width, tile), grid=...  71.6 us
    ppermute x10, waiting for transfers between devices, swap_x(): return lax.ppermute(v, 'fsdp', [(i, i ^ 1) for i in range(4)])  60.2 us
    ppermute x9, waiting for transfers between devices, ring_up(): return lax.ppermute(v, 'ctx', [(i, (i + 1) % n) for i in range(n)])  38.8 us
    ppermute x9, starting transfers between devices, ring_down(): return lax.ppermute(v, 'ctx', [((i + 1) % n, i) for i in range(n)])  31.1 us
    ppermute x10, starting transfers between devices, swap_x(): return lax.ppermute(v, 'fsdp', [(i, i ^ 1) for i in range(4)])  29.2 us
    dot_general x11, matrix products, mm(): return lax.dot_general(a, b, dims, preferred_element_type=f32)  26 us
    ppermute x9, starting transfers between devices, ring_up(): return lax.ppermute(v, 'ctx', [(i, (i + 1) % n) for i in range(n)])  22.9 us
    unnamed x120, local copies, waits for them, and re-layouts  21.2 us
  transfers between devices with their start and end apart: 54, of which 20 were waited for; matrix products, arithmetic and copies ran while one was open for 25% of the time, Pallas kernels for 12%

profile of v2, /device:TPU:0, one launch (start us, length us, event | category | flops | bytes accessed | tf_op | source)
XLA Modules:
  0.0 494.4 jit_solution(16032623176475619462)
XLA Ops:
  2.5 3.0 collective-permute-start
  8.1 2.5 collective-permute-start.11
  20.4 3.6 fusion.11
  24.2 3.6 convert_bitcast_fusion.refs_1_
  33.0 3.6 collective-permute-done.1
  37.3 5.9 %collective-permute-done.2 = bf16[56,1024]{1,0:T(8,128)(2,1)S(1)} collective-permute-done((bf16[56,1024]{1,0:T(8,128)(2,1)S(1)}, bf16[56,1024]{1,0:T(8,128)(2,1)S(1)}, u32[]{:S(2)}, u32[]{:S(2)}) %collective-permute-start.2) | collective-permute-done | bytes 114720 | tf_op jit(solution)/shard_map/ppermute | solution.py:47
  48.7 11.2 %collective-permute-done.18 = bf16[56,3456]{1,0:T(8,128)(2,1)} collective-permute-done((bf16[56,3456]{1,0:T(8,128)(2,1)}, bf16[56,3456]{1,0:T(8,128)(2,1)}, u32[]{:S(2)}, u32[]{:S(2)}) %collective-permute-start.18) | collective-permute-done | bytes 387104 | tf_op jit(solution)/shard_map/ppermute | solution.py:47
  65.1 2.8 collective-permute-done.5
  73.6 2.7 collective-permute-start.8
  76.3 5.0 %collective-permute-start.9 = (bf16[2,512,128]{1,2,0:T(8,128)(2,1)}, bf16[2,512,128]{1,2,0:T(8,128)(2,1)}, u32[]{:S(2)}, u32[]{:S(2)}) collective-permute-start(bf16[2,512,128]{1,2,0:T(8,128)(2,1)} %copy.36), channel_id=1, source_target_pairs={{0,6},{1,7},{8,14},{9,15},{16,22},{17,23},{24,30},{25,31}} | collective-permute-start | bytes 786440 | tf_op jit(solution)/shard_map/ppermute | solution.py:488
  81.4 3.4 collective-permute-start.7
  89.6 2.1 fusion.92
  91.7 5.3 %collective-permute-start.13 = (bf16[56,7680]{1,0:T(8,128)(2,1)}, bf16[56,7680]{1,0:T(8,128)(2,1)}, u32[]{:S(2)}, u32[]{:S(2)}) collective-permute-start(bf16[56,7680]{1,0:T(8,128)(2,1)} %collective-permute-done.12), channel_id=1, source_target_pairs={{0,2},{2,4},{4,6},{6,0},{1,3},{3,5},{5,7},{7,1},{8,10},{10,12},{12... | collective-permute-start | bytes 2580488 | tf_op jit(solution)/shard_map/ppermute | solution.py:47
  97.0 2.3 collective-permute-done.7
  99.3 2.2 fusion.90
  103.3 9.0 %attend.1 = (bf16[448,1024]{1,0:T(8,128)(2,1)S(1)}, f32[2,8,512]{2,1,0:T(8,128)S(1)}) custom-call(s32[2]{0:T(128)S(1)} %minimum_add_fusion.count_ref, bf16[448,1024]{1,0:T(8,128)(2,1)S(1)} %bitcast.104, s32[2,1,512]{2,1,0:T(1,128)S(1)} %reshape.326.pos_ref, bf16[2,4,512,128]{3,2,1,0:T(8,128)(2,1)S(1)} %copy.40.kv_ref, ...), custom_call_target="tpu_custom_call" | custom-call | flops 15032385536 | bytes 4194304 | tf_op jit(solution)/shard_map/attend/pallas_call | solution.py:264
  114.1 11.4 %collective-permute-start.14 = (bf16[56,7680]{1,0:T(8,128)(2,1)}, bf16[56,7680]{1,0:T(8,128)(2,1)S(1)}, u32[]{:S(2)}, u32[]{:S(2)}) collective-permute-start(bf16[56,7680]{1,0:T(8,128)(2,1)} %collective-permute-done.13), channel_id=1, source_target_pairs={{0,2},{2,4},{4,6},{6,0},{1,3},{3,5},{5,7},{7,1},{8,10},{10,12},{12... | collective-permute-start | bytes 2580488 | tf_op jit(solution)/shard_map/ppermute | solution.py:47
  132.9 17.9 %collective-permute-done.14 = bf16[56,7680]{1,0:T(8,128)(2,1)S(1)} collective-permute-done((bf16[56,7680]{1,0:T(8,128)(2,1)}, bf16[56,7680]{1,0:T(8,128)(2,1)S(1)}, u32[]{:S(2)}, u32[]{:S(2)}) %collective-permute-start.14) | collective-permute-done | bytes 860192 | tf_op jit(solution)/shard_map/ppermute | solution.py:47
  154.4 34.4 %feed.3 = (bf16[1024,896]{1,0:T(8,128)(2,1)}, bf16[1024,896]{1,0:T(8,128)(2,1)}, bf16[224,3456]{1,0:T(8,128)(2,1)S(1)}, bf16[224,3456]{1,0:T(8,128)(2,1)S(1)}, b...) custom-call(bf16[1024,896]{1,0:T(8,128)(2,1)} %multiply_convert_fusion.refs_0_, ...), custom_call_target="tpu_custom_call" | custom-call | flops 19025362944 | bytes 19726336 | tf_op jit(solution)/shard_map/feed/pallas_call | solution.py:379
  190.2 7.0 %collective-permute-start.15 = (bf16[224,3840]{1,0:T(8,128)(2,1)S(1)}, bf16[224,3840]{1,0:T(8,128)(2,1)S(1)}, u32[]{:S(2)}, u32[]{:S(2)}) collective-permute-start(bf16[224,3840]{1,0:T(8,128)(2,1)S(1)} %pad_maximum_fusion.1.refs_2_), channel_id=1, source_target_pairs={{0,8},{8,0},{16,24},{24,16},{1,9},{9,1},{17,25},{25,17},{2,10},{10... | collective-permute-start | bytes 5160968 | tf_op jit(solution)/shard_map/ppermute | solution.py:38
  199.4 9.6 %collective-permute-done.47 = bf16[112,3456]{1,0:T(8,128)(2,1)S(1)} collective-permute-done((bf16[112,3456]{1,0:T(8,128)(2,1)S(1)}, bf16[112,3456]{1,0:T(8,128)(2,1)S(1)}, u32[]{:S(2)}, u32[]{:S(2)}) %collective-permute-start.47) | collective-permute-done | bytes 774176 | tf_op jit(solution)/shard_map/ppermute | solution.py:42
  210.5 5.0 %collective-permute-start.48 = (bf16[224,3456]{1,0:T(8,128)(2,1)}, bf16[224,3456]{1,0:T(8,128)(2,1)}, u32[]{:S(2)}, u32[]{:S(2)}) collective-permute-start(bf16[224,3456]{1,0:T(8,128)(2,1)} %pad_maximum_fusion.3), channel_id=1, source_target_pairs={{0,8},{8,0},{16,24},{24,16},{1,9},{9,1},{17,25},{25,17},{2,10},{10... | collective-permute-start | bytes 4644872 | tf_op jit(solution)/shard_map/ppermute | solution.py:38
  215.4 36.8 %collective-permute-done.49 = bf16[112,3456]{1,0:T(8,128)(2,1)S(1)} collective-permute-done((bf16[112,3456]{1,0:T(8,128)(2,1)S(1)}, bf16[112,3456]{1,0:T(8,128)(2,1)S(1)}, u32[]{:S(2)}, u32[]{:S(2)}) %collective-permute-start.49) | collective-permute-done | bytes 774176 | tf_op jit(solution)/shard_map/ppermute | solution.py:38
  254.9 37.2 %feed.2 = (bf16[1024,896]{1,0:T(8,128)(2,1)}, bf16[1024,896]{1,0:T(8,128)(2,1)}, bf16[224,3840]{1,0:T(8,128)(2,1)S(1)}, bf16[224,3840]{1,0:T(8,128)(2,1)S(1)}, b...) custom-call(bf16[1024,896]{1,0:T(8,128)(2,1)} %multiply_convert_fusion.refs_0_, ...), custom_call_target="tpu_custom_call" | custom-call | flops 21139292160 | bytes 21102592 | tf_op jit(solution)/shard_map/feed/pallas_call | solution.py:379
  292.2 2.1 collective-permute-start.41
  296.2 2.7 add_convert_fusion
  300.1 2.4 add_convert_fusion.3
  304.8 2.2 fusion.37
  307.0 7.0 %collective-permute-done.51 = bf16[56,3456]{1,0:T(8,128)(2,1)S(1)} collective-permute-done((bf16[56,3456]{1,0:T(8,128)(2,1)S(1)}, bf16[56,3456]{1,0:T(8,128)(2,1)S(1)}, u32[]{:S(2)}, u32[]{:S(2)}) %collective-permute-start.51) | collective-permute-done | bytes 387104 | tf_op jit(solution)/shard_map/ppermute | solution.py:52
  314.1 3.6 collective-permute-start.52
  317.7 12.2 %collective-permute-done.41 = bf16[224,3840]{1,0:T(8,128)(2,1)S(1)} collective-permute-done((bf16[224,3840]{1,0:T(8,128)(2,1)S(1)}, bf16[224,3840]{1,0:T(8,128)(2,1)S(1)}, u32[]{:S(2)}, u32[]{:S(2)}) %collective-permute-start.41) | collective-permute-done | bytes 1720352 | tf_op jit(solution)/shard_map/ppermute | solution.py:38
  339.5 12.0 %attend_back.1 = (f32[448,1024]{1,0:T(8,128)}, bf16[2,4,512,128]{3,2,1,0:T(8,128)(2,1)S(1)}) custom-call(s32[2]{0:T(128)S(1)} %minimum_add_fusion.count_ref, bf16[448,1024]{1,0:T(8,128)(2,1)S(1)} %bitcast.105, s32[2,1,512]{2,1,0:T(1,128)S(1)} %reshape.326.pos_ref, bf16[2,4,512,128]{3,2,1,0:T(8,128)(2,1)S(1)} %copy.40.kv_ref, ...), custom_call_target="tpu_custom_call" | custom-call | flops 37580963840 | bytes 8388608 | tf_op jit(solution)/shard_map/attend_back/pallas_call | solution.py:293
  358.7 20.8 %collective-permute-start.53 = (bf16[56,3456]{1,0:T(8,128)(2,1)}, bf16[56,3456]{1,0:T(8,128)(2,1)}, u32[]{:S(2)}, u32[]{:S(2)}) collective-permute-start(bf16[56,3456]{1,0:T(8,128)(2,1)} %add_convert_fusion.11), channel_id=1, source_target_pairs={{2,0},{4,2},{6,4},{0,6},{3,1},{5,3},{7,5},{1,7},{10,8},{12,10},{14... | collective-permute-start | bytes 1161224 | tf_op jit(solution)/shard_map/ppermute | solution.py:52
  379.5 7.4 %collective-permute-done.27 = bf16[2,512,128]{2,1,0:T(8,128)(2,1)S(1)} collective-permute-done((bf16[2,512,128]{2,1,0:T(8,128)(2,1)S(1)}, bf16[2,512,128]{2,1,0:T(8,128)(2,1)S(1)}, u32[]{:S(2)}, u32[]{:S(2)}) %collective-permute-start.27) | collective-permute-done | bytes 262176 | tf_op jit(solution)/shard_map/ppermute | solution.py:541
  386.9 2.6 collective-permute-done.28
  397.6 7.6 %collective-permute-start.36 = (bf16[112,1024]{0,1:T(8,128)(2,1)S(1)}, bf16[112,1024]{0,1:T(8,128)(2,1)S(1)}, u32[]{:S(2)}, u32[]{:S(2)}) collective-permute-start(bf16[112,1024]{0,1:T(8,128)(2,1)S(1)} %get-tuple-element.91), channel_id=1, source_target_pairs={{0,8},{8,0},{16,24},{24,16},{1,9},{9,1},{17,25},{25,17},{2,10},{10... | collective-permute-start | bytes 688136 | tf_op jit(solution)/shard_map/ppermute | solution.py:38
  405.2 3.1 convolution_convert_fusion
  412.6 2.3 add_convert_fusion.6
  414.8 8.7 %collective-permute-done.35 = bf16[224,1024]{0,1:T(8,128)(2,1)S(1)} collective-permute-done((bf16[224,1024]{0,1:T(8,128)(2,1)S(1)}, bf16[224,1024]{0,1:T(8,128)(2,1)S(1)}, u32[]{:S(2)}, u32[]{:S(2)}) %collective-permute-start.35) | collective-permute-done | bytes 458784 | tf_op jit(solution)/shard_map/ppermute | solution.py:38
  428.7 2.3 reshape.348
  431.0 9.2 %collective-permute-done.38 = bf16[56,1024]{0,1:T(8,128)(2,1)} collective-permute-done((bf16[56,1024]{0,1:T(8,128)(2,1)}, bf16[56,1024]{0,1:T(8,128)(2,1)}, u32[]{:S(2)}, u32[]{:S(2)}) %collective-permute-start.38) | collective-permute-done | bytes 114720 | tf_op jit(solution)/shard_map/ppermute | solution.py:52
  441.5 2.1 collective-permute-start.39
  443.6 4.6 slice_reduce_fusion.3
  453.0 2.3 add_convert_fusion.5
  455.7 3.4 fusion.10
  472.1 4.2 collective-permute-done.32
  480.3 5.2 %fusion.28 = bf16[1024,896]{1,0:T(8,128)(2,1)S(1)} fusion(f32[1024,896]{1,0:T(8,128)S(1)} %copy-done.8, bf16[896,1024]{0,1:T(8,128)(2,1)S(1)} %copy-done.13, bf16[1024,896]{1,0:T(8,128)(2,1)} %collective-permute-done.29, bf16[1024,896]{1,0:T(8,128)(2,1)} %convolution_convert_fusion, f32[1024]{0:T(1024)S(1)} %broadcast_multiply_fusion, ...), kind=kOutput, calls=%fused_computation.66 | convolution fusion | flops 1655980032 | bytes 11025408 | tf_op jit(solution)/shard_map/dot_general | solution.py:24
  489.3 2.3 slice_reduce_fusion
  (315 shorter events, 132.2 us)
Async XLA Ops:
  2.5 27.2 %collective-permute-start = (bf16[56,1024]{1,0:T(8,128)(2,1)}, bf16[56,1024]{1,0:T(8,128)(2,1)}, u32[]{:S(2)}, u32[]{:S(2)}) collective-permute-start(bf16[56,1024]{1,0:T(8,128)(2,1)} %get-tuple-element.81), channel_id=1, source_target_pairs={{0,2},{2,4},{4,6},{6,0},{1,3},{3,5},{5,7},{7,1},{8,10},{10,12},{12... | collective-permute-start | bytes 344072 | tf_op jit(solution)/shard_map/ppermute | solution.py:47
  8.1 39.7 %collective-permute-start.11 = (bf16[56,3840]{1,0:T(8,128)(2,1)S(1)}, bf16[56,3840]{1,0:T(8,128)(2,1)S(1)}, u32[]{:S(2)}, u32[]{:S(2)}) collective-permute-start(bf16[56,3840]{1,0:T(8,128)(2,1)S(1)} %bitcast.114), channel_id=1, source_target_pairs={{0,24},{8,16},{16,8},{24,0},{1,25},{9,17},{17,9},{25,1},{2,26},{10... | collective-permute-start | bytes 1290248 | tf_op jit(solution)/shard_map/ppermute | solution.py:56
  16.9 29.1 %collective-permute-start.17 = (bf16[56,3456]{1,0:T(8,128)(2,1)}, bf16[56,3456]{1,0:T(8,128)(2,1)}, u32[]{:S(2)}, u32[]{:S(2)}) collective-permute-start(bf16[56,3456]{1,0:T(8,128)(2,1)} %bitcast.36), channel_id=1, source_target_pairs={{0,2},{2,4},{4,6},{6,0},{1,3},{3,5},{5,7},{7,1},{8,10},{10,12},{12... | collective-permute-start | bytes 1161224 | tf_op jit(solution)/shard_map/ppermute | solution.py:47
  29.8 6.9 %collective-permute-start.1 = (bf16[56,1024]{1,0:T(8,128)(2,1)}, bf16[56,1024]{1,0:T(8,128)(2,1)S(1)}, u32[]{:S(2)}, u32[]{:S(2)}) collective-permute-start(bf16[56,1024]{1,0:T(8,128)(2,1)} %collective-permute-done), channel_id=1, source_target_pairs={{0,2},{2,4},{4,6},{6,0},{1,3},{3,5},{5,7},{7,1},{8,10},{10,12},{12... | collective-permute-start | bytes 344072 | tf_op jit(solution)/shard_map/ppermute | solution.py:47
  36.6 6.6 %collective-permute-start.2 = (bf16[56,1024]{1,0:T(8,128)(2,1)S(1)}, bf16[56,1024]{1,0:T(8,128)(2,1)S(1)}, u32[]{:S(2)}, u32[]{:S(2)}) collective-permute-start(bf16[56,1024]{1,0:T(8,128)(2,1)S(1)} %collective-permute-done.1), channel_id=1, source_target_pairs={{0,2},{2,4},{4,6},{6,0},{1,3},{3,5},{5,7},{7,1},{8,10},{10,12},{12... | collective-permute-start | bytes 344072 | tf_op jit(solution)/shard_map/ppermute | solution.py:47
  44.2 17.6 %collective-permute-start.3 = (bf16[224,1024]{1,0:T(8,128)(2,1)S(1)}, bf16[224,1024]{1,0:T(8,128)(2,1)S(1)}, u32[]{:S(2)}, u32[]{:S(2)}) collective-permute-start(bf16[224,1024]{1,0:T(8,128)(2,1)S(1)} %pad_maximum_fusion.17), channel_id=1, source_target_pairs={{0,8},{8,0},{16,24},{24,16},{1,9},{9,1},{17,25},{25,17},{2,10},{10... | collective-permute-start | bytes 1376264 | tf_op jit(solution)/shard_map/ppermute | solution.py:38
  44.8 18.6 %collective-permute-start.4 = (bf16[224,1024]{1,0:T(8,128)(2,1)S(1)}, bf16[224,1024]{1,0:T(8,128)(2,1)S(1)}, u32[]{:S(2)}, u32[]{:S(2)}) collective-permute-start(bf16[224,1024]{1,0:T(8,128)(2,1)S(1)} %pad_maximum_fusion.17), channel_id=1, source_target_pairs={{0,16},{8,24},{16,0},{24,8},{1,17},{9,25},{17,1},{25,9},{2,18},{10... | collective-permute-start | bytes 1376264 | tf_op jit(solution)/shard_map/ppermute | solution.py:42
  46.0 14.0 %collective-permute-start.18 = (bf16[56,3456]{1,0:T(8,128)(2,1)}, bf16[56,3456]{1,0:T(8,128)(2,1)}, u32[]{:S(2)}, u32[]{:S(2)}) collective-permute-start(bf16[56,3456]{1,0:T(8,128)(2,1)} %collective-permute-done.17), channel_id=1, source_target_pairs={{0,2},{2,4},{4,6},{6,0},{1,3},{3,5},{5,7},{7,1},{8,10},{10,12},{12... | collective-permute-start | bytes 1161224 | tf_op jit(solution)/shard_map/ppermute | solution.py:47
  48.7 40.4 %collective-permute-start.12 = (bf16[56,7680]{1,0:T(8,128)(2,1)}, bf16[56,7680]{1,0:T(8,128)(2,1)}, u32[]{:S(2)}, u32[]{:S(2)}) collective-permute-start(bf16[56,7680]{1,0:T(8,128)(2,1)} %pad_maximum_fusion.9), channel_id=1, source_target_pairs={{0,2},{2,4},{4,6},{6,0},{1,3},{3,5},{5,7},{7,1},{8,10},{10,12},{12... | collective-permute-start | bytes 2580488 | tf_op jit(solution)/shard_map/ppermute | solution.py:47
  60.0 25.8 %collective-permute-start.19 = (bf16[56,3456]{1,0:T(8,128)(2,1)}, bf16[56,3456]{1,0:T(8,128)(2,1)}, u32[]{:S(2)}, u32[]{:S(2)}) collective-permute-start(bf16[56,3456]{1,0:T(8,128)(2,1)} %collective-permute-done.18), channel_id=1, source_target_pairs={{0,2},{2,4},{4,6},{6,0},{1,3},{3,5},{5,7},{7,1},{8,10},{10,12},{12... | collective-permute-start | bytes 1161224 | tf_op jit(solution)/shard_map/ppermute | solution.py:47
  73.6 18.1 %collective-permute-start.8 = (bf16[2,512,128]{1,2,0:T(8,128)(2,1)}, bf16[2,512,128]{1,2,0:T(8,128)(2,1)}, u32[]{:S(2)}, u32[]{:S(2)}) collective-permute-start(bf16[2,512,128]{1,2,0:T(8,128)(2,1)} %copy.36), channel_id=1, source_target_pairs={{0,4},{2,6},{1,5},{3,7},{8,12},{10,14},{9,13},{11,15},{16,20},{18,... | collective-permute-start | bytes 786440 | tf_op jit(solution)/shard_map/ppermute | solution.py:488
  76.3 20.7 %collective-permute-start.9 = (bf16[2,512,128]{1,2,0:T(8,128)(2,1)}, bf16[2,512,128]{1,2,0:T(8,128)(2,1)}, u32[]{:S(2)}, u32[]{:S(2)}) collective-permute-start(bf16[2,512,128]{1,2,0:T(8,128)(2,1)} %copy.36), channel_id=1, source_target_pairs={{0,6},{1,7},{8,14},{9,15},{16,22},{17,23},{24,30},{25,31}} | collective-permute-start | bytes 786440 | tf_op jit(solution)/shard_map/ppermute | solution.py:488
  81.4 18.0 %collective-permute-start.7 = (bf16[2,512,128]{1,2,0:T(8,128)(2,1)}, bf16[2,512,128]{1,2,0:T(8,128)(2,1)}, u32[]{:S(2)}, u32[]{:S(2)}) collective-permute-start(bf16[2,512,128]{1,2,0:T(8,128)(2,1)} %copy.36), channel_id=1, source_target_pairs={{0,2},{2,4},{4,6},{1,3},{3,5},{5,7},{8,10},{10,12},{12,14},{9,11},... | collective-permute-start | bytes 786440 | tf_op jit(solution)/shard_map/ppermute | solution.py:488
  87.6 39.8 %collective-permute-start.20 = (bf16[224,3456]{1,0:T(8,128)(2,1)}, bf16[224,3456]{1,0:T(8,128)(2,1)}, u32[]{:S(2)}, u32[]{:S(2)}) collective-permute-start(bf16[224,3456]{1,0:T(8,128)(2,1)} %constant_dynamic-update-slice_fusion.8.refs_2_), channel_id=1, source_target_pairs={{0,8},{8,0},{16,24},{24,16},{1,9},{9,1},{17,25},{25,17},{2,10},{10... | collective-permute-start | bytes 4644872 | tf_op jit(solution)/shard_map/ppermute | solution.py:38
  89.1 41.1 %collective-permute-start.21 = (bf16[224,3456]{1,0:T(8,128)(2,1)}, bf16[224,3456]{1,0:T(8,128)(2,1)}, u32[]{:S(2)}, u32[]{:S(2)}) collective-permute-start(bf16[224,3456]{1,0:T(8,128)(2,1)} %constant_dynamic-update-slice_fusion.8.refs_2_), channel_id=1, source_target_pairs={{0,16},{8,24},{16,0},{24,8},{1,17},{9,25},{17,1},{25,9},{2,18},{10... | collective-permute-start | bytes 4644872 | tf_op jit(solution)/shard_map/ppermute | solution.py:42
  91.7 22.3 %collective-permute-start.13 = (bf16[56,7680]{1,0:T(8,128)(2,1)}, bf16[56,7680]{1,0:T(8,128)(2,1)}, u32[]{:S(2)}, u32[]{:S(2)}) collective-permute-start(bf16[56,7680]{1,0:T(8,128)(2,1)} %collective-permute-done.12), channel_id=1, source_target_pairs={{0,2},{2,4},{4,6},{6,0},{1,3},{3,5},{5,7},{7,1},{8,10},{10,12},{12... | collective-permute-start | bytes 2580488 | tf_op jit(solution)/shard_map/ppermute | solution.py:47
  114.0 37.8 %collective-permute-start.10 = (bf16[1024,896]{1,0:T(8,128)(2,1)S(1)}, bf16[1024,896]{1,0:T(8,128)(2,1)S(1)}, u32[]{:S(2)}, u32[]{:S(2)}) collective-permute-start(bf16[1024,896]{1,0:T(8,128)(2,1)S(1)} %convolution_convert_fusion.1), channel_id=1, source_target_pairs={{0,1},{1,0},{2,3},{3,2},{4,5},{5,4},{6,7},{7,6},{8,9},{9,8},{10,11... | collective-permute-start | bytes 5505032 | tf_op jit(solution)/shard_map/ppermute | solution.py:29
  114.1 36.8 %collective-permute-start.14 = (bf16[56,7680]{1,0:T(8,128)(2,1)}, bf16[56,7680]{1,0:T(8,128)(2,1)S(1)}, u32[]{:S(2)}, u32[]{:S(2)}) collective-permute-start(bf16[56,7680]{1,0:T(8,128)(2,1)} %collective-permute-done.13), channel_id=1, source_target_pairs={{0,2},{2,4},{4,6},{6,0},{1,3},{3,5},{5,7},{7,1},{8,10},{10,12},{12... | collective-permute-start | bytes 2580488 | tf_op jit(solution)/shard_map/ppermute | solution.py:47
  128.6 25.8 %collective-permute-start.22 = (bf16[112,3456]{1,0:T(8,128)(2,1)S(1)}, bf16[112,3456]{1,0:T(8,128)(2,1)S(1)}, u32[]{:S(2)}, u32[]{:S(2)}) collective-permute-start(bf16[112,3456]{1,0:T(8,128)(2,1)S(1)} %slice.334), channel_id=1, source_target_pairs={{0,16},{8,24},{16,0},{24,8},{1,17},{9,25},{17,1},{25,9},{2,18},{10... | collective-permute-start | bytes 2322440 | tf_op jit(solution)/shard_map/ppermute | solution.py:42
  131.4 23.0 %collective-permute-start.23 = (bf16[112,3456]{1,0:T(8,128)(2,1)S(1)}, bf16[112,3456]{1,0:T(8,128)(2,1)S(1)}, u32[]{:S(2)}, u32[]{:S(2)}) collective-permute-start(bf16[112,3456]{1,0:T(8,128)(2,1)S(1)} %slice.335), channel_id=1, source_target_pairs={{0,8},{8,0},{16,24},{24,16},{1,9},{9,1},{17,25},{25,17},{2,10},{10... | collective-permute-start | bytes 2322440 | tf_op jit(solution)/shard_map/ppermute | solution.py:38
  188.7 20.2 %collective-permute-start.47 = (bf16[112,3456]{1,0:T(8,128)(2,1)S(1)}, bf16[112,3456]{1,0:T(8,128)(2,1)S(1)}, u32[]{:S(2)}, u32[]{:S(2)}) collective-permute-start(bf16[112,3456]{1,0:T(8,128)(2,1)S(1)} %get-tuple-element.41), channel_id=1, source_target_pairs={{0,16},{8,24},{16,0},{24,8},{1,17},{9,25},{17,1},{25,9},{2,18},{10... | collective-permute-start | bytes 2322440 | tf_op jit(solution)/shard_map/ppermute | solution.py:42
  190.2 63.5 %collective-permute-start.15 = (bf16[224,3840]{1,0:T(8,128)(2,1)S(1)}, bf16[224,3840]{1,0:T(8,128)(2,1)S(1)}, u32[]{:S(2)}, u32[]{:S(2)}) collective-permute-start(bf16[224,3840]{1,0:T(8,128)(2,1)S(1)} %pad_maximum_fusion.1.refs_2_), channel_id=1, source_target_pairs={{0,8},{8,0},{16,24},{24,16},{1,9},{9,1},{17,25},{25,17},{2,10},{10... | collective-permute-start | bytes 5160968 | tf_op jit(solution)/shard_map/ppermute | solution.py:38
  197.2 57.8 %collective-permute-start.16 = (bf16[224,3840]{1,0:T(8,128)(2,1)S(1)}, bf16[224,3840]{1,0:T(8,128)(2,1)}, u32[]{:S(2)}, u32[]{:S(2)}) collective-permute-start(bf16[224,3840]{1,0:T(8,128)(2,1)S(1)} %pad_maximum_fusion.1.refs_2_), channel_id=1, source_target_pairs={{0,16},{8,24},{16,0},{24,8},{1,17},{9,25},{17,1},{25,9},{2,18},{10... | collective-permute-start | bytes 5160968 | tf_op jit(solution)/shard_map/ppermute | solution.py:42
  198.6 53.5 %collective-permute-start.49 = (bf16[112,3456]{1,0:T(8,128)(2,1)S(1)}, bf16[112,3456]{1,0:T(8,128)(2,1)S(1)}, u32[]{:S(2)}, u32[]{:S(2)}) collective-permute-start(bf16[112,3456]{1,0:T(8,128)(2,1)S(1)} %get-tuple-element.43), channel_id=1, source_target_pairs={{0,8},{8,0},{16,24},{24,16},{1,9},{9,1},{17,25},{25,17},{2,10},{10... | collective-permute-start | bytes 2322440 | tf_op jit(solution)/shard_map/ppermute | solution.py:38
  210.5 89.5 %collective-permute-start.48 = (bf16[224,3456]{1,0:T(8,128)(2,1)}, bf16[224,3456]{1,0:T(8,128)(2,1)}, u32[]{:S(2)}, u32[]{:S(2)}) collective-permute-start(bf16[224,3456]{1,0:T(8,128)(2,1)} %pad_maximum_fusion.3), channel_id=1, source_target_pairs={{0,8},{8,0},{16,24},{24,16},{1,9},{9,1},{17,25},{25,17},{2,10},{10... | collective-permute-start | bytes 4644872 | tf_op jit(solution)/shard_map/ppermute | solution.py:38
  253.6 46.5 %collective-permute-start.50 = (bf16[224,3456]{1,0:T(8,128)(2,1)}, bf16[224,3456]{1,0:T(8,128)(2,1)}, u32[]{:S(2)}, u32[]{:S(2)}) collective-permute-start(bf16[224,3456]{1,0:T(8,128)(2,1)} %pad_maximum_fusion.4), channel_id=1, source_target_pairs={{0,16},{8,24},{16,0},{24,8},{1,17},{9,25},{17,1},{25,9},{2,18},{10... | collective-permute-start | bytes 4644872 | tf_op jit(solution)/shard_map/ppermute | solution.py:42
  292.2 37.7 %collective-permute-start.41 = (bf16[224,3840]{1,0:T(8,128)(2,1)S(1)}, bf16[224,3840]{1,0:T(8,128)(2,1)S(1)}, u32[]{:S(2)}, u32[]{:S(2)}) collective-permute-start(bf16[224,3840]{1,0:T(8,128)(2,1)S(1)} %get-tuple-element.36), channel_id=1, source_target_pairs={{0,8},{8,0},{16,24},{24,16},{1,9},{9,1},{17,25},{25,17},{2,10},{10... | collective-permute-start | bytes 5160968 | tf_op jit(solution)/shard_map/ppermute | solution.py:38
  294.3 36.7 %collective-permute-start.42 = (bf16[224,3840]{1,0:T(8,128)(2,1)S(1)}, bf16[224,3840]{1,0:T(8,128)(2,1)S(1)}, u32[]{:S(2)}, u32[]{:S(2)}) collective-permute-start(bf16[224,3840]{1,0:T(8,128)(2,1)S(1)} %get-tuple-element.37), channel_id=1, source_target_pairs={{0,16},{8,24},{16,0},{24,8},{1,17},{9,25},{17,1},{25,9},{2,18},{10... | collective-permute-start | bytes 5160968 | tf_op jit(solution)/shard_map/ppermute | solution.py:42
  298.9 35.5 %collective-permute-start.25 = (bf16[1024,896]{1,0:T(8,128)(2,1)S(1)}, bf16[1024,896]{1,0:T(8,128)(2,1)S(1)}, u32[]{:S(2)}, u32[]{:S(2)}) collective-permute-start(bf16[1024,896]{1,0:T(8,128)(2,1)S(1)} %add_convert_fusion), channel_id=1, source_target_pairs={{0,1},{1,0},{2,3},{3,2},{4,5},{5,4},{6,7},{7,6},{8,9},{9,8},{10,11... | collective-permute-start | bytes 5505032 | tf_op jit(solution)/shard_map/ppermute | solution.py:29
  302.6 11.4 %collective-permute-start.51 = (bf16[56,3456]{1,0:T(8,128)(2,1)S(1)}, bf16[56,3456]{1,0:T(8,128)(2,1)S(1)}, u32[]{:S(2)}, u32[]{:S(2)}) collective-permute-start(bf16[56,3456]{1,0:T(8,128)(2,1)S(1)} %slice.374), channel_id=1, source_target_pairs={{2,0},{4,2},{6,4},{0,6},{3,1},{5,3},{7,5},{1,7},{10,8},{12,10},{14... | collective-permute-start | bytes 1161224 | tf_op jit(solution)/shard_map/ppermute | solution.py:52
  314.1 42.5 %collective-permute-start.52 = (bf16[56,3456]{1,0:T(8,128)(2,1)S(1)}, bf16[56,3456]{1,0:T(8,128)(2,1)S(1)}, u32[]{:S(2)}, u32[]{:S(2)}) collective-permute-start(bf16[56,3456]{1,0:T(8,128)(2,1)S(1)} %add_convert_fusion.12), channel_id=1, source_target_pairs={{2,0},{4,2},{6,4},{0,6},{3,1},{5,3},{7,5},{1,7},{10,8},{12,10},{14... | collective-permute-start | bytes 1161224 | tf_op jit(solution)/shard_map/ppermute | solution.py:52
  333.4 79.1 %collective-permute-start.43 = (bf16[56,7680]{1,0:T(8,128)(2,1)}, bf16[56,7680]{1,0:T(8,128)(2,1)}, u32[]{:S(2)}, u32[]{:S(2)}) collective-permute-start(bf16[56,7680]{1,0:T(8,128)(2,1)} %fusion.46), channel_id=1, source_target_pairs={{2,0},{4,2},{6,4},{0,6},{3,1},{5,3},{7,5},{1,7},{10,8},{12,10},{14... | collective-permute-start | bytes 2580488 | tf_op jit(solution)/shard_map/ppermute | solution.py:52
  351.5 28.0 %collective-permute-start.26 = (bf16[2,512,128]{2,1,0:T(8,128)(2,1)S(1)}, bf16[2,512,128]{2,1,0:T(8,128)(2,1)S(1)}, u32[]{:S(2)}, u32[]{:S(2)}) collective-permute-start(bf16[2,512,128]{2,1,0:T(8,128)(2,1)S(1)} %get-tuple-element.92), channel_id=1, source_target_pairs={{2,0},{4,2},{6,4},{3,1},{5,3},{7,5},{10,8},{12,10},{14,12},{11,9},... | collective-permute-start | bytes 786440 | tf_op jit(solution)/shard_map/ppermute | solution.py:541
  352.8 34.1 %collective-permute-start.27 = (bf16[2,512,128]{2,1,0:T(8,128)(2,1)S(1)}, bf16[2,512,128]{2,1,0:T(8,128)(2,1)S(1)}, u32[]{:S(2)}, u32[]{:S(2)}) collective-permute-start(bf16[2,512,128]{2,1,0:T(8,128)(2,1)S(1)} %get-tuple-element.93), channel_id=1, source_target_pairs={{4,0},{6,2},{5,1},{7,3},{12,8},{14,10},{13,9},{15,11},{20,16},{22,... | collective-permute-start | bytes 786440 | tf_op jit(solution)/shard_map/ppermute | solution.py:541
  354.1 35.3 %collective-permute-start.28 = (bf16[2,512,128]{2,1,0:T(8,128)(2,1)S(1)}, bf16[2,512,128]{2,1,0:T(8,128)(2,1)S(1)}, u32[]{:S(2)}, u32[]{:S(2)}) collective-permute-start(bf16[2,512,128]{2,1,0:T(8,128)(2,1)S(1)} %slice_bitcast_fusion.4), channel_id=1, source_target_pairs={{6,0},{7,1},{14,8},{15,9},{22,16},{23,17},{30,24},{31,25}} | collective-permute-start | bytes 786440 | tf_op jit(solution)/shard_map/ppermute | solution.py:541
  358.7 67.9 %collective-permute-start.53 = (bf16[56,3456]{1,0:T(8,128)(2,1)}, bf16[56,3456]{1,0:T(8,128)(2,1)}, u32[]{:S(2)}, u32[]{:S(2)}) collective-permute-start(bf16[56,3456]{1,0:T(8,128)(2,1)} %add_convert_fusion.11), channel_id=1, source_target_pairs={{2,0},{4,2},{6,4},{0,6},{3,1},{5,3},{7,5},{1,7},{10,8},{12,10},{14... | collective-permute-start | bytes 1161224 | tf_op jit(solution)/shard_map/ppermute | solution.py:52
  397.2 11.4 %collective-permute-start.34 = (bf16[112,1024]{0,1:T(8,128)(2,1)S(1)}, bf16[112,1024]{0,1:T(8,128)(2,1)S(1)}, u32[]{:S(2)}, u32[]{:S(2)}) collective-permute-start(bf16[112,1024]{0,1:T(8,128)(2,1)S(1)} %get-tuple-element.88), channel_id=1, source_target_pairs={{0,16},{8,24},{16,0},{24,8},{1,17},{9,25},{17,1},{25,9},{2,18},{10... | collective-permute-start | bytes 688136 | tf_op jit(solution)/shard_map/ppermute | solution.py:42
  397.6 12.0 %collective-permute-start.36 = (bf16[112,1024]{0,1:T(8,128)(2,1)S(1)}, bf16[112,1024]{0,1:T(8,128)(2,1)S(1)}, u32[]{:S(2)}, u32[]{:S(2)}) collective-permute-start(bf16[112,1024]{0,1:T(8,128)(2,1)S(1)} %get-tuple-element.91), channel_id=1, source_target_pairs={{0,8},{8,0},{16,24},{24,16},{1,9},{9,1},{17,25},{25,17},{2,10},{10... | collective-permute-start | bytes 688136 | tf_op jit(solution)/shard_map/ppermute | solution.py:38
  408.3 47.4 %collective-permute-start.29 = (bf16[1024,896]{1,0:T(8,128)(2,1)}, bf16[1024,896]{1,0:T(8,128)(2,1)}, u32[]{:S(2)}, u32[]{:S(2)}) collective-permute-start(bf16[1024,896]{1,0:T(8,128)(2,1)} %convolution_convert_fusion), channel_id=1, source_target_pairs={{0,1},{1,0},{2,3},{3,2},{4,5},{5,4},{6,7},{7,6},{8,9},{9,8},{10,11... | collective-permute-start | bytes 5505032 | tf_op jit(solution)/shard_map/ppermute | solution.py:29
  410.1 13.4 %collective-permute-start.35 = (bf16[224,1024]{0,1:T(8,128)(2,1)S(1)}, bf16[224,1024]{0,1:T(8,128)(2,1)S(1)}, u32[]{:S(2)}, u32[]{:S(2)}) collective-permute-start(bf16[224,1024]{0,1:T(8,128)(2,1)S(1)} %pad_maximum_fusion.14), channel_id=1, source_target_pairs={{0,8},{8,0},{16,24},{24,16},{1,9},{9,1},{17,25},{25,17},{2,10},{10... | collective-permute-start | bytes 1376264 | tf_op jit(solution)/shard_map/ppermute | solution.py:38
  412.4 11.4 %collective-permute-start.37 = (bf16[224,1024]{0,1:T(8,128)(2,1)S(1)}, bf16[224,1024]{0,1:T(8,128)(2,1)S(1)}, u32[]{:S(2)}, u32[]{:S(2)}) collective-permute-start(bf16[224,1024]{0,1:T(8,128)(2,1)S(1)} %pad_maximum_fusion.15), channel_id=1, source_target_pairs={{0,16},{8,24},{16,0},{24,8},{1,17},{9,25},{17,1},{25,9},{2,18},{10... | collective-permute-start | bytes 1376264 | tf_op jit(solution)/shard_map/ppermute | solution.py:42
  414.8 38.2 %collective-permute-start.44 = (bf16[56,7680]{1,0:T(8,128)(2,1)}, bf16[56,7680]{1,0:T(8,128)(2,1)}, u32[]{:S(2)}, u32[]{:S(2)}) collective-permute-start(bf16[56,7680]{1,0:T(8,128)(2,1)} %add_convert_fusion.6), channel_id=1, source_target_pairs={{2,0},{4,2},{6,4},{0,6},{3,1},{5,3},{7,5},{1,7},{10,8},{12,10},{14... | collective-permute-start | bytes 2580488 | tf_op jit(solution)/shard_map/ppermute | solution.py:52
  426.6 13.6 %collective-permute-start.38 = (bf16[56,1024]{0,1:T(8,128)(2,1)}, bf16[56,1024]{0,1:T(8,128)(2,1)}, u32[]{:S(2)}, u32[]{:S(2)}) collective-permute-start(bf16[56,1024]{0,1:T(8,128)(2,1)} %slice.357), channel_id=1, source_target_pairs={{2,0},{4,2},{6,4},{0,6},{3,1},{5,3},{7,5},{1,7},{10,8},{12,10},{14... | collective-permute-start | bytes 344072 | tf_op jit(solution)/shard_map/ppermute | solution.py:52
  441.5 8.9 %collective-permute-start.39 = (bf16[56,1024]{0,1:T(8,128)(2,1)S(1)}, bf16[56,1024]{0,1:T(8,128)(2,1)S(1)}, u32[]{:S(2)}, u32[]{:S(2)}) collective-permute-start(bf16[56,1024]{0,1:T(8,128)(2,1)S(1)} %add_convert_fusion.14), channel_id=1, source_target_pairs={{2,0},{4,2},{6,4},{0,6},{3,1},{5,3},{7,5},{1,7},{10,8},{12,10},{14... | collective-permute-start | bytes 344072 | tf_op jit(solution)/shard_map/ppermute | solution.py:52
  451.5 10.4 %collective-permute-start.40 = (bf16[56,1024]{0,1:T(8,128)(2,1)S(1)}, bf16[56,1024]{0,1:T(8,128)(2,1)S(1)}, u32[]{:S(2)}, u32[]{:S(2)}) collective-permute-start(bf16[56,1024]{0,1:T(8,128)(2,1)S(1)} %add_convert_fusion.13), channel_id=1, source_target_pairs={{2,0},{4,2},{6,4},{0,6},{3,1},{5,3},{7,5},{1,7},{10,8},{12,10},{14... | collective-permute-start | bytes 344072 | tf_op jit(solution)/shard_map/ppermute | solution.py:52
  455.3 21.4 %collective-permute-start.45 = (bf16[56,7680]{1,0:T(8,128)(2,1)}, bf16[56,7680]{1,0:T(8,128)(2,1)}, u32[]{:S(2)}, u32[]{:S(2)}) collective-permute-start(bf16[56,7680]{1,0:T(8,128)(2,1)} %add_convert_fusion.5), channel_id=1, source_target_pairs={{2,0},{4,2},{6,4},{0,6},{3,1},{5,3},{7,5},{1,7},{10,8},{12,10},{14... | collective-permute-start | bytes 2580488 | tf_op jit(solution)/shard_map/ppermute | solution.py:52
  476.4 11.2 %collective-permute-start.33 = (f32[1,2368]{1,0:T(1,128)S(1)}, f32[1,2368]{1,0:T(1,128)S(1)}, u32[]{:S(2)}, u32[]{:S(2)}) collective-permute-start(f32[1,2368]{1,0:T(1,128)S(1)} %add.244), channel_id=1, source_target_pairs={{0,4},{2,6},{4,0},{6,2},{1,5},{3,7},{5,1},{7,3},{8,12},{10,14},{12... | collective-permute-start | bytes 28424 | tf_op jit(solution)/shard_map/ppermute | solution.py:67
  478.2 10.6 %collective-permute-start.46 = (bf16[56,3840]{1,0:T(8,128)(2,1)S(1)}, bf16[56,3840]{1,0:T(8,128)(2,1)S(1)}, u32[]{:S(2)}, u32[]{:S(2)}) collective-permute-start(bf16[56,3840]{1,0:T(8,128)(2,1)S(1)} %slice.502), channel_id=1, source_target_pairs={{0,24},{8,16},{16,8},{24,0},{1,25},{9,17},{17,9},{25,1},{2,26},{10... | collective-permute-start | bytes 1290248 | tf_op jit(solution)/shard_map/ppermute | solution.py:56
  (56 other events, 488.7 us)

commit v3 on v2

v3 whole, which is shorter than its diff:
```python
import functools

import jax
import jax.numpy as jnp
from jax import lax
from jax.experimental import pallas as pl
from jax.experimental.pallas import tpu as pltpu
from jax.sharding import PartitionSpec as P

HD = 64
GROUP = 7

epsilon = 1e-06
rope_base = 1000000.0
masked_value = -1e30
contract_rows = (((0,), (0,)), ((), ()))
contract_last = (((1,), (1,)), ((), ()))
contract_first_last = (((0,), (1,)), ((), ()))
f32 = jnp.float32
bf16 = jnp.bfloat16


def mm(a, b, dims=(((1,), (0,)), ((), ()))):
    return lax.dot_general(a, b, dims, preferred_element_type=f32)


def after_all(values, *deps):
    return lax.optimization_barrier((*values, *deps))[: len(values)]


def swap_tp(v):
    n = lax.axis_size("tp")
    return lax.ppermute(v, "tp", [(i, (i + 1) % n) for i in range(n)])


def sum_tp(part):
    low = part.astype(bf16)
    return low.astype(f32) + swap_tp(low).astype(f32)


def swap_x(v):
    return lax.ppermute(v, "fsdp", [(i, i ^ 1) for i in range(4)])


def swap_y(v):
    return lax.ppermute(v, "fsdp", [(i, i ^ 2) for i in range(4)])


def exchange(v, axis):
    return lax.all_to_all(v, axis, 0, 0)


def spread(v, axis):
    return exchange(jnp.broadcast_to(v[None], (lax.axis_size(axis),) + v.shape), axis)


def after(v, *deps):
    return lax.optimization_barrier((v, *deps))[0]


def sum_all(v):
    return jnp.sum(spread(v, ("fsdp", "ctx")), 0)


def square_plane():
    return lax.axis_size("fsdp") == 4


def gather_line(w):
    return spread(w, "ctx").reshape(-1, w.shape[1])


def gather_rows(line):
    return spread(line, "fsdp").reshape(-1, line.shape[1])


def gather_pieces(line, far=None):
    if not square_plane():
        return [gather_rows(line)]
    xs, ys = swap_x(line), swap_y(line)
    if far is not None:
        return [line, xs, ys, far]
    half = line.shape[0] // 2
    return [line, xs, ys, swap_y(xs[:half]), swap_x(ys[half:])]


def piece_starts(rows):
    if not square_plane():
        return jnp.zeros((1,), jnp.int32)
    me = lax.axis_index("fsdp")
    far = (me ^ 3) * rows
    return jnp.stack([me * rows, (me ^ 1) * rows, (me ^ 2) * rows, far, far + rows // 2]).astype(jnp.int32)


def swap_xy(v):
    return lax.ppermute(v, "fsdp", [(i, i ^ 3) for i in range(4)])


def add_low(*terms):
    return sum(t.astype(f32) for t in terms).astype(bf16)


def sum_line(v):
    count = lax.axis_size("ctx")
    return jnp.sum(exchange(v.reshape(count, -1, v.shape[1]), "ctx").astype(f32), 0)


def sum_plane(g):
    n = lax.axis_size("fsdp")
    return jnp.sum(exchange(g.reshape(n, -1, g.shape[1]), "fsdp").astype(f32), 0).astype(bf16)


def start_far(pieces):
    return (*pieces[:3], swap_y(pieces[3]), swap_x(pieces[4]))


def finish_far(state, dep):
    own, gx, gy, r1, r2 = after_all(state, dep)
    half = own.shape[0] // 2
    gx = jnp.concatenate([add_low(gx[:half], r1), gx[half:]], 0)
    gy = jnp.concatenate([gy[:half], add_low(gy[half:], r2)], 0)
    return own, gx, gy


def start_near(state):
    own, gx, gy = state
    return own, swap_x(gx), swap_y(gy)


def finish_plane(state, dep):
    return add_low(*after_all(state, dep))


def finish_near(state, dep):
    terms = after_all(state, dep)
    n = lax.axis_size("ctx")
    rows = terms[0].shape[0] // n
    blocks = []
    for i in range(n):
        start = (lax.axis_index("ctx") + i) % n * rows
        blocks.append(add_low(*(lax.dynamic_slice_in_dim(t, start, rows, 0) for t in terms)))
    return blocks


def start_line(blocks):
    n = len(blocks)
    moved = [
        lax.ppermute(blocks[i], "ctx", [(j, (j + i) % n) for j in range(n)]) for i in range(1, n)
    ]
    return [blocks[0]] + moved


def finish_line(blocks, dep):
    return sum(v.astype(f32) for v in after_all(blocks, dep))


def allowed_pairs(pos, offset, keys, block):
    gap = (
        lax.broadcasted_iota(jnp.int32, (keys, block), 1)
        - lax.broadcasted_iota(jnp.int32, (keys, block), 0)
        + offset
    )
    return (gap >= 0) & (gap <= pos)


def attend_kernel(
    seq, count_ref, q_ref, pos_ref, kv_ref, vt_ref, _, o_ref, lse_ref, m_ref, l_ref, acc_ref
):
    block = q_ref.shape[1]
    pos = pos_ref[0]
    m_ref[...] = jnp.full(m_ref.shape, masked_value, f32)
    l_ref[...] = jnp.zeros(l_ref.shape, f32)
    acc_ref[...] = jnp.zeros(acc_ref.shape, f32)

    def step(s, carry):
        keep = allowed_pairs(pos, s * block, block, block)
        keys = kv_ref[0, s, :, :HD]
        values_t = vt_ref[0, s]
        for g in range(GROUP):
            rows = slice(g * HD, (g + 1) * HD)
            scores = jnp.where(keep, mm(keys, q_ref[rows, :]), masked_value)
            old = m_ref[g : g + 1, :]
            top = jnp.maximum(old, jnp.max(scores, 0, keepdims=True))
            weight = jnp.exp(scores - top)
            shrink = jnp.exp(old - top)
            m_ref[g : g + 1, :] = top
            l_ref[g : g + 1, :] = l_ref[g : g + 1, :] * shrink + jnp.sum(weight, 0, keepdims=True)
            acc_ref[rows, :] = acc_ref[rows, :] * shrink + mm(values_t, weight.astype(bf16))
        return carry

    lax.fori_loop(0, count_ref[seq], step, 0)
    for g in range(GROUP):
        rows = slice(g * HD, (g + 1) * HD)
        total = l_ref[g : g + 1, :]
        o_ref[rows, :] = (acc_ref[rows, :] / total).astype(bf16)
        lse_ref[0, g : g + 1, :] = m_ref[g : g + 1, :] + jnp.log(total)
    lse_ref[0, GROUP : GROUP + 1, :] = jnp.zeros((1, block), f32)


def attend_back_kernel(
    count_ref, q_ref, pos_ref, kv_ref, kt_ref, o_ref, lse_ref, do_ref, table_ref,
    dq_ref, dkv_ref, dq_acc
):
    block = q_ref.shape[1]
    last = count_ref.shape[0] - 1
    pos = pos_ref[0]
    dkv_ref[...] = jnp.zeros(dkv_ref.shape, bf16)
    dq_acc[...] = jnp.zeros(dq_acc.shape, f32)

    def step(s, carry):
        keep = allowed_pairs(pos, s * block, block, block)
        keys = kv_ref[0, s, :, :HD]
        values = kv_ref[0, s, :, HD:]
        keys_t = kt_ref[0, s]
        key_grad = jnp.zeros((block, HD), f32)
        value_grad = jnp.zeros((block, HD), f32)
        for g in range(GROUP):
            rows = slice(g * HD, (g + 1) * HD)
            query = q_ref[rows, :]
            grad = do_ref[rows, :]
            centre = jnp.sum(grad.astype(f32) * o_ref[rows, :].astype(f32), 0, keepdims=True)
            scores = mm(keys, query) - lse_ref[0, g : g + 1, :]
            probs = jnp.exp(jnp.where(keep, scores, masked_value))
            prob_grad = mm(values, grad)
            score_grad = (probs * (prob_grad - centre)).astype(bf16)
            value_grad = value_grad + mm(probs.astype(bf16), grad, contract_last)
            key_grad = key_grad + mm(score_grad, query, contract_last)
            dq_acc[rows, :] += mm(keys_t, score_grad)
        dkv_ref[count_ref[last] - s, 0, :, :HD] = key_grad.astype(bf16)
        dkv_ref[count_ref[last] - s, 0, :, HD:] = value_grad.astype(bf16)
        return carry

    lax.fori_loop(0, count_ref[pl.program_id(0)], step, 0)
    cosine, sine = table_ref[: HD // 2, :], table_ref[HD // 2 :, :]
    for g in range(GROUP):
        low = dq_acc[g * HD : g * HD + HD // 2, :] * HD ** (-0.5)
        high = dq_acc[g * HD + HD // 2 : (g + 1) * HD, :] * HD ** (-0.5)
        dq_ref[g * HD : g * HD + HD // 2, :] = (low * cosine + high * sine).astype(bf16)
        dq_ref[g * HD + HD // 2 : (g + 1) * HD, :] = (high * cosine - low * sine).astype(bf16)


def attention_specs(seq, block, count):
    return dict(
        wide=pl.BlockSpec((GROUP * HD, block), lambda i, *_: (0, seq + i)),
        pos=pl.BlockSpec((1, 1, block), lambda i, *_: (seq + i, 0, 0)),
        kv=pl.BlockSpec((1, count, block, 2 * HD), lambda i, *_: (seq + i, 0, 0, 0)),
        half=pl.BlockSpec((1, count, HD, block), lambda i, *_: (seq + i, 0, 0, 0)),
        lse=pl.BlockSpec((1, GROUP + 1, block), lambda i, *_: (i, 0, 0)),
        table=pl.BlockSpec((HD, block), lambda i, *_: (0, seq + i)),
        dkv=pl.BlockSpec((count, 1, block, 2 * HD), lambda i, *_: (0, i, 0, 0)),
        rest=pl.BlockSpec(memory_space=pl.ANY),
    )


VMEM_BYTES = 48 * 1024 * 1024


def attend(seq, counts, queries, pos, kv, values_t, mixed, block):
    count = kv.shape[1]
    spec = attention_specs(seq, block, count)
    work = GROUP * block * block * count
    return pl.pallas_call(
        functools.partial(attend_kernel, seq),
        grid_spec=pltpu.PrefetchScalarGridSpec(
            num_scalar_prefetch=1,
            grid=(1,),
            in_specs=[spec["wide"], spec["pos"], spec["kv"], spec["half"], spec["rest"]],
            out_specs=[spec["wide"], spec["lse"]],
            scratch_shapes=[
                pltpu.VMEM((GROUP + 1, block), f32),
                pltpu.VMEM((GROUP + 1, block), f32),
                pltpu.VMEM((GROUP * HD, block), f32),
            ],
        ),
        out_shape=[
            jax.ShapeDtypeStruct(queries.shape, bf16),
            jax.ShapeDtypeStruct((1, GROUP + 1, block), f32),
        ],
        input_output_aliases={5: 0},
        compiler_params=pltpu.CompilerParams(vmem_limit_bytes=VMEM_BYTES),
        cost_estimate=pl.CostEstimate(
            flops=4 * HD * work * 4, bytes_accessed=2 * 1024 * 1024, transcendentals=work
        ),
        name="attend",
    )(counts, queries, pos, kv, values_t, mixed)


def attend_back(counts, queries, pos, kv, keys_t, mixed, lse, mixed_grad, tables, block):
    seqs, count = kv.shape[:2]
    spec = attention_specs(0, block, count)
    work = seqs * GROUP * block * block * count
    return pl.pallas_call(
        attend_back_kernel,
        grid_spec=pltpu.PrefetchScalarGridSpec(
            num_scalar_prefetch=1,
            grid=(seqs,),
            in_specs=[
                spec["wide"], spec["pos"], spec["kv"], spec["half"],
                spec["wide"], spec["lse"], spec["wide"], spec["table"],
            ],
            out_specs=[spec["wide"], spec["dkv"]],
            scratch_shapes=[pltpu.VMEM((GROUP * HD, block), f32)],
        ),
        out_shape=[
            jax.ShapeDtypeStruct(queries.shape, bf16),
            jax.ShapeDtypeStruct((count, seqs, block, 2 * HD), bf16),
        ],
        compiler_params=pltpu.CompilerParams(vmem_limit_bytes=VMEM_BYTES),
        cost_estimate=pl.CostEstimate(
            flops=10 * HD * work * 4, bytes_accessed=8 * 1024 * 1024, transcendentals=work
        ),
        name="attend_back",
    )(counts, queries, pos, kv, keys_t, mixed, lse, mixed_grad, tables)


def feed_kernel(k, grads, width, tile, start_ref, *refs):
    n_ref, c_ref = refs[:2]
    w_refs = refs[2 : 2 + k]
    out_ref, dn_ref = refs[2 + k : 4 + k]
    g_refs = refs[4 + k : 4 + k + grads]
    gate_up, down, n_t, c_t, hidden_s, pair_s, grad_s, out_acc, dn_acc = refs[4 + k + grads :]
    step = pl.program_id(0)

    @pl.when(step == 0)
    def _():
        n_t[...] = n_ref[...].T
        c_t[...] = c_ref[...].T
        out_acc[...] = jnp.zeros(out_acc.shape, f32)
        dn_acc[...] = jnp.zeros(dn_acc.shape, f32)

    def piece_rows(i, size):
        return pl.ds(pl.multiple_of(start_ref[i], size), size)

    for i, w_ref in enumerate(w_refs):
        rows = piece_rows(i, w_ref.shape[0])
        gate_up[rows, :] = w_ref[:, : 2 * width]
        down[rows, :] = w_ref[:, 2 * width :]

    def token_tile(t, carry):
        rows = pl.ds(pl.multiple_of(t * tile, tile), tile)
        both = mm(n_ref[rows, :], gate_up[...])
        hidden_grad = mm(c_ref[rows, :], down[...])
        gate, up = both[:, :width], both[:, width:]
        sigmoid = jax.nn.sigmoid(gate)
        silu = gate * sigmoid
        hidden = (silu * up).astype(bf16)
        gate_grad = hidden_grad * up * (sigmoid * (1.0 + gate * (1.0 - sigmoid)))
        pair = jnp.concatenate([gate_grad.astype(bf16), (hidden_grad * silu).astype(bf16)], 1)
        hidden_s[rows, :] = hidden
        pair_s[rows, :] = pair
        out_acc[rows, :] += mm(hidden, down[...], contract_last)
        dn_acc[rows, :] += mm(pair, gate_up[...], contract_last)
        return carry

    lax.fori_loop(0, n_ref.shape[0] // tile, token_tile, 0)
    grad_s[:, : 2 * width] = mm(n_t[...], pair_s[...]).astype(bf16)
    grad_s[:, 2 * width :] = mm(c_t[...], hidden_s[...]).astype(bf16)
    for i, g_ref in enumerate(g_refs):
        g_ref[...] = grad_s[piece_rows(i, g_ref.shape[0]), :]

    @pl.when(step == pl.num_programs(0) - 1)
    def _():
        out_ref[...] = out_acc[...].astype(bf16)
        dn_ref[...] = dn_acc[...].astype(bf16)


def feed_group(normed, upstream, pieces, width, chunks):
    rows, model = normed.shape
    tile = min(rows, 256)
    whole = pl.BlockSpec((rows, model), lambda j, *_: (0, 0))
    blocks = [pl.BlockSpec((p.shape[0], 3 * width), lambda j, *_: (0, j)) for p in pieces]
    hidden = chunks * width
    sizes = [p.shape[0] for p in pieces]
    if square_plane():
        sizes = sizes[:3] + [sizes[0] // 2] * 2
    grads = [pl.BlockSpec((r, 3 * width), lambda j, *_: (0, j)) for r in sizes]
    return pl.pallas_call(
        functools.partial(feed_kernel, len(pieces), len(sizes), width, tile),
        grid_spec=pltpu.PrefetchScalarGridSpec(
            num_scalar_prefetch=1,
            grid=(chunks,),
            in_specs=[whole, whole] + blocks,
            out_specs=[whole, whole] + grads,
            scratch_shapes=[
                pltpu.VMEM((model, 2 * width), bf16),
                pltpu.VMEM((model, width), bf16),
                pltpu.VMEM((model, rows), bf16),
                pltpu.VMEM((model, rows), bf16),
                pltpu.VMEM((rows, width), bf16),
                pltpu.VMEM((rows, 2 * width), bf16),
                pltpu.VMEM((model, 3 * width), bf16),
                pltpu.VMEM((rows, model), f32),
                pltpu.VMEM((rows, model), f32),
            ],
        ),
        out_shape=[jax.ShapeDtypeStruct((rows, model), bf16)] * 2
        + [jax.ShapeDtypeStruct((r, 3 * width * chunks), bf16) for r in sizes],
        compiler_params=pltpu.CompilerParams(vmem_limit_bytes=VMEM_BYTES),
        cost_estimate=pl.CostEstimate(
            flops=18 * rows * model * hidden,
            bytes_accessed=12 * model * hidden + 8 * rows * model,
            transcendentals=rows * hidden,
        ),
        name="feed",
    )(piece_starts(pieces[0].shape[0]), normed, upstream, *pieces)


def rotate_rows(v, cosine, sine):
    half = HD // 2
    low, high = v[:, :half], v[:, half:]
    return jnp.concatenate([low * cosine - high * sine, high * cosine + low * sine], 1)


def feed_plan(hidden):
    tiles = hidden // 128
    threes = next((b for b in range(tiles // 6, 0, -1) if (tiles - 3 * b) % 2 == 0), 0)
    if hidden % 128 or not threes:
        return [(0, hidden, 1)]
    return [(0, 384, threes), (384 * threes, 256, (tiles - 3 * threes) // 2)]


def pack_columns(arrays, first, width, chunks):
    cut = [v[:, first : first + width * chunks].reshape(v.shape[0], chunks, width) for v in arrays]
    return jnp.concatenate(cut, 2).reshape(arrays[0].shape[0], -1)


def unpack_columns(v, width, chunks):
    v = v.reshape(v.shape[0], chunks, 3, width)
    return [v[:, :, i].reshape(v.shape[0], -1) for i in range(3)]


def shards(
    tokens,
    cotangent,
    segments,
    positions,
    norm_one,
    qkv_weight,
    qkv_bias,
    out_weight,
    norm_two,
    gate_weight,
    up_weight,
    down_weight,
):
    del segments
    seqs, block, width = tokens.shape
    rows = seqs * block
    count = lax.axis_size("ctx")
    tp = lax.axis_size("tp")
    half_len = block // tp
    half_start = lax.axis_index("tp") * half_len

    query_cols = GROUP * HD
    every = ("fsdp", "ctx")
    kv_full = spread(qkv_weight[:, 0, query_cols:], every).reshape(width, -1)
    query_full = gather_rows(gather_line(after(qkv_weight[:, 0, :query_cols], kv_full)))

    inputs = tokens.reshape(rows, width).astype(f32)
    upstream_low = cotangent.reshape(rows, width)
    gain_one, gain_two = norm_one.astype(f32)[None], norm_two.astype(f32)[None]
    scale_one = lax.rsqrt(jnp.mean(inputs * inputs, -1, keepdims=True) + epsilon)
    unit_one = inputs * scale_one
    normed = (unit_one * gain_one).astype(bf16)

    bias = qkv_bias[0].astype(f32)[:, None]
    frequency = rope_base ** (-(jnp.arange(HD // 2, dtype=f32) * 2.0) / HD)
    angles = positions.reshape(1, rows).astype(f32) * frequency[:, None]
    cosine, sine = jnp.cos(angles), jnp.sin(angles)
    tables = jnp.concatenate([cosine, sine], 0)
    kv_projected = mm(kv_full, normed, contract_first_last) + bias[query_cols:]
    turned_key = rotate_rows(kv_projected[None, :HD], cosine, sine)[0]
    kv_t = jnp.concatenate([turned_key, kv_projected[HD:]], 0).astype(bf16)
    kv_own = kv_t.T.reshape(seqs, block, 2 * HD)
    kv_blocks = [kv_own]
    for s in range(1, count):
        kv_blocks.append(lax.ppermute(kv_own, "ctx", [(i, i + s) for i in range(count - s)]))
    plan = feed_plan(gate_weight.shape[1])
    packs = [pack_columns([gate_weight, up_weight, down_weight], *group) for group in plan]
    packs[0] = jnp.concatenate([packs[0], out_weight], 1)
    lines = [gather_line(after(packs[0], query_full, *kv_blocks[1:]))]
    far_packs = [swap_xy(after(own, kv_full)) for own in packs[1:]] if square_plane() else []
    kv = jnp.stack(after_all(kv_blocks, *far_packs), 1)
    kv_turned = jnp.swapaxes(kv, 2, 3)
    keys_t, values_t = kv_turned[:, :, :HD], kv_turned[:, :, HD:]
    projected = mm(query_full, normed, contract_first_last) + bias[:query_cols]
    turned = rotate_rows(projected.reshape(GROUP, HD, rows), cosine, sine)
    queries = (turned * HD ** (-0.5)).astype(bf16).reshape(query_cols, rows)
    place = jnp.arange(block, dtype=jnp.int32)
    reach = jnp.max(positions - place[None], 1)
    counts = 1 + jnp.minimum((jnp.maximum(reach, 0) + block - 1) // block, lax.axis_index("ctx"))
    counts = jnp.concatenate([counts, lax.axis_index("ctx")[None]]).astype(jnp.int32)
    pos = positions.reshape(seqs, 1, block)

    mixed, log_totals = jnp.zeros(queries.shape, bf16), []
    ready = queries
    for s in range(seqs):
        mixed, lse = attend(s, counts, ready, pos, kv, values_t, mixed, block)
        log_totals.append(lse)
    lines[0] = after(lines[0], mixed)
    for own in packs[1:]:
        lines.append(gather_line(after(own, lines[-1])))
    far_lines = [gather_line(after(own, lines[-1])) for own in far_packs]
    feed_pieces = [gather_pieces(lines[0])]
    for i, line in enumerate(lines[1:]):
        feed_pieces.append(gather_pieces(line, far_lines[i] if far_lines else None))
    out_full = jnp.zeros((width, query_cols), bf16)
    for start, piece in zip(piece_starts(feed_pieces[0][0].shape[0]), feed_pieces[0]):
        out_full = lax.dynamic_update_slice_in_dim(out_full, piece[:, -query_cols:], start, 0)
    branch = sum_tp(mm(mixed, out_full, contract_first_last))
    middle = inputs + branch
    scale_two = lax.rsqrt(jnp.mean(middle * middle, -1, keepdims=True) + epsilon)
    unit_two = middle * scale_two
    normed_two = (unit_two * gain_two).astype(bf16)

    feed_out, normed_two_part, far, near, blocks = [], [], [], [], []
    turn = normed_two
    staged = square_plane() and len(plan) == 2
    for i, ((first, chunk, chunks), pieces) in enumerate(zip(plan, feed_pieces)):
        if i + 1 < len(plan):
            turn = after(turn, lines[i + 1])
        out_low, part_low, *parts = feed_group(turn, upstream_low, pieces, chunk, chunks)
        feed_out.append(out_low)
        normed_two_part.append(part_low)
        turn = after(normed_two, part_low)
        if not staged:
            far.append(parts)
            continue
        if far:
            near.append(start_near(finish_far(far[-1], part_low)))
        far.append(start_far(parts))
    feed_out = sum(v.astype(f32) for v in feed_out)
    normed_two_part = sum(v.astype(f32) for v in normed_two_part)

    feed_low = feed_out.astype(bf16).reshape(seqs, block, width)

    def own_rows(v, start):
        return lax.dynamic_slice_in_dim(v, start, half_len, 1)

    other_start = (half_len * (tp - 1) - half_start) if tp == 2 else None
    feed_other = swap_tp(own_rows(feed_low, other_start))
    feed_sum = own_rows(feed_low, half_start).astype(f32) + feed_other.astype(f32)
    block_low = (own_rows(middle.reshape(seqs, block, width), half_start) + feed_sum).astype(bf16)
    block_out = block_low

    normed_two_grad = sum_tp(normed_two_part)
    gain_two_grad = jnp.sum(normed_two_grad * unit_two, 0, keepdims=True)
    scaled_two = normed_two_grad * gain_two
    middle_grad = upstream_low.astype(f32) + scale_two * (
        scaled_two - unit_two * jnp.mean(scaled_two * unit_two, -1, keepdims=True)
    )
    branch_low = middle_grad.astype(bf16)
    mixed_grad = mm(out_full, branch_low, contract_first_last).astype(bf16)
    out_weight_grad = mm(branch_low, mixed, contract_first_last_rows).astype(bf16)

    feed_totals, grad_in = [], mixed_grad
    if staged:
        second_far = finish_far(far[1], branch_low)
        grad_in = after(grad_in, *second_far)
        near.append(start_near(second_far))
    query_grads, pack_grads = attend_back(
        counts, queries, pos, kv, keys_t, mixed, jnp.concatenate(log_totals, 0), grad_in, tables,
        block,
    )
    if staged:
        blocks = finish_near(near[0], pack_grads)
        query_grads, pack_grads = after_all((query_grads, pack_grads), *blocks)
        line = start_line(blocks)
    pack_sum = jnp.sum(exchange(pack_grads, "ctx").astype(f32), 0)
    normed_one_part = mm(query_grads, query_full, contract_first_last)
    query_weight_grad = mm(normed, query_grads, contract_first_last_rows).astype(bf16)
    pack_t = pack_sum.reshape(rows, 2 * HD).T
    turned_back = rotate_rows(pack_t[None, :HD], cosine, -sine)[0]
    kv_grads = jnp.concatenate([turned_back, pack_t[HD:]], 0).astype(bf16)
    kv_weight_grad = mm(normed, kv_grads, contract_first_last_rows).astype(bf16)
    weight_grads = jnp.concatenate([query_weight_grad, kv_weight_grad, out_weight_grad], 1)
    attention_plane = sum_plane(weight_grads)
    attention_total = sum_line(attention_plane)
    kv_grads = after(kv_grads, weight_grads)
    if staged:
        feed_totals.append(finish_line(line, attention_plane))
        feed_totals.append(
            sum(v.astype(f32) for v in start_line(finish_near(near[1], attention_plane)))
        )
    else:
        for g in far:
            if square_plane():
                g = finish_near(start_near(finish_far(start_far(g), normed)), normed)
                feed_totals.append(sum(v.astype(f32) for v in start_line(g)))
            else:
                feed_totals.append(sum_line(sum_plane(g[0])))
    feed_grads = [
        unpack_columns(v, chunk, chunks) for v, (_, chunk, chunks) in zip(feed_totals, plan)
    ]
    feed_grads = [jnp.concatenate([p[j] for p in feed_grads], 1) for j in range(3)]
    bias_grad = jnp.concatenate(
        [jnp.sum(query_grads.astype(f32), 1), jnp.sum(kv_grads.astype(f32), 1)]
    )[None]

    normed_one_grad = sum_tp(normed_one_part + mm(kv_grads, kv_full, contract_first_last))
    gain_one_grad = jnp.sum(normed_one_grad * unit_one, 0, keepdims=True)
    scaled_one = normed_one_grad * gain_one
    input_grad = middle_grad + scale_one * (
        scaled_one - unit_one * jnp.mean(scaled_one * unit_one, -1, keepdims=True)
    )
    input_grad = input_grad.astype(bf16).astype(f32)
    gain_grads = jnp.concatenate([gain_one_grad, gain_two_grad], 0)
    small = sum_all(jnp.concatenate([gain_grads.reshape(1, -1), bias_grad], 1))
    gain_total = small[:, : 2 * width].reshape(2, width)
    bias_total = small[:, 2 * width :]
    return (
        block_out,
        input_grad.reshape(seqs, block, width),
        gain_total[0],
        attention_total[:, None, : query_cols + 2 * HD],
        bias_total,
        attention_total[:, query_cols + 2 * HD :],
        gain_total[1],
        feed_grads[0],
        feed_grads[1],
        feed_grads[2],
    )


contract_first_last_rows = (((0,), (1,)), ((), ()))


def solution(mesh):
    weight = P(("fsdp", "ctx"), "tp")
    return jax.shard_map(
        shards,
        mesh=mesh,
        in_specs=(
            P("fsdp", "ctx", None),
            P("fsdp", "ctx", None),
            P("fsdp", None),
            P("fsdp", "ctx"),
            P(),
            P(("fsdp", "ctx"), "tp", None),
            P("tp", None),
            weight,
            P(),
            weight,
            weight,
            weight,
        ),
        out_specs=(
            P("fsdp", ("ctx", "tp"), None),
            P("fsdp", "ctx", None),
            P(),
            P(("fsdp", "ctx"), "tp", None),
            P("tp", None),
            weight,
            P(),
            weight,
            weight,
            weight,
        ),
        check_vma=False,
    )
```

time: 500 us -> 520 us (1.040)
  waiting for transfers between devices: 147 us -> 165 us
  local copies, waits for them, and re-layouts: 58 us -> 45.5 us
  other arithmetic: 52.5 us -> 62 us
  matrix products: 27.5 us -> 19.1 us
  starting transfers between devices: 114 us -> 120 us
    all_to_all x0 -> x10, starting transfers between devices: none -> 77.8 us  [exchange(): return lax.all_to_all(v, axis, 0, 0)]
    all_to_all x0 -> x10, waiting for transfers between devices: none -> 65.6 us  [exchange(): return lax.all_to_all(v, axis, 0, 0)]
    ppermute x25 -> x6, starting transfers between devices: 62.1 us -> 14.1 us  [start_line(): lax.ppermute(blocks[i], 'ctx', [(j, (j + i) % n) for j in range(n)])]
    ppermute x25 -> x6, waiting for transfers between devices: 70.8 us -> 24.6 us  [start_line(): lax.ppermute(blocks[i], 'ctx', [(j, (j + i) % n) for j in range(n)])]
    ppermute x10 -> x7, waiting for transfers between devices: 60.2 us -> 40.9 us  [swap_x(): return lax.ppermute(v, 'fsdp', [(i, i ^ 1) for i in range(4)])]
    ppermute x10 -> x7, starting transfers between devices: 29.2 us -> 10 us  [swap_x(): return lax.ppermute(v, 'fsdp', [(i, i ^ 1) for i in range(4)])]
    ppermute x10 -> x7, waiting for transfers between devices: 13.9 us -> 28.2 us  [swap_y(): return lax.ppermute(v, 'fsdp', [(i, i ^ 2) for i in range(4)])]
    unnamed x120 -> x134, local copies, waits for them, and re-layouts: 21.2 us -> 8.59 us
  transfers between devices with their start and end apart: 54 -> 38, of which waited for: 20 -> 19; matrix products, arithmetic and copies ran while one was open for 25% -> 22% of each run, Pallas kernels for 12% -> 19%
where the time goes in v3:
time: 520 us; the launch traced here: 510 us
  waiting for transfers between devices  165 us (32%)
  starting transfers between devices  120 us (23%)
  Pallas kernels  95.7 us (18%)
  other arithmetic  62 us (12%)
  local copies, waits for them, and re-layouts  45.5 us (9%)
  matrix products  19.1 us (4%)
    all_to_all x10, starting transfers between devices, exchange(): return lax.all_to_all(v, axis, 0, 0)  77.8 us
    pallas_call x2, Pallas kernels, feed_group(): pl.pallas_call(functools.partial(feed_kernel, len(pieces), len(sizes), wi...  73.7 us
    all_to_all x10, waiting for transfers between devices, exchange(): return lax.all_to_all(v, axis, 0, 0)  65.6 us
    ppermute x7, waiting for transfers between devices, swap_x(): return lax.ppermute(v, 'fsdp', [(i, i ^ 1) for i in range(4)])  40.9 us
    ppermute x7, waiting for transfers between devices, swap_y(): return lax.ppermute(v, 'fsdp', [(i, i ^ 2) for i in range(4)])  28.2 us
    ppermute x6, waiting for transfers between devices, start_line(): lax.ppermute(blocks[i], 'ctx', [(j, (j + i) % n) for j in range(n)])  24.6 us
    dot_general x9, matrix products, mm(): return lax.dot_general(a, b, dims, preferred_element_type=f32)  19.1 us
    ppermute x6, starting transfers between devices, start_line(): lax.ppermute(blocks[i], 'ctx', [(j, (j + i) % n) for j in range(n)])  14.1 us
  transfers between devices with their start and end apart: 38, of which 19 were waited for; matrix products, arithmetic and copies ran while one was open for 22% of the time, Pallas kernels for 19%

profile of v3, /device:TPU:0, one launch (start us, length us, event | category | flops | bytes accessed | tf_op | source)
XLA Modules:
  0.0 509.8 jit_solution(15870760985354413493)
XLA Ops:
  2.4 8.3 %all-to-all-start = ((bf16[16,56,128]{2,1,0:T(8,128)(2,1)}), bf16[16,56,128]{2,1,0:T(8,128)(2,1)S(1)}, u32[]{:S(2)}, u32[]{:S(2)}) async-start(bf16[16,56,128]{2,1,0:T(8,128)(2,1)} %broadcast_in_dim.40), calls=%async_computation | async-start | bytes 458752 | tf_op jit(solution)/shard_map/all_to_all | solution.py:50
  17.2 3.4 all-to-all-done
  21.3 3.4 all-to-all-start.1
  27.6 3.6 all-to-all-done.1
  32.2 4.2 all-to-all-start.2
  36.8 3.4 collective-permute-start
  40.2 3.1 collective-permute-start.1
  44.6 2.9 collective-permute-start.3
  48.1 3.1 collective-permute-done.1
  51.2 2.8 collective-permute-done.2
  55.4 10.1 %all-to-all-start.3 = ((bf16[4,56,3904]{2,1,0:T(8,128)(2,1)}), bf16[4,56,3904]{2,1,0:T(8,128)(2,1)}, u32[]{:S(2)}, u32[]{:S(2)}) async-start(bf16[4,56,3904]{2,1,0:T(8,128)(2,1)} %broadcast_in_dim.47), calls=%async_computation.3 | async-start | bytes 3555328 | tf_op jit(solution)/shard_map/all_to_all | solution.py:50
  71.2 2.4 convolution_add_fusion
  74.2 4.7 attend.2
  79.0 4.9 attend.3
  83.9 14.5 %all-to-all-done.3 = bf16[4,56,3904]{2,1,0:T(8,128)(2,1)} async-done(((bf16[4,56,3904]{2,1,0:T(8,128)(2,1)}), bf16[4,56,3904]{2,1,0:T(8,128)(2,1)}, u32[]{:S(2)}, u32[]{:S(2)}) %all-to-all-start.3) | async-done | bytes 1749024 | tf_op jit(solution)/shard_map/all_to_all | solution.py:50
  98.3 2.6 collective-permute-start.4
  102.5 33.4 %collective-permute-done.4.refs_3_ = bf16[224,3904]{1,0:T(8,128)(2,1)S(1)} collective-permute-done((bf16[224,3904]{1,0:T(8,128)(2,1)}, bf16[224,3904]{1,0:T(8,128)(2,1)S(1)}, u32[]{:S(2)}, u32[]{:S(2)}) %collective-permute-start.4) | collective-permute-done | bytes 1749024 | tf_op jit(solution)/shard_map/ppermute | solution.py:42
  140.8 4.4 all-to-all-start.4
  151.2 5.1 %collective-permute-done.6.refs_5_ = bf16[112,3904]{1,0:T(8,128)(2,1)S(1)} collective-permute-done((bf16[112,3904]{1,0:T(8,128)(2,1)}, bf16[112,3904]{1,0:T(8,128)(2,1)S(1)}, u32[]{:S(2)}, u32[]{:S(2)}) %collective-permute-start.6) | collective-permute-done | bytes 874528 | tf_op jit(solution)/shard_map/ppermute | solution.py:46
  156.4 6.7 %collective-permute-done.7.refs_6_ = bf16[112,3904]{1,0:T(8,128)(2,1)S(1)} collective-permute-done((bf16[112,3904]{1,0:T(8,128)(2,1)S(1)}, bf16[112,3904]{1,0:T(8,128)(2,1)S(1)}, u32[]{:S(2)}, u32[]{:S(2)}) %collective-permute-start.7) | collective-permute-done | bytes 874528 | tf_op jit(solution)/shard_map/ppermute | solution.py:42
  164.0 2.6 convolution_convert_fusion
  167.3 13.4 %all-to-all-done.4 = bf16[4,56,3840]{2,1,0:T(8,128)(2,1)} async-done(((bf16[4,56,3840]{2,1,0:T(8,128)(2,1)}), bf16[4,56,3840]{2,1,0:T(8,128)(2,1)}, u32[]{:S(2)}, u32[]{:S(2)}) %all-to-all-start.4) | async-done | bytes 1720352 | tf_op jit(solution)/shard_map/all_to_all | solution.py:50
  185.1 4.6 all-to-all-start.5
  189.7 5.3 %multiply_reduce_fusion.2 = (f32[1024]{0:T(1024)S(1)}, f32[1024,896]{1,0:T(8,128)S(1)}, bf16[1024,896]{1,0:T(8,128)(2,1)}) fusion(bf16[1024,896]{1,0:T(8,128)(2,1)} %collective-permute-done.8, bf16[1024,896]{1,0:T(8,128)(2,1)} %convolution_convert_fusion, bf16[2,512,896]{2,1,0:T(8,128)(2,1)} %param.12, f32[896]{0:T(1024)S(1)} %convert_element_type.299, ...), kind=kLoop, calls=%fused_computation.27 | loop fusion | flops 9174016 | bytes 11021824 | tf_op jit(solution)/shard_map/reduce_sum | solution.py:512
  197.5 35.2 %feed.2 = (bf16[1024,896]{1,0:T(8,128)(2,1)}, bf16[1024,896]{1,0:T(8,128)(2,1)}, bf16[224,3456]{1,0:T(8,128)(2,1)S(1)}, bf16[224,3456]{1,0:T(8,128)(2,1)}, bf16[...) custom-call(s32[5]{0:T(128)S(1)} %stack.49.start_ref, ...), custom_call_target="tpu_custom_call" | custom-call | flops 19025362944 | bytes 19726336 | tf_op jit(solution)/shard_map/feed/pallas_call | solution.py:377
  234.7 38.5 %feed.3 = (bf16[1024,896]{1,0:T(8,128)(2,1)}, bf16[1024,896]{1,0:T(8,128)(2,1)}, bf16[224,3840]{1,0:T(8,128)(2,1)S(1)}, bf16[224,3840]{1,0:T(8,128)(2,1)S(1)}, b...) custom-call(s32[5]{0:T(128)S(1)} %stack.49.start_ref, ...), custom_call_target="tpu_custom_call" | custom-call | flops 21139292160 | bytes 21102592 | tf_op jit(solution)/shard_map/feed/pallas_call | solution.py:377
  290.0 7.4 %collective-permute-done.13 = bf16[112,3840]{1,0:T(8,128)(2,1)S(1)} collective-permute-done((bf16[112,3840]{1,0:T(8,128)(2,1)S(1)}, bf16[112,3840]{1,0:T(8,128)(2,1)S(1)}, u32[]{:S(2)}, u32[]{:S(2)}) %collective-permute-start.13) | collective-permute-done | bytes 860192 | tf_op jit(solution)/shard_map/ppermute | solution.py:46
  302.3 12.3 %attend_back.1 = (bf16[448,1024]{1,0:T(8,128)(2,1)S(1)}, bf16[4,2,512,128]{3,2,1,0:T(8,128)(2,1)S(1)}) custom-call(s32[3]{0:T(128)S(1)} %pad_add_fusion.count_ref, bf16[448,1024]{1,0:T(8,128)(2,1)S(1)} %bitcast.128, s32[2,1,512]{2,1,0:T(1,128)S(1)} %reshape.352.pos_ref, bf16[2,4,512,128]{3,2,1,0:T(8,128)(2,1)} %copy-done, ...), custom_call_target="tpu_custom_call" | custom-call | flops 37580963840 | bytes 8388608 | tf_op jit(solution)/shard_map/attend_back/pallas_call | solution.py:292
  314.6 15.7 %collective-permute-done.18 = bf16[224,3456]{1,0:T(8,128)(2,1)} collective-permute-done((bf16[224,3456]{1,0:T(8,128)(2,1)}, bf16[224,3456]{1,0:T(8,128)(2,1)}, u32[]{:S(2)}, u32[]{:S(2)}) %collective-permute-start.18) | collective-permute-done | bytes 1548320 | tf_op jit(solution)/shard_map/ppermute | solution.py:46
  330.5 3.5 add_convert_fusion.12
  334.0 14.4 %all-to-all-start.6 = ((bf16[4,2,512,128]{3,2,1,0:T(8,128)(2,1)}), bf16[4,2,512,128]{3,2,1,0:T(8,128)(2,1)}, u32[]{:S(2)}, u32[]{:S(2)}) async-start(bf16[4,2,512,128]{3,2,1,0:T(8,128)(2,1)} %copy-done.1), calls=%async_computation.6 | async-start | bytes 2097152 | tf_op jit(solution)/shard_map/all_to_all | solution.py:50
  348.4 2.6 add_convert_fusion.2
  357.8 15.2 %all-to-all-done.6 = bf16[4,2,512,128]{3,2,1,0:T(8,128)(2,1)} async-done(((bf16[4,2,512,128]{3,2,1,0:T(8,128)(2,1)}), bf16[4,2,512,128]{3,2,1,0:T(8,128)(2,1)}, u32[]{:S(2)}, u32[]{:S(2)}) %all-to-all-start.6) | async-done | bytes 1048608 | tf_op jit(solution)/shard_map/all_to_all | solution.py:50
  381.5 3.8 copy.69
  385.3 4.4 all-to-all-start.8
  389.8 3.3 add_convert_fusion.3
  397.3 2.5 fusion.39
  402.6 9.5 %all-to-all-done.8 = bf16[4,224,1024]{2,1,0:T(8,128)(2,1)} async-done(((bf16[4,224,1024]{2,1,0:T(8,128)(2,1)}), bf16[4,224,1024]{2,1,0:T(8,128)(2,1)}, u32[]{:S(2)}, u32[]{:S(2)}) %all-to-all-start.8) | async-done | bytes 1835040 | tf_op jit(solution)/shard_map/all_to_all | solution.py:50
  412.1 2.8 reduce_sum.124
  414.9 7.1 %collective-permute-done.21 = bf16[56,3456]{1,0:T(8,128)(2,1)} collective-permute-done((bf16[56,3456]{1,0:T(8,128)(2,1)}, bf16[56,3456]{1,0:T(8,128)(2,1)}, u32[]{:S(2)}, u32[]{:S(2)}) %collective-permute-start.21) | collective-permute-done | bytes 387104 | tf_op jit(solution)/shard_map/ppermute | solution.py:148
  421.9 3.1 add_convert_fusion.10
  425.0 7.8 %collective-permute-start.25 = (bf16[56,3840]{1,0:T(8,128)(2,1)}, bf16[56,3840]{1,0:T(8,128)(2,1)}, u32[]{:S(2)}, u32[]{:S(2)}) collective-permute-start(bf16[56,3840]{1,0:T(8,128)(2,1)} %get-tuple-element.156), channel_id=1, source_target_pairs={{0,2},{2,4},{4,6},{6,0},{1,3},{3,5},{5,7},{7,1},{8,10},{10,12},{12... | collective-permute-start | bytes 1290248 | tf_op jit(solution)/shard_map/ppermute | solution.py:148
  440.6 3.7 all-to-all-start.9
  444.3 15.7 %collective-permute-done.26 = bf16[56,3840]{1,0:T(8,128)(2,1)} collective-permute-done((bf16[56,3840]{1,0:T(8,128)(2,1)}, bf16[56,3840]{1,0:T(8,128)(2,1)}, u32[]{:S(2)}, u32[]{:S(2)}) %collective-permute-start.26) | collective-permute-done | bytes 430112 | tf_op jit(solution)/shard_map/ppermute | solution.py:148
  469.9 3.1 fusion.10
  473.1 4.1 fusion.9
  480.1 20.3 %all-to-all-start.7 = ((f32[16,1,2368]{2,1,0:T(1,128)}), f32[16,1,2368]{2,1,0:T(1,128)S(1)}, u32[]{:S(2)}, u32[]{:S(2)}) async-start(f32[16,1,2368]{2,1,0:T(1,128)} %broadcast_in_dim.55), calls=%async_computation.7 | async-start | bytes 311296 | tf_op jit(solution)/shard_map/all_to_all | solution.py:50
  502.0 6.0 %all-to-all-done.7 = f32[16,1,2368]{2,1,0:T(1,128)S(1)} async-done(((f32[16,1,2368]{2,1,0:T(1,128)}), f32[16,1,2368]{2,1,0:T(1,128)S(1)}, u32[]{:S(2)}, u32[]{:S(2)}) %all-to-all-start.7) | async-done | bytes 151584 | tf_op jit(solution)/shard_map/all_to_all | solution.py:50
  (305 shorter events, 112.6 us)
Async XLA Ops:
  2.4 18.2 %all-to-all-start = ((bf16[16,56,128]{2,1,0:T(8,128)(2,1)}), bf16[16,56,128]{2,1,0:T(8,128)(2,1)S(1)}, u32[]{:S(2)}, u32[]{:S(2)}) async-start(bf16[16,56,128]{2,1,0:T(8,128)(2,1)} %broadcast_in_dim.40), calls=%async_computation | async-start | bytes 458752 | tf_op jit(solution)/shard_map/all_to_all | solution.py:50
  10.7 36.8 %copy-start.57 = (f32[32]{0:T(128)}, f32[32]{0:T(128)S(1)}, u32[]{:S(2)}) copy-start(f32[32]{0:T(128)S(1)} %multiply_power_fusion) | copy-start | bytes 388
  13.0 34.6 %copy-start.48 = (f32[1,4,2,128]{3,1,2,0:T(4,128)}, f32[1,4,2,128]{3,1,2,0:T(4,128)S(1)}, u32[]{:S(2)}) copy-start(f32[1,4,2,128]{3,1,2,0:T(4,128)S(1)} %copy.73) | copy-start | bytes 12292
  21.3 9.9 %all-to-all-start.1 = ((bf16[4,56,448]{2,1,0:T(8,128)(2,1)}), bf16[4,56,448]{2,1,0:T(8,128)(2,1)S(1)}, u32[]{:S(2)}, u32[]{:S(2)}) async-start(bf16[4,56,448]{2,1,0:T(8,128)(2,1)} %broadcast_in_dim.41), calls=%async_computation.1 | async-start | bytes 458752 | tf_op jit(solution)/shard_map/all_to_all | solution.py:50
  32.2 21.9 %all-to-all-start.2 = ((bf16[4,224,448]{2,1,0:T(8,128)(2,1)}), bf16[4,224,448]{2,1,0:T(8,128)(2,1)}, u32[]{:S(2)}, u32[]{:S(2)}) async-start(bf16[4,224,448]{2,1,0:T(8,128)(2,1)} %broadcast_in_dim.43), calls=%async_computation.2 | async-start | bytes 1835008 | tf_op jit(solution)/shard_map/all_to_all | solution.py:50
  36.8 11.3 %collective-permute-start = (bf16[2,512,128]{1,2,0:T(8,128)(2,1)S(1)}, bf16[2,512,128]{1,2,0:T(8,128)(2,1)S(1)}, u32[]{:S(2)}, u32[]{:S(2)}) collective-permute-start(bf16[2,512,128]{1,2,0:T(8,128)(2,1)S(1)} %copy.60), channel_id=1, source_target_pairs={{0,2},{2,4},{4,6},{1,3},{3,5},{5,7},{8,10},{10,12},{12,14},{9,11},... | collective-permute-start | bytes 786440 | tf_op jit(solution)/shard_map/ppermute | solution.py:477
  40.2 11.0 %collective-permute-start.1 = (bf16[2,512,128]{1,2,0:T(8,128)(2,1)S(1)}, bf16[2,512,128]{1,2,0:T(8,128)(2,1)S(1)}, u32[]{:S(2)}, u32[]{:S(2)}) collective-permute-start(bf16[2,512,128]{1,2,0:T(8,128)(2,1)S(1)} %copy.60), channel_id=1, source_target_pairs={{0,4},{2,6},{1,5},{3,7},{8,12},{10,14},{9,13},{11,15},{16,20},{18,... | collective-permute-start | bytes 786440 | tf_op jit(solution)/shard_map/ppermute | solution.py:477
  43.3 10.8 %collective-permute-start.2 = (bf16[2,512,128]{1,2,0:T(8,128)(2,1)S(1)}, bf16[2,512,128]{1,2,0:T(8,128)(2,1)S(1)}, u32[]{:S(2)}, u32[]{:S(2)}) collective-permute-start(bf16[2,512,128]{1,2,0:T(8,128)(2,1)S(1)} %copy.60), channel_id=1, source_target_pairs={{0,6},{1,7},{8,14},{9,15},{16,22},{17,23},{24,30},{25,31}} | collective-permute-start | bytes 786440 | tf_op jit(solution)/shard_map/ppermute | solution.py:477
  44.6 21.0 %collective-permute-start.3 = (bf16[56,3840]{1,0:T(8,128)(2,1)S(1)}, bf16[56,3840]{1,0:T(8,128)(2,1)S(1)}, u32[]{:S(2)}, u32[]{:S(2)}) collective-permute-start(bf16[56,3840]{1,0:T(8,128)(2,1)S(1)} %bitcast.149), channel_id=1, source_target_pairs={{0,24},{8,16},{16,8},{24,0},{1,25},{9,17},{17,9},{25,1},{2,26},{10... | collective-permute-start | bytes 1290248 | tf_op jit(solution)/shard_map/ppermute | solution.py:96
  48.1 25.5 %copy-start.37 = (f32[32,1024]{1,0:T(8,128)}, f32[32,1024]{1,0:T(8,128)S(1)}, u32[]{:S(2)}) copy-start(f32[32,1024]{1,0:T(8,128)S(1)} %get-tuple-element.175) | copy-start | bytes 393220
  55.4 42.9 %all-to-all-start.3 = ((bf16[4,56,3904]{2,1,0:T(8,128)(2,1)}), bf16[4,56,3904]{2,1,0:T(8,128)(2,1)}, u32[]{:S(2)}, u32[]{:S(2)}) async-start(bf16[4,56,3904]{2,1,0:T(8,128)(2,1)} %broadcast_in_dim.47), calls=%async_computation.3 | async-start | bytes 3555328 | tf_op jit(solution)/shard_map/all_to_all | solution.py:50
  83.9 79.2 %copy-start.4 = (bf16[448,1024]{1,0:T(8,128)(2,1)}, bf16[448,1024]{1,0:T(8,128)(2,1)S(1)}, u32[]{:S(2)}) copy-start(bf16[448,1024]{1,0:T(8,128)(2,1)S(1)} %get-tuple-element.73.o_ref) | copy-start | bytes 2752516
  98.3 37.5 %collective-permute-start.4 = (bf16[224,3904]{1,0:T(8,128)(2,1)}, bf16[224,3904]{1,0:T(8,128)(2,1)S(1)}, u32[]{:S(2)}, u32[]{:S(2)}) collective-permute-start(bf16[224,3904]{1,0:T(8,128)(2,1)} %bitcast.22.refs_2_), channel_id=1, source_target_pairs={{0,8},{8,0},{16,24},{24,16},{1,9},{9,1},{17,25},{25,17},{2,10},{10... | collective-permute-start | bytes 5246984 | tf_op jit(solution)/shard_map/ppermute | solution.py:42
  101.0 44.2 %collective-permute-start.5 = (bf16[224,3904]{1,0:T(8,128)(2,1)}, bf16[224,3904]{1,0:T(8,128)(2,1)}, u32[]{:S(2)}, u32[]{:S(2)}) collective-permute-start(bf16[224,3904]{1,0:T(8,128)(2,1)} %bitcast.22.refs_2_), channel_id=1, source_target_pairs={{0,16},{8,24},{16,0},{24,8},{1,17},{9,25},{17,1},{25,9},{2,18},{10... | collective-permute-start | bytes 5246984 | tf_op jit(solution)/shard_map/ppermute | solution.py:46
  138.0 18.3 %collective-permute-start.6 = (bf16[112,3904]{1,0:T(8,128)(2,1)}, bf16[112,3904]{1,0:T(8,128)(2,1)S(1)}, u32[]{:S(2)}, u32[]{:S(2)}) collective-permute-start(bf16[112,3904]{1,0:T(8,128)(2,1)} %slice.220), channel_id=1, source_target_pairs={{0,16},{8,24},{16,0},{24,8},{1,17},{9,25},{17,1},{25,9},{2,18},{10... | collective-permute-start | bytes 2623496 | tf_op jit(solution)/shard_map/ppermute | solution.py:46
  140.8 39.9 %all-to-all-start.4 = ((bf16[4,56,3840]{2,1,0:T(8,128)(2,1)}), bf16[4,56,3840]{2,1,0:T(8,128)(2,1)}, u32[]{:S(2)}, u32[]{:S(2)}) async-start(bf16[4,56,3840]{2,1,0:T(8,128)(2,1)} %broadcast_in_dim.48), calls=%async_computation.4 | async-start | bytes 3440640 | tf_op jit(solution)/shard_map/all_to_all | solution.py:50
  146.4 16.6 %collective-permute-start.7 = (bf16[112,3904]{1,0:T(8,128)(2,1)S(1)}, bf16[112,3904]{1,0:T(8,128)(2,1)S(1)}, u32[]{:S(2)}, u32[]{:S(2)}) collective-permute-start(bf16[112,3904]{1,0:T(8,128)(2,1)S(1)} %slice.222), channel_id=1, source_target_pairs={{0,8},{8,0},{16,24},{24,16},{1,9},{9,1},{17,25},{25,17},{2,10},{10... | collective-permute-start | bytes 2623496 | tf_op jit(solution)/shard_map/ppermute | solution.py:42
  166.5 23.2 %collective-permute-start.8 = (bf16[1024,896]{1,0:T(8,128)(2,1)}, bf16[1024,896]{1,0:T(8,128)(2,1)}, u32[]{:S(2)}, u32[]{:S(2)}) collective-permute-start(bf16[1024,896]{1,0:T(8,128)(2,1)} %convolution_convert_fusion), channel_id=1, source_target_pairs={{0,1},{1,0},{2,3},{3,2},{4,5},{5,4},{6,7},{7,6},{8,9},{9,8},{10,11... | collective-permute-start | bytes 5505032 | tf_op jit(solution)/shard_map/ppermute | solution.py:33
  166.5 23.2 %copy-start.50 = (f32[1,4,2,128]{3,1,2,0:T(4,128)}, f32[1,4,2,128]{3,1,2,0:T(4,128)S(1)}, u32[]{:S(2)}) copy-start(f32[1,4,2,128]{3,1,2,0:T(4,128)S(1)} %copy.76) | copy-start | bytes 12292
  180.7 54.0 %collective-permute-start.10 = (bf16[224,3840]{1,0:T(8,128)(2,1)}, bf16[224,3840]{1,0:T(8,128)(2,1)}, u32[]{:S(2)}, u32[]{:S(2)}) collective-permute-start(bf16[224,3840]{1,0:T(8,128)(2,1)} %bitcast.29.refs_2_), channel_id=1, source_target_pairs={{0,16},{8,24},{16,0},{24,8},{1,17},{9,25},{17,1},{25,9},{2,18},{10... | collective-permute-start | bytes 5160968 | tf_op jit(solution)/shard_map/ppermute | solution.py:46
  181.2 53.5 %collective-permute-start.9 = (bf16[224,3840]{1,0:T(8,128)(2,1)}, bf16[224,3840]{1,0:T(8,128)(2,1)}, u32[]{:S(2)}, u32[]{:S(2)}) collective-permute-start(bf16[224,3840]{1,0:T(8,128)(2,1)} %bitcast.29.refs_2_), channel_id=1, source_target_pairs={{0,8},{8,0},{16,24},{24,16},{1,9},{9,1},{17,25},{25,17},{2,10},{10... | collective-permute-start | bytes 5160968 | tf_op jit(solution)/shard_map/ppermute | solution.py:42
  185.1 49.7 %all-to-all-start.5 = ((bf16[4,56,3840]{2,1,0:T(8,128)(2,1)}), bf16[4,56,3840]{2,1,0:T(8,128)(2,1)}, u32[]{:S(2)}, u32[]{:S(2)}) async-start(bf16[4,56,3840]{2,1,0:T(8,128)(2,1)} %broadcast_in_dim.49), calls=%async_computation.5 | async-start | bytes 3440640 | tf_op jit(solution)/shard_map/all_to_all | solution.py:50
  232.7 44.9 %collective-permute-start.15 = (bf16[112,3456]{1,0:T(8,128)(2,1)}, bf16[112,3456]{1,0:T(8,128)(2,1)}, u32[]{:S(2)}, u32[]{:S(2)}) collective-permute-start(bf16[112,3456]{1,0:T(8,128)(2,1)} %get-tuple-element.102), channel_id=1, source_target_pairs={{0,16},{8,24},{16,0},{24,8},{1,17},{9,25},{17,1},{25,9},{2,18},{10... | collective-permute-start | bytes 2322440 | tf_op jit(solution)/shard_map/ppermute | solution.py:46
  234.2 43.4 %collective-permute-start.16 = (bf16[112,3456]{1,0:T(8,128)(2,1)}, bf16[112,3456]{1,0:T(8,128)(2,1)}, u32[]{:S(2)}, u32[]{:S(2)}) collective-permute-start(bf16[112,3456]{1,0:T(8,128)(2,1)} %get-tuple-element.103), channel_id=1, source_target_pairs={{0,8},{8,0},{16,24},{24,16},{1,9},{9,1},{17,25},{25,17},{2,10},{10... | collective-permute-start | bytes 2322440 | tf_op jit(solution)/shard_map/ppermute | solution.py:42
  234.7 38.5 %copy-start.32 = (bf16[1024,896]{1,0:T(8,128)(2,1)S(1)}, bf16[1024,896]{1,0:T(8,128)(2,1)}, u32[]{:S(2)}) copy-start(bf16[1024,896]{1,0:T(8,128)(2,1)} %get-tuple-element.79) | copy-start | bytes 5505028
  275.4 9.8 %collective-permute-start.12 = (bf16[1024,896]{1,0:T(8,128)(2,1)S(1)}, bf16[1024,896]{1,0:T(8,128)(2,1)S(1)}, u32[]{:S(2)}, u32[]{:S(2)}) collective-permute-start(bf16[1024,896]{1,0:T(8,128)(2,1)S(1)} %add_convert_fusion.1), channel_id=1, source_target_pairs={{0,1},{1,0},{2,3},{3,2},{4,5},{5,4},{6,7},{7,6},{8,9},{9,8},{10,11... | collective-permute-start | bytes 5505032 | tf_op jit(solution)/shard_map/ppermute | solution.py:33
  275.4 22.0 %collective-permute-start.13 = (bf16[112,3840]{1,0:T(8,128)(2,1)S(1)}, bf16[112,3840]{1,0:T(8,128)(2,1)S(1)}, u32[]{:S(2)}, u32[]{:S(2)}) collective-permute-start(bf16[112,3840]{1,0:T(8,128)(2,1)S(1)} %get-tuple-element.89), channel_id=1, source_target_pairs={{0,16},{8,24},{16,0},{24,8},{1,17},{9,25},{17,1},{25,9},{2,18},{10... | collective-permute-start | bytes 2580488 | tf_op jit(solution)/shard_map/ppermute | solution.py:46
  276.1 22.0 %collective-permute-start.14 = (bf16[112,3840]{1,0:T(8,128)(2,1)S(1)}, bf16[112,3840]{1,0:T(8,128)(2,1)S(1)}, u32[]{:S(2)}, u32[]{:S(2)}) collective-permute-start(bf16[112,3840]{1,0:T(8,128)(2,1)S(1)} %get-tuple-element.90), channel_id=1, source_target_pairs={{0,8},{8,0},{16,24},{24,16},{1,9},{9,1},{17,25},{25,17},{2,10},{10... | collective-permute-start | bytes 2580488 | tf_op jit(solution)/shard_map/ppermute | solution.py:42
  280.2 50.0 %collective-permute-start.18 = (bf16[224,3456]{1,0:T(8,128)(2,1)}, bf16[224,3456]{1,0:T(8,128)(2,1)}, u32[]{:S(2)}, u32[]{:S(2)}) collective-permute-start(bf16[224,3456]{1,0:T(8,128)(2,1)} %pad_maximum_fusion.4), channel_id=1, source_target_pairs={{0,16},{8,24},{16,0},{24,8},{1,17},{9,25},{17,1},{25,9},{2,18},{10... | collective-permute-start | bytes 4644872 | tf_op jit(solution)/shard_map/ppermute | solution.py:46
  284.6 46.0 %collective-permute-start.17 = (bf16[224,3456]{1,0:T(8,128)(2,1)}, bf16[224,3456]{1,0:T(8,128)(2,1)}, u32[]{:S(2)}, u32[]{:S(2)}) collective-permute-start(bf16[224,3456]{1,0:T(8,128)(2,1)} %pad_maximum_fusion.3), channel_id=1, source_target_pairs={{0,8},{8,0},{16,24},{24,16},{1,9},{9,1},{17,25},{25,17},{2,10},{10... | collective-permute-start | bytes 4644872 | tf_op jit(solution)/shard_map/ppermute | solution.py:42
  314.6 19.5 %copy-start.1 = (bf16[4,2,512,128]{3,2,1,0:T(8,128)(2,1)}, bf16[4,2,512,128]{3,2,1,0:T(8,128)(2,1)S(1)}, u32[]{:S(2)}) copy-start(bf16[4,2,512,128]{3,2,1,0:T(8,128)(2,1)S(1)} %get-tuple-element.113) | copy-start | bytes 3145732
  334.0 39.0 %all-to-all-start.6 = ((bf16[4,2,512,128]{3,2,1,0:T(8,128)(2,1)}), bf16[4,2,512,128]{3,2,1,0:T(8,128)(2,1)}, u32[]{:S(2)}, u32[]{:S(2)}) async-start(bf16[4,2,512,128]{3,2,1,0:T(8,128)(2,1)} %copy-done.1), calls=%async_computation.6 | async-start | bytes 2097152 | tf_op jit(solution)/shard_map/all_to_all | solution.py:50
  352.1 37.7 %collective-permute-start.11 = (bf16[2,256,896]{2,1,0:T(8,128)(2,1)}, bf16[2,256,896]{2,1,0:T(8,128)(2,1)}, u32[]{:S(2)}, u32[]{:S(2)}) collective-permute-start(bf16[2,256,896]{2,1,0:T(8,128)(2,1)} %constant_dynamic-slice_fusion), channel_id=1, source_target_pairs={{0,1},{1,0},{2,3},{3,2},{4,5},{5,4},{6,7},{7,6},{8,9},{9,8},{10,11... | collective-permute-start | bytes 2752520 | tf_op jit(solution)/shard_map/ppermute | solution.py:33
  352.1 69.8 %collective-permute-start.24 = (bf16[224,3840]{1,0:T(8,128)(2,1)}, bf16[224,3840]{1,0:T(8,128)(2,1)}, u32[]{:S(2)}, u32[]{:S(2)}) collective-permute-start(bf16[224,3840]{1,0:T(8,128)(2,1)} %pad_maximum_fusion.2), channel_id=1, source_target_pairs={{0,16},{8,24},{16,0},{24,8},{1,17},{9,25},{17,1},{25,9},{2,18},{10... | collective-permute-start | bytes 5160968 | tf_op jit(solution)/shard_map/ppermute | solution.py:46
  352.1 69.8 %collective-permute-start.23 = (bf16[224,3840]{1,0:T(8,128)(2,1)}, bf16[224,3840]{1,0:T(8,128)(2,1)}, u32[]{:S(2)}, u32[]{:S(2)}) collective-permute-start(bf16[224,3840]{1,0:T(8,128)(2,1)} %pad_maximum_fusion.1), channel_id=1, source_target_pairs={{0,8},{8,0},{16,24},{24,16},{1,9},{9,1},{17,25},{25,17},{2,10},{10... | collective-permute-start | bytes 5160968 | tf_op jit(solution)/shard_map/ppermute | solution.py:42
  357.8 19.7 %copy-start.49 = (f32[1,4,2,128]{3,1,2,0:T(4,128)S(1)}, f32[1,4,2,128]{3,1,2,0:T(4,128)}, u32[]{:S(2)}) copy-start(f32[1,4,2,128]{3,1,2,0:T(4,128)} %copy-done.48) | copy-start | bytes 12292
  357.8 19.7 %copy-start.58 = (f32[32]{0:T(128)S(1)}, f32[32]{0:T(128)}, u32[]{:S(2)}) copy-start(f32[32]{0:T(128)} %copy-done.57) | copy-start | bytes 388
  385.3 26.7 %all-to-all-start.8 = ((bf16[4,224,1024]{2,1,0:T(8,128)(2,1)}), bf16[4,224,1024]{2,1,0:T(8,128)(2,1)}, u32[]{:S(2)}, u32[]{:S(2)}) async-start(bf16[4,224,1024]{2,1,0:T(8,128)(2,1)} %bitcast.133), calls=%async_computation.8 | async-start | bytes 3670016 | tf_op jit(solution)/shard_map/all_to_all | solution.py:50
  393.1 21.8 %collective-permute-start.20 = (bf16[56,3456]{1,0:T(8,128)(2,1)}, bf16[56,3456]{1,0:T(8,128)(2,1)}, u32[]{:S(2)}, u32[]{:S(2)}) collective-permute-start(bf16[56,3456]{1,0:T(8,128)(2,1)} %get-tuple-element.161), channel_id=1, source_target_pairs={{0,2},{2,4},{4,6},{6,0},{1,3},{3,5},{5,7},{7,1},{8,10},{10,12},{12... | collective-permute-start | bytes 1161224 | tf_op jit(solution)/shard_map/ppermute | solution.py:148
  393.1 28.8 %collective-permute-start.21 = (bf16[56,3456]{1,0:T(8,128)(2,1)}, bf16[56,3456]{1,0:T(8,128)(2,1)}, u32[]{:S(2)}, u32[]{:S(2)}) collective-permute-start(bf16[56,3456]{1,0:T(8,128)(2,1)} %get-tuple-element.160), channel_id=1, source_target_pairs={{0,4},{2,6},{4,0},{6,2},{1,5},{3,7},{5,1},{7,3},{8,12},{10,14},{12... | collective-permute-start | bytes 1161224 | tf_op jit(solution)/shard_map/ppermute | solution.py:148
  395.1 26.8 %collective-permute-start.22 = (bf16[56,3456]{1,0:T(8,128)(2,1)S(1)}, bf16[56,3456]{1,0:T(8,128)(2,1)}, u32[]{:S(2)}, u32[]{:S(2)}) collective-permute-start(bf16[56,3456]{1,0:T(8,128)(2,1)S(1)} %copy-done.47), channel_id=1, source_target_pairs={{0,6},{2,0},{4,2},{6,4},{1,7},{3,1},{5,3},{7,5},{8,14},{10,8},{12,... | collective-permute-start | bytes 1161224 | tf_op jit(solution)/shard_map/ppermute | solution.py:148
  414.8 20.3 %copy-start.34 = (bf16[56,3456]{1,0:T(8,128)(2,1)S(1)}, bf16[56,3456]{1,0:T(8,128)(2,1)}, u32[]{:S(2)}) copy-start(bf16[56,3456]{1,0:T(8,128)(2,1)} %get-tuple-element.115) | copy-start | bytes 1161220
  414.9 55.0 %collective-permute-start.19 = (bf16[1024,896]{1,0:T(8,128)(2,1)}, bf16[1024,896]{1,0:T(8,128)(2,1)}, u32[]{:S(2)}, u32[]{:S(2)}) collective-permute-start(bf16[1024,896]{1,0:T(8,128)(2,1)} %add_convert_fusion), channel_id=1, source_target_pairs={{0,1},{1,0},{2,3},{3,2},{4,5},{5,4},{6,7},{7,6},{8,9},{9,8},{10,11... | collective-permute-start | bytes 5505032 | tf_op jit(solution)/shard_map/ppermute | solution.py:33
  425.0 19.3 %collective-permute-start.25 = (bf16[56,3840]{1,0:T(8,128)(2,1)}, bf16[56,3840]{1,0:T(8,128)(2,1)}, u32[]{:S(2)}, u32[]{:S(2)}) collective-permute-start(bf16[56,3840]{1,0:T(8,128)(2,1)} %get-tuple-element.156), channel_id=1, source_target_pairs={{0,2},{2,4},{4,6},{6,0},{1,3},{3,5},{5,7},{7,1},{8,10},{10,12},{12... | collective-permute-start | bytes 1290248 | tf_op jit(solution)/shard_map/ppermute | solution.py:148
  432.8 27.3 %collective-permute-start.26 = (bf16[56,3840]{1,0:T(8,128)(2,1)}, bf16[56,3840]{1,0:T(8,128)(2,1)}, u32[]{:S(2)}, u32[]{:S(2)}) collective-permute-start(bf16[56,3840]{1,0:T(8,128)(2,1)} %get-tuple-element.158), channel_id=1, source_target_pairs={{0,4},{2,6},{4,0},{6,2},{1,5},{3,7},{5,1},{7,3},{8,12},{10,14},{12... | collective-permute-start | bytes 1290248 | tf_op jit(solution)/shard_map/ppermute | solution.py:148
  432.8 29.2 %collective-permute-start.27 = (bf16[56,3840]{1,0:T(8,128)(2,1)}, bf16[56,3840]{1,0:T(8,128)(2,1)}, u32[]{:S(2)}, u32[]{:S(2)}) collective-permute-start(bf16[56,3840]{1,0:T(8,128)(2,1)} %get-tuple-element.157), channel_id=1, source_target_pairs={{0,6},{2,0},{4,2},{6,4},{1,7},{3,1},{5,3},{7,5},{8,14},{10,8},{12,... | collective-permute-start | bytes 1290248 | tf_op jit(solution)/shard_map/ppermute | solution.py:148
  440.6 38.7 %all-to-all-start.9 = ((bf16[4,56,1024]{2,1,0:T(8,128)(2,1)}), bf16[4,56,1024]{2,1,0:T(8,128)(2,1)S(1)}, u32[]{:S(2)}, u32[]{:S(2)}) async-start(bf16[4,56,1024]{2,1,0:T(8,128)(2,1)} %bitcast.39), calls=%async_computation.9 | async-start | bytes 917504 | tf_op jit(solution)/shard_map/all_to_all | solution.py:50
  480.1 28.0 %all-to-all-start.7 = ((f32[16,1,2368]{2,1,0:T(1,128)}), f32[16,1,2368]{2,1,0:T(1,128)S(1)}, u32[]{:S(2)}, u32[]{:S(2)}) async-start(f32[16,1,2368]{2,1,0:T(1,128)} %broadcast_in_dim.55), calls=%async_computation.7 | async-start | bytes 311296 | tf_op jit(solution)/shard_map/all_to_all | solution.py:50
  (56 other events, 233.3 us)

commit v4 on v2

--- a/solution.py
+++ b/solution.py
@@ -57,16 +57,9 @@
 
 
 def sum_all(v):
-    for axis in ("fsdp", "ctx"):
-        n = lax.axis_size(axis)
-        if n & (n - 1):
-            v = lax.psum(v, axis)
-            continue
-        step = 1
-        while step < n:
-            v = v + lax.ppermute(v, axis, [(i, i ^ step) for i in range(n)])
-            step *= 2
-    return v
+    axes = ("fsdp", "ctx")
+    count = lax.axis_size("fsdp") * lax.axis_size("ctx")
+    return jnp.sum(lax.all_to_all(jnp.broadcast_to(v[None], (count,) + v.shape), axes, 0, 0), 0)
 
 
 def relative_order():
@@ -110,7 +103,15 @@
     return ring_down(total).astype(f32) + v[0].astype(f32)
 
 
-def scatter_plane(pieces):
+def direct_sum(v):
+    n = v.shape[0]
+    total = v[0].astype(f32)
+    for s in range(1, n):
+        total = total + lax.ppermute(v[s], "ctx", [(i, (i - s) % n) for i in range(n)]).astype(f32)
+    return total
+
+
+def scatter_plane(pieces, line_sum=ring_sum):
     if not relative_order():
         return lax.psum_scatter(
             pieces[0], ("fsdp", "ctx"), scatter_dimension=0, tiled=True
@@ -122,7 +123,7 @@
     gx = jnp.concatenate([add_low(gx[:half], r1), gx[half:]], 0)
     gy = jnp.concatenate([gy[:half], add_low(gy[half:], r2)], 0)
     plane = add_low(own, swap_x(gx), swap_y(gy))
-    return ring_sum(plane.reshape(count, -1, own.shape[1]))
+    return line_sum(plane.reshape(count, -1, own.shape[1]))
 
 
 def scatter_line(pieces):
@@ -547,7 +548,9 @@
     projected_grad = jnp.concatenate([turned_back, pack_t[HD:]], 0).astype(bf16)
     bias_grad = jnp.sum(projected_grad.astype(f32), 1)[None]
     qkv_weight_grad = mm(normed, projected_grad, contract_first_last_rows).astype(bf16)
-    attention_total = scatter_plane(row_pieces(jnp.concatenate([qkv_weight_grad, out_weight_grad], 1)))
+    attention_total = scatter_plane(
+        row_pieces(jnp.concatenate([qkv_weight_grad, out_weight_grad], 1)), direct_sum
+    )
 
     normed_one_grad = sum_tp(mm(projected_grad, qkv_full, contract_first_last))
     gain_one_grad = jnp.sum(normed_one_grad * unit_one, 0, keepdims=True)

time: 500 us -> 518 us (1.036)
  waiting for transfers between devices: 147 us -> 175 us
  local copies, waits for them, and re-layouts: 58 us -> 51.4 us
    ppermute x10, starting transfers between devices: 29.2 us -> 8.51 us  [swap_x(): return lax.ppermute(v, 'fsdp', [(i, i ^ 1) for i in range(4)])]
    ppermute x4 -> x3, waiting for transfers between devices: 5.77 us -> 20.2 us  [direct_sum(): lax.ppermute(v[s], 'ctx', [(i, (i - s) % n) for i in range(n)]).astype(f32)]
    ppermute x9 -> x6, starting transfers between devices: 31.1 us -> 39.8 us  [ring_down(): return lax.ppermute(v, 'ctx', [((i + 1) % n, i) for i in range(n)])]
    ppermute x9, waiting for transfers between devices: 38.8 us -> 46.8 us  [ring_up(): return lax.ppermute(v, 'ctx', [(i, (i + 1) % n) for i in range(n)])]
    all_to_all x0 -> x1, starting transfers between devices: none -> 7.51 us  [sum_all(): lax.all_to_all(jnp.broadcast_to(v[None], (count,) + v.shape), axes, 0, 0)]
    ppermute x9 -> x6, waiting for transfers between devices: 16.3 us -> 10.3 us  [ring_down(): return lax.ppermute(v, 'ctx', [((i + 1) % n, i) for i in range(n)])]
    ppermute x10, waiting for transfers between devices: 13.9 us -> 19.5 us  [swap_y(): return lax.ppermute(v, 'fsdp', [(i, i ^ 2) for i in range(4)])]
    convert_element_type x12 -> x10, other arithmetic: 13.9 us -> 9.9 us  [add_low(): return sum((t.astype(f32) for t in terms)).astype(bf16)]
  transfers between devices with their start and end apart: 54 -> 51, of which waited for: 20 -> 21; matrix products, arithmetic and copies ran while one was open for 25% -> 23% of each run, Pallas kernels for 12% -> 11%
where the time goes in v4:
time: 518 us; the launch traced here: 511 us
  waiting for transfers between devices  175 us (34%)
  starting transfers between devices  109 us (21%)
  Pallas kernels  92.5 us (18%)
  other arithmetic  52.8 us (10%)
  local copies, waits for them, and re-layouts  51.4 us (10%)
  matrix products  28.6 us (6%)
    pallas_call x2, Pallas kernels, feed_group(): pl.pallas_call(functools.partial(feed_kernel, starts, width, tile), grid=...  71.5 us
    ppermute x10, waiting for transfers between devices, swap_x(): return lax.ppermute(v, 'fsdp', [(i, i ^ 1) for i in range(4)])  61.2 us
    ppermute x9, waiting for transfers between devices, ring_up(): return lax.ppermute(v, 'ctx', [(i, (i + 1) % n) for i in range(n)])  46.8 us
    ppermute x6, starting transfers between devices, ring_down(): return lax.ppermute(v, 'ctx', [((i + 1) % n, i) for i in range(n)])  39.8 us
    dot_general x11, matrix products, mm(): return lax.dot_general(a, b, dims, preferred_element_type=f32)  27.1 us
    ppermute x9, starting transfers between devices, ring_up(): return lax.ppermute(v, 'ctx', [(i, (i + 1) % n) for i in range(n)])  22.9 us
    unnamed x125, local copies, waits for them, and re-layouts  21.4 us
    ppermute x3, waiting for transfers between devices, direct_sum(): lax.ppermute(v[s], 'ctx', [(i, (i - s) % n) for i in range(n)]).astype(f32)  20.2 us
  transfers between devices with their start and end apart: 51, of which 21 were waited for; matrix products, arithmetic and copies ran while one was open for 23% of the time, Pallas kernels for 11%

profile of v4, /device:TPU:0, one launch (start us, length us, event | category | flops | bytes accessed | tf_op | source)
XLA Modules:
  0.0 511.4 jit_solution(1070031545115789792)
XLA Ops:
  2.5 3.0 collective-permute-start
  8.1 2.5 collective-permute-start.11
  20.3 3.6 fusion.11
  24.2 3.6 convert_bitcast_fusion.refs_1_
  33.0 3.6 collective-permute-done.1
  37.3 5.9 %collective-permute-done.2 = bf16[56,1024]{1,0:T(8,128)(2,1)S(1)} collective-permute-done((bf16[56,1024]{1,0:T(8,128)(2,1)S(1)}, bf16[56,1024]{1,0:T(8,128)(2,1)S(1)}, u32[]{:S(2)}, u32[]{:S(2)}) %collective-permute-start.2) | collective-permute-done | bytes 114720 | tf_op jit(solution)/shard_map/ppermute | solution.py:47
  48.7 11.2 %collective-permute-done.18 = bf16[56,3456]{1,0:T(8,128)(2,1)} collective-permute-done((bf16[56,3456]{1,0:T(8,128)(2,1)}, bf16[56,3456]{1,0:T(8,128)(2,1)}, u32[]{:S(2)}, u32[]{:S(2)}) %collective-permute-start.18) | collective-permute-done | bytes 387104 | tf_op jit(solution)/shard_map/ppermute | solution.py:47
  65.1 2.8 collective-permute-done.5
  73.6 2.7 collective-permute-start.8
  76.3 5.0 collective-permute-start.9
  81.3 3.4 collective-permute-start.7
  89.6 2.1 fusion.92
  91.8 5.3 %collective-permute-start.13 = (bf16[56,7680]{1,0:T(8,128)(2,1)}, bf16[56,7680]{1,0:T(8,128)(2,1)}, u32[]{:S(2)}, u32[]{:S(2)}) collective-permute-start(bf16[56,7680]{1,0:T(8,128)(2,1)} %collective-permute-done.12), channel_id=1, source_target_pairs={{0,2},{2,4},{4,6},{6,0},{1,3},{3,5},{5,7},{7,1},{8,10},{10,12},{12... | collective-permute-start | bytes 2580488 | tf_op jit(solution)/shard_map/ppermute | solution.py:47
  97.0 2.3 collective-permute-done.7
  99.3 2.2 fusion.90
  103.3 9.0 %attend.1 = (bf16[448,1024]{1,0:T(8,128)(2,1)S(1)}, f32[2,8,512]{2,1,0:T(8,128)S(1)}) custom-call(s32[2]{0:T(128)S(1)} %minimum_add_fusion.count_ref, bf16[448,1024]{1,0:T(8,128)(2,1)S(1)} %bitcast.104, s32[2,1,512]{2,1,0:T(1,128)S(1)} %reshape.330.pos_ref, bf16[2,4,512,128]{3,2,1,0:T(8,128)(2,1)S(1)} %copy.72.kv_ref, ...), custom_call_target="tpu_custom_call" | custom-call | flops 15032385536 | bytes 4194304 | tf_op jit(solution)/shard_map/attend/pallas_call | solution.py:265
  114.1 11.4 %collective-permute-start.14 = (bf16[56,7680]{1,0:T(8,128)(2,1)}, bf16[56,7680]{1,0:T(8,128)(2,1)S(1)}, u32[]{:S(2)}, u32[]{:S(2)}) collective-permute-start(bf16[56,7680]{1,0:T(8,128)(2,1)} %collective-permute-done.13), channel_id=1, source_target_pairs={{0,2},{2,4},{4,6},{6,0},{1,3},{3,5},{5,7},{7,1},{8,10},{10,12},{12... | collective-permute-start | bytes 2580488 | tf_op jit(solution)/shard_map/ppermute | solution.py:47
  132.9 25.9 %collective-permute-done.14 = bf16[56,7680]{1,0:T(8,128)(2,1)S(1)} collective-permute-done((bf16[56,7680]{1,0:T(8,128)(2,1)}, bf16[56,7680]{1,0:T(8,128)(2,1)S(1)}, u32[]{:S(2)}, u32[]{:S(2)}) %collective-permute-start.14) | collective-permute-done | bytes 860192 | tf_op jit(solution)/shard_map/ppermute | solution.py:47
  162.4 34.3 %feed.3 = (bf16[1024,896]{1,0:T(8,128)(2,1)}, bf16[1024,896]{1,0:T(8,128)(2,1)}, bf16[224,3456]{1,0:T(8,128)(2,1)S(1)}, bf16[224,3456]{1,0:T(8,128)(2,1)S(1)}, b...) custom-call(bf16[1024,896]{1,0:T(8,128)(2,1)} %multiply_convert_fusion.refs_0_, ...), custom_call_target="tpu_custom_call" | custom-call | flops 19025362944 | bytes 19726336 | tf_op jit(solution)/shard_map/feed/pallas_call | solution.py:380
  203.6 13.3 %collective-permute-done.43 = bf16[112,3456]{1,0:T(8,128)(2,1)S(1)} collective-permute-done((bf16[112,3456]{1,0:T(8,128)(2,1)S(1)}, bf16[112,3456]{1,0:T(8,128)(2,1)S(1)}, u32[]{:S(2)}, u32[]{:S(2)}) %collective-permute-start.43) | collective-permute-done | bytes 774176 | tf_op jit(solution)/shard_map/ppermute | solution.py:42
  218.4 36.8 %collective-permute-done.45 = bf16[112,3456]{1,0:T(8,128)(2,1)S(1)} collective-permute-done((bf16[112,3456]{1,0:T(8,128)(2,1)S(1)}, bf16[112,3456]{1,0:T(8,128)(2,1)S(1)}, u32[]{:S(2)}, u32[]{:S(2)}) %collective-permute-start.45) | collective-permute-done | bytes 774176 | tf_op jit(solution)/shard_map/ppermute | solution.py:38
  259.9 37.2 %feed.2 = (bf16[1024,896]{1,0:T(8,128)(2,1)}, bf16[1024,896]{1,0:T(8,128)(2,1)}, bf16[224,3840]{1,0:T(8,128)(2,1)S(1)}, bf16[224,3840]{1,0:T(8,128)(2,1)S(1)}, b...) custom-call(bf16[1024,896]{1,0:T(8,128)(2,1)} %multiply_convert_fusion.refs_0_, ...), custom_call_target="tpu_custom_call" | custom-call | flops 21139292160 | bytes 21102592 | tf_op jit(solution)/shard_map/feed/pallas_call | solution.py:380
  297.4 2.7 add_convert_fusion
  301.2 2.4 add_convert_fusion.3
  303.7 2.6 collective-permute-start.47
  306.6 2.2 fusion.37
  308.8 6.3 %collective-permute-done.47 = bf16[56,3456]{1,0:T(8,128)(2,1)S(1)} collective-permute-done((bf16[56,3456]{1,0:T(8,128)(2,1)S(1)}, bf16[56,3456]{1,0:T(8,128)(2,1)S(1)}, u32[]{:S(2)}, u32[]{:S(2)}) %collective-permute-start.47) | collective-permute-done | bytes 387104 | tf_op jit(solution)/shard_map/ppermute | solution.py:52
  315.2 4.3 collective-permute-start.48
  319.5 14.0 %collective-permute-done.37 = bf16[224,3840]{1,0:T(8,128)(2,1)S(1)} collective-permute-done((bf16[224,3840]{1,0:T(8,128)(2,1)S(1)}, bf16[224,3840]{1,0:T(8,128)(2,1)S(1)}, u32[]{:S(2)}, u32[]{:S(2)}) %collective-permute-start.37) | collective-permute-done | bytes 1720352 | tf_op jit(solution)/shard_map/ppermute | solution.py:38
  342.7 12.0 %attend_back.1 = (f32[448,1024]{1,0:T(8,128)}, bf16[2,4,512,128]{3,2,1,0:T(8,128)(2,1)S(1)}) custom-call(s32[2]{0:T(128)S(1)} %minimum_add_fusion.count_ref, bf16[448,1024]{1,0:T(8,128)(2,1)S(1)} %bitcast.105, s32[2,1,512]{2,1,0:T(1,128)S(1)} %reshape.330.pos_ref, bf16[2,4,512,128]{3,2,1,0:T(8,128)(2,1)S(1)} %copy.72.kv_ref, ...), custom_call_target="tpu_custom_call" | custom-call | flops 37580963840 | bytes 8388608 | tf_op jit(solution)/shard_map/attend_back/pallas_call | solution.py:294
  360.9 30.2 %collective-permute-start.49 = (bf16[56,3456]{1,0:T(8,128)(2,1)}, bf16[56,3456]{1,0:T(8,128)(2,1)}, u32[]{:S(2)}, u32[]{:S(2)}) collective-permute-start(bf16[56,3456]{1,0:T(8,128)(2,1)} %add_convert_fusion.11), channel_id=1, source_target_pairs={{2,0},{4,2},{6,4},{0,6},{3,1},{5,3},{7,5},{1,7},{10,8},{12,10},{14... | collective-permute-start | bytes 1161224 | tf_op jit(solution)/shard_map/ppermute | solution.py:52
  391.3 11.9 %collective-permute-done.28 = bf16[2,512,128]{2,1,0:T(8,128)(2,1)S(1)} collective-permute-done((bf16[2,512,128]{2,1,0:T(8,128)(2,1)S(1)}, bf16[2,512,128]{2,1,0:T(8,128)(2,1)S(1)}, u32[]{:S(2)}, u32[]{:S(2)}) %collective-permute-start.28) | collective-permute-done | bytes 262176 | tf_op jit(solution)/shard_map/ppermute | solution.py:542
  407.2 2.6 convolution_convert_fusion.2
  409.8 2.6 fusion.57
  412.5 3.1 convolution_convert_fusion
  423.4 2.1 collective-permute-start.33
  427.0 8.8 %collective-permute-done.31 = bf16[224,1024]{0,1:T(8,128)(2,1)S(1)} collective-permute-done((bf16[224,1024]{0,1:T(8,128)(2,1)S(1)}, bf16[224,1024]{0,1:T(8,128)(2,1)S(1)}, u32[]{:S(2)}, u32[]{:S(2)}) %collective-permute-start.31) | collective-permute-done | bytes 458784 | tf_op jit(solution)/shard_map/ppermute | solution.py:38
  435.8 2.1 collective-permute-done.33
  441.4 2.2 slice_reduce_fusion.3
  445.8 10.1 %collective-permute-done.34 = bf16[56,1024]{0,1:T(8,128)(2,1)S(1)} collective-permute-done((bf16[56,1024]{0,1:T(8,128)(2,1)S(1)}, bf16[56,1024]{0,1:T(8,128)(2,1)S(1)}, u32[]{:S(2)}, u32[]{:S(2)}) %collective-permute-start.34) | collective-permute-done | bytes 114720 | tf_op jit(solution)/shard_map/ppermute | solution.py:110
  455.9 10.1 %collective-permute-done.35 = bf16[56,1024]{0,1:T(8,128)(2,1)S(1)} collective-permute-done((bf16[56,1024]{0,1:T(8,128)(2,1)S(1)}, bf16[56,1024]{0,1:T(8,128)(2,1)S(1)}, u32[]{:S(2)}, u32[]{:S(2)}) %collective-permute-start.35) | collective-permute-done | bytes 114720 | tf_op jit(solution)/shard_map/ppermute | solution.py:110
  473.5 4.0 fusion.10
  479.8 7.5 %all-to-all-start = ((f32[16,1,2368]{2,1,0:T(1,128)}), f32[16,1,2368]{2,1,0:T(1,128)}, u32[]{:S(2)}, u32[]{:S(2)}) async-start(f32[16,1,2368]{2,1,0:T(1,128)} %broadcast_in_dim.16), calls=%async_computation | async-start | bytes 311296 | tf_op jit(solution)/shard_map/all_to_all | solution.py:62
  487.3 4.0 collective-permute-done.41
  494.1 5.2 %fusion.28 = bf16[1024,896]{1,0:T(8,128)(2,1)S(1)} fusion(f32[1024,896]{1,0:T(8,128)S(1)} %copy-done.8, bf16[896,1024]{0,1:T(8,128)(2,1)S(1)} %copy-done.12, bf16[1024,896]{1,0:T(8,128)(2,1)} %collective-permute-done.29, bf16[1024,896]{1,0:T(8,128)(2,1)} %convolution_convert_fusion, f32[1024]{0:T(1024)S(1)} %broadcast_multiply_fusion, ...), kind=kOutput, calls=%fused_computation.66 | convolution fusion | flops 1655980032 | bytes 11025408 | tf_op jit(solution)/shard_map/dot_general | solution.py:24
  499.3 2.1 convert.35
  503.6 2.1 collective-permute-done.42
  506.3 2.3 slice_reduce_fusion
  (312 shorter events, 122.3 us)
Async XLA Ops:
  2.5 27.2 %collective-permute-start = (bf16[56,1024]{1,0:T(8,128)(2,1)}, bf16[56,1024]{1,0:T(8,128)(2,1)}, u32[]{:S(2)}, u32[]{:S(2)}) collective-permute-start(bf16[56,1024]{1,0:T(8,128)(2,1)} %get-tuple-element.101), channel_id=1, source_target_pairs={{0,2},{2,4},{4,6},{6,0},{1,3},{3,5},{5,7},{7,1},{8,10},{10,12},{12... | collective-permute-start | bytes 344072 | tf_op jit(solution)/shard_map/ppermute | solution.py:47
  8.1 39.7 %collective-permute-start.11 = (bf16[56,3840]{1,0:T(8,128)(2,1)S(1)}, bf16[56,3840]{1,0:T(8,128)(2,1)S(1)}, u32[]{:S(2)}, u32[]{:S(2)}) collective-permute-start(bf16[56,3840]{1,0:T(8,128)(2,1)S(1)} %bitcast.114), channel_id=1, source_target_pairs={{0,24},{8,16},{16,8},{24,0},{1,25},{9,17},{17,9},{25,1},{2,26},{10... | collective-permute-start | bytes 1290248 | tf_op jit(solution)/shard_map/ppermute | solution.py:56
  16.9 29.1 %collective-permute-start.17 = (bf16[56,3456]{1,0:T(8,128)(2,1)}, bf16[56,3456]{1,0:T(8,128)(2,1)}, u32[]{:S(2)}, u32[]{:S(2)}) collective-permute-start(bf16[56,3456]{1,0:T(8,128)(2,1)} %bitcast.36), channel_id=1, source_target_pairs={{0,2},{2,4},{4,6},{6,0},{1,3},{3,5},{5,7},{7,1},{8,10},{10,12},{12... | collective-permute-start | bytes 1161224 | tf_op jit(solution)/shard_map/ppermute | solution.py:47
  29.7 6.9 %collective-permute-start.1 = (bf16[56,1024]{1,0:T(8,128)(2,1)}, bf16[56,1024]{1,0:T(8,128)(2,1)S(1)}, u32[]{:S(2)}, u32[]{:S(2)}) collective-permute-start(bf16[56,1024]{1,0:T(8,128)(2,1)} %collective-permute-done), channel_id=1, source_target_pairs={{0,2},{2,4},{4,6},{6,0},{1,3},{3,5},{5,7},{7,1},{8,10},{10,12},{12... | collective-permute-start | bytes 344072 | tf_op jit(solution)/shard_map/ppermute | solution.py:47
  36.6 6.6 %collective-permute-start.2 = (bf16[56,1024]{1,0:T(8,128)(2,1)S(1)}, bf16[56,1024]{1,0:T(8,128)(2,1)S(1)}, u32[]{:S(2)}, u32[]{:S(2)}) collective-permute-start(bf16[56,1024]{1,0:T(8,128)(2,1)S(1)} %collective-permute-done.1), channel_id=1, source_target_pairs={{0,2},{2,4},{4,6},{6,0},{1,3},{3,5},{5,7},{7,1},{8,10},{10,12},{12... | collective-permute-start | bytes 344072 | tf_op jit(solution)/shard_map/ppermute | solution.py:47
  44.2 17.6 %collective-permute-start.3 = (bf16[224,1024]{1,0:T(8,128)(2,1)S(1)}, bf16[224,1024]{1,0:T(8,128)(2,1)S(1)}, u32[]{:S(2)}, u32[]{:S(2)}) collective-permute-start(bf16[224,1024]{1,0:T(8,128)(2,1)S(1)} %pad_maximum_fusion.17), channel_id=1, source_target_pairs={{0,8},{8,0},{16,24},{24,16},{1,9},{9,1},{17,25},{25,17},{2,10},{10... | collective-permute-start | bytes 1376264 | tf_op jit(solution)/shard_map/ppermute | solution.py:38
  44.8 18.6 %collective-permute-start.4 = (bf16[224,1024]{1,0:T(8,128)(2,1)S(1)}, bf16[224,1024]{1,0:T(8,128)(2,1)S(1)}, u32[]{:S(2)}, u32[]{:S(2)}) collective-permute-start(bf16[224,1024]{1,0:T(8,128)(2,1)S(1)} %pad_maximum_fusion.17), channel_id=1, source_target_pairs={{0,16},{8,24},{16,0},{24,8},{1,17},{9,25},{17,1},{25,9},{2,18},{10... | collective-permute-start | bytes 1376264 | tf_op jit(solution)/shard_map/ppermute | solution.py:42
  46.0 14.0 %collective-permute-start.18 = (bf16[56,3456]{1,0:T(8,128)(2,1)}, bf16[56,3456]{1,0:T(8,128)(2,1)}, u32[]{:S(2)}, u32[]{:S(2)}) collective-permute-start(bf16[56,3456]{1,0:T(8,128)(2,1)} %collective-permute-done.17), channel_id=1, source_target_pairs={{0,2},{2,4},{4,6},{6,0},{1,3},{3,5},{5,7},{7,1},{8,10},{10,12},{12... | collective-permute-start | bytes 1161224 | tf_op jit(solution)/shard_map/ppermute | solution.py:47
  48.7 40.4 %collective-permute-start.12 = (bf16[56,7680]{1,0:T(8,128)(2,1)}, bf16[56,7680]{1,0:T(8,128)(2,1)}, u32[]{:S(2)}, u32[]{:S(2)}) collective-permute-start(bf16[56,7680]{1,0:T(8,128)(2,1)} %pad_maximum_fusion.9), channel_id=1, source_target_pairs={{0,2},{2,4},{4,6},{6,0},{1,3},{3,5},{5,7},{7,1},{8,10},{10,12},{12... | collective-permute-start | bytes 2580488 | tf_op jit(solution)/shard_map/ppermute | solution.py:47
  60.0 25.8 %collective-permute-start.19 = (bf16[56,3456]{1,0:T(8,128)(2,1)}, bf16[56,3456]{1,0:T(8,128)(2,1)}, u32[]{:S(2)}, u32[]{:S(2)}) collective-permute-start(bf16[56,3456]{1,0:T(8,128)(2,1)} %collective-permute-done.18), channel_id=1, source_target_pairs={{0,2},{2,4},{4,6},{6,0},{1,3},{3,5},{5,7},{7,1},{8,10},{10,12},{12... | collective-permute-start | bytes 1161224 | tf_op jit(solution)/shard_map/ppermute | solution.py:47
  73.6 18.1 %collective-permute-start.8 = (bf16[2,512,128]{1,2,0:T(8,128)(2,1)}, bf16[2,512,128]{1,2,0:T(8,128)(2,1)}, u32[]{:S(2)}, u32[]{:S(2)}) collective-permute-start(bf16[2,512,128]{1,2,0:T(8,128)(2,1)} %copy.68), channel_id=1, source_target_pairs={{0,4},{2,6},{1,5},{3,7},{8,12},{10,14},{9,13},{11,15},{16,20},{18,... | collective-permute-start | bytes 786440 | tf_op jit(solution)/shard_map/ppermute | solution.py:489
  76.3 20.7 %collective-permute-start.9 = (bf16[2,512,128]{1,2,0:T(8,128)(2,1)}, bf16[2,512,128]{1,2,0:T(8,128)(2,1)}, u32[]{:S(2)}, u32[]{:S(2)}) collective-permute-start(bf16[2,512,128]{1,2,0:T(8,128)(2,1)} %copy.68), channel_id=1, source_target_pairs={{0,6},{1,7},{8,14},{9,15},{16,22},{17,23},{24,30},{25,31}} | collective-permute-start | bytes 786440 | tf_op jit(solution)/shard_map/ppermute | solution.py:489
  81.3 18.0 %collective-permute-start.7 = (bf16[2,512,128]{1,2,0:T(8,128)(2,1)}, bf16[2,512,128]{1,2,0:T(8,128)(2,1)}, u32[]{:S(2)}, u32[]{:S(2)}) collective-permute-start(bf16[2,512,128]{1,2,0:T(8,128)(2,1)} %copy.68), channel_id=1, source_target_pairs={{0,2},{2,4},{4,6},{1,3},{3,5},{5,7},{8,10},{10,12},{12,14},{9,11},... | collective-permute-start | bytes 786440 | tf_op jit(solution)/shard_map/ppermute | solution.py:489
  87.6 39.7 %collective-permute-start.20 = (bf16[224,3456]{1,0:T(8,128)(2,1)}, bf16[224,3456]{1,0:T(8,128)(2,1)}, u32[]{:S(2)}, u32[]{:S(2)}) collective-permute-start(bf16[224,3456]{1,0:T(8,128)(2,1)} %constant_dynamic-update-slice_fusion.8.refs_2_), channel_id=1, source_target_pairs={{0,8},{8,0},{16,24},{24,16},{1,9},{9,1},{17,25},{25,17},{2,10},{10... | collective-permute-start | bytes 4644872 | tf_op jit(solution)/shard_map/ppermute | solution.py:38
  89.1 41.0 %collective-permute-start.21 = (bf16[224,3456]{1,0:T(8,128)(2,1)}, bf16[224,3456]{1,0:T(8,128)(2,1)}, u32[]{:S(2)}, u32[]{:S(2)}) collective-permute-start(bf16[224,3456]{1,0:T(8,128)(2,1)} %constant_dynamic-update-slice_fusion.8.refs_2_), channel_id=1, source_target_pairs={{0,16},{8,24},{16,0},{24,8},{1,17},{9,25},{17,1},{25,9},{2,18},{10... | collective-permute-start | bytes 4644872 | tf_op jit(solution)/shard_map/ppermute | solution.py:42
  91.8 22.3 %collective-permute-start.13 = (bf16[56,7680]{1,0:T(8,128)(2,1)}, bf16[56,7680]{1,0:T(8,128)(2,1)}, u32[]{:S(2)}, u32[]{:S(2)}) collective-permute-start(bf16[56,7680]{1,0:T(8,128)(2,1)} %collective-permute-done.12), channel_id=1, source_target_pairs={{0,2},{2,4},{4,6},{6,0},{1,3},{3,5},{5,7},{7,1},{8,10},{10,12},{12... | collective-permute-start | bytes 2580488 | tf_op jit(solution)/shard_map/ppermute | solution.py:47
  114.0 45.9 %collective-permute-start.10 = (bf16[1024,896]{1,0:T(8,128)(2,1)S(1)}, bf16[1024,896]{1,0:T(8,128)(2,1)S(1)}, u32[]{:S(2)}, u32[]{:S(2)}) collective-permute-start(bf16[1024,896]{1,0:T(8,128)(2,1)S(1)} %convolution_convert_fusion.1), channel_id=1, source_target_pairs={{0,1},{1,0},{2,3},{3,2},{4,5},{5,4},{6,7},{7,6},{8,9},{9,8},{10,11... | collective-permute-start | bytes 5505032 | tf_op jit(solution)/shard_map/ppermute | solution.py:29
  114.1 44.8 %collective-permute-start.14 = (bf16[56,7680]{1,0:T(8,128)(2,1)}, bf16[56,7680]{1,0:T(8,128)(2,1)S(1)}, u32[]{:S(2)}, u32[]{:S(2)}) collective-permute-start(bf16[56,7680]{1,0:T(8,128)(2,1)} %collective-permute-done.13), channel_id=1, source_target_pairs={{0,2},{2,4},{4,6},{6,0},{1,3},{3,5},{5,7},{7,1},{8,10},{10,12},{12... | collective-permute-start | bytes 2580488 | tf_op jit(solution)/shard_map/ppermute | solution.py:47
  128.6 33.8 %collective-permute-start.22 = (bf16[112,3456]{1,0:T(8,128)(2,1)S(1)}, bf16[112,3456]{1,0:T(8,128)(2,1)S(1)}, u32[]{:S(2)}, u32[]{:S(2)}) collective-permute-start(bf16[112,3456]{1,0:T(8,128)(2,1)S(1)} %slice.334), channel_id=1, source_target_pairs={{0,16},{8,24},{16,0},{24,8},{1,17},{9,25},{17,1},{25,9},{2,18},{10... | collective-permute-start | bytes 2322440 | tf_op jit(solution)/shard_map/ppermute | solution.py:42
  131.3 31.0 %collective-permute-start.23 = (bf16[112,3456]{1,0:T(8,128)(2,1)S(1)}, bf16[112,3456]{1,0:T(8,128)(2,1)S(1)}, u32[]{:S(2)}, u32[]{:S(2)}) collective-permute-start(bf16[112,3456]{1,0:T(8,128)(2,1)S(1)} %slice.335), channel_id=1, source_target_pairs={{0,8},{8,0},{16,24},{24,16},{1,9},{9,1},{17,25},{25,17},{2,10},{10... | collective-permute-start | bytes 2322440 | tf_op jit(solution)/shard_map/ppermute | solution.py:38
  196.7 20.2 %collective-permute-start.43 = (bf16[112,3456]{1,0:T(8,128)(2,1)S(1)}, bf16[112,3456]{1,0:T(8,128)(2,1)S(1)}, u32[]{:S(2)}, u32[]{:S(2)}) collective-permute-start(bf16[112,3456]{1,0:T(8,128)(2,1)S(1)} %get-tuple-element.41), channel_id=1, source_target_pairs={{0,16},{8,24},{16,0},{24,8},{1,17},{9,25},{17,1},{25,9},{2,18},{10... | collective-permute-start | bytes 2322440 | tf_op jit(solution)/shard_map/ppermute | solution.py:42
  198.1 60.5 %collective-permute-start.15 = (bf16[224,3840]{1,0:T(8,128)(2,1)S(1)}, bf16[224,3840]{1,0:T(8,128)(2,1)S(1)}, u32[]{:S(2)}, u32[]{:S(2)}) collective-permute-start(bf16[224,3840]{1,0:T(8,128)(2,1)S(1)} %pad_maximum_fusion.1.refs_2_), channel_id=1, source_target_pairs={{0,8},{8,0},{16,24},{24,16},{1,9},{9,1},{17,25},{25,17},{2,10},{10... | collective-permute-start | bytes 5160968 | tf_op jit(solution)/shard_map/ppermute | solution.py:38
  198.2 61.7 %collective-permute-start.16 = (bf16[224,3840]{1,0:T(8,128)(2,1)S(1)}, bf16[224,3840]{1,0:T(8,128)(2,1)}, u32[]{:S(2)}, u32[]{:S(2)}) collective-permute-start(bf16[224,3840]{1,0:T(8,128)(2,1)S(1)} %pad_maximum_fusion.1.refs_2_), channel_id=1, source_target_pairs={{0,16},{8,24},{16,0},{24,8},{1,17},{9,25},{17,1},{25,9},{2,18},{10... | collective-permute-start | bytes 5160968 | tf_op jit(solution)/shard_map/ppermute | solution.py:42
  201.6 53.7 %collective-permute-start.45 = (bf16[112,3456]{1,0:T(8,128)(2,1)S(1)}, bf16[112,3456]{1,0:T(8,128)(2,1)S(1)}, u32[]{:S(2)}, u32[]{:S(2)}) collective-permute-start(bf16[112,3456]{1,0:T(8,128)(2,1)S(1)} %get-tuple-element.43), channel_id=1, source_target_pairs={{0,8},{8,0},{16,24},{24,16},{1,9},{9,1},{17,25},{25,17},{2,10},{10... | collective-permute-start | bytes 2322440 | tf_op jit(solution)/shard_map/ppermute | solution.py:38
  218.4 82.6 %collective-permute-start.44 = (bf16[224,3456]{1,0:T(8,128)(2,1)}, bf16[224,3456]{1,0:T(8,128)(2,1)}, u32[]{:S(2)}, u32[]{:S(2)}) collective-permute-start(bf16[224,3456]{1,0:T(8,128)(2,1)} %pad_maximum_fusion.3), channel_id=1, source_target_pairs={{0,8},{8,0},{16,24},{24,16},{1,9},{9,1},{17,25},{25,17},{2,10},{10... | collective-permute-start | bytes 4644872 | tf_op jit(solution)/shard_map/ppermute | solution.py:38
  256.7 44.5 %collective-permute-start.46 = (bf16[224,3456]{1,0:T(8,128)(2,1)}, bf16[224,3456]{1,0:T(8,128)(2,1)}, u32[]{:S(2)}, u32[]{:S(2)}) collective-permute-start(bf16[224,3456]{1,0:T(8,128)(2,1)} %pad_maximum_fusion.4), channel_id=1, source_target_pairs={{0,16},{8,24},{16,0},{24,8},{1,17},{9,25},{17,1},{25,9},{2,18},{10... | collective-permute-start | bytes 4644872 | tf_op jit(solution)/shard_map/ppermute | solution.py:42
  297.1 36.4 %collective-permute-start.37 = (bf16[224,3840]{1,0:T(8,128)(2,1)S(1)}, bf16[224,3840]{1,0:T(8,128)(2,1)S(1)}, u32[]{:S(2)}, u32[]{:S(2)}) collective-permute-start(bf16[224,3840]{1,0:T(8,128)(2,1)S(1)} %get-tuple-element.36), channel_id=1, source_target_pairs={{0,8},{8,0},{16,24},{24,16},{1,9},{9,1},{17,25},{25,17},{2,10},{10... | collective-permute-start | bytes 5160968 | tf_op jit(solution)/shard_map/ppermute | solution.py:38
  297.2 36.7 %collective-permute-start.38 = (bf16[224,3840]{1,0:T(8,128)(2,1)S(1)}, bf16[224,3840]{1,0:T(8,128)(2,1)S(1)}, u32[]{:S(2)}, u32[]{:S(2)}) collective-permute-start(bf16[224,3840]{1,0:T(8,128)(2,1)S(1)} %get-tuple-element.37), channel_id=1, source_target_pairs={{0,16},{8,24},{16,0},{24,8},{1,17},{9,25},{17,1},{25,9},{2,18},{10... | collective-permute-start | bytes 5160968 | tf_op jit(solution)/shard_map/ppermute | solution.py:42
  300.0 37.6 %collective-permute-start.25 = (bf16[1024,896]{1,0:T(8,128)(2,1)S(1)}, bf16[1024,896]{1,0:T(8,128)(2,1)S(1)}, u32[]{:S(2)}, u32[]{:S(2)}) collective-permute-start(bf16[1024,896]{1,0:T(8,128)(2,1)S(1)} %add_convert_fusion), channel_id=1, source_target_pairs={{0,1},{1,0},{2,3},{3,2},{4,5},{5,4},{6,7},{7,6},{8,9},{9,8},{10,11... | collective-permute-start | bytes 5505032 | tf_op jit(solution)/shard_map/ppermute | solution.py:29
  303.7 11.4 %collective-permute-start.47 = (bf16[56,3456]{1,0:T(8,128)(2,1)S(1)}, bf16[56,3456]{1,0:T(8,128)(2,1)S(1)}, u32[]{:S(2)}, u32[]{:S(2)}) collective-permute-start(bf16[56,3456]{1,0:T(8,128)(2,1)S(1)} %slice.374), channel_id=1, source_target_pairs={{2,0},{4,2},{6,4},{0,6},{3,1},{5,3},{7,5},{1,7},{10,8},{12,10},{14... | collective-permute-start | bytes 1161224 | tf_op jit(solution)/shard_map/ppermute | solution.py:52
  315.2 44.6 %collective-permute-start.48 = (bf16[56,3456]{1,0:T(8,128)(2,1)S(1)}, bf16[56,3456]{1,0:T(8,128)(2,1)S(1)}, u32[]{:S(2)}, u32[]{:S(2)}) collective-permute-start(bf16[56,3456]{1,0:T(8,128)(2,1)S(1)} %add_convert_fusion.12), channel_id=1, source_target_pairs={{2,0},{4,2},{6,4},{0,6},{3,1},{5,3},{7,5},{1,7},{10,8},{12,10},{14... | collective-permute-start | bytes 1161224 | tf_op jit(solution)/shard_map/ppermute | solution.py:52
  336.3 89.2 %collective-permute-start.39 = (bf16[56,7680]{1,0:T(8,128)(2,1)}, bf16[56,7680]{1,0:T(8,128)(2,1)}, u32[]{:S(2)}, u32[]{:S(2)}) collective-permute-start(bf16[56,7680]{1,0:T(8,128)(2,1)} %fusion.46), channel_id=1, source_target_pairs={{2,0},{4,2},{6,4},{0,6},{3,1},{5,3},{7,5},{1,7},{10,8},{12,10},{14... | collective-permute-start | bytes 2580488 | tf_op jit(solution)/shard_map/ppermute | solution.py:52
  354.8 36.3 %collective-permute-start.26 = (bf16[2,512,128]{2,1,0:T(8,128)(2,1)S(1)}, bf16[2,512,128]{2,1,0:T(8,128)(2,1)S(1)}, u32[]{:S(2)}, u32[]{:S(2)}) collective-permute-start(bf16[2,512,128]{2,1,0:T(8,128)(2,1)S(1)} %get-tuple-element.112), channel_id=1, source_target_pairs={{2,0},{4,2},{6,4},{3,1},{5,3},{7,5},{10,8},{12,10},{14,12},{11,9},... | collective-permute-start | bytes 786440 | tf_op jit(solution)/shard_map/ppermute | solution.py:542
  356.1 35.3 %collective-permute-start.27 = (bf16[2,512,128]{2,1,0:T(8,128)(2,1)S(1)}, bf16[2,512,128]{2,1,0:T(8,128)(2,1)S(1)}, u32[]{:S(2)}, u32[]{:S(2)}) collective-permute-start(bf16[2,512,128]{2,1,0:T(8,128)(2,1)S(1)} %get-tuple-element.113), channel_id=1, source_target_pairs={{4,0},{6,2},{5,1},{7,3},{12,8},{14,10},{13,9},{15,11},{20,16},{22,... | collective-permute-start | bytes 786440 | tf_op jit(solution)/shard_map/ppermute | solution.py:542
  357.4 45.9 %collective-permute-start.28 = (bf16[2,512,128]{2,1,0:T(8,128)(2,1)S(1)}, bf16[2,512,128]{2,1,0:T(8,128)(2,1)S(1)}, u32[]{:S(2)}, u32[]{:S(2)}) collective-permute-start(bf16[2,512,128]{2,1,0:T(8,128)(2,1)S(1)} %slice_bitcast_fusion.4), channel_id=1, source_target_pairs={{6,0},{7,1},{14,8},{15,9},{22,16},{23,17},{30,24},{31,25}} | collective-permute-start | bytes 786440 | tf_op jit(solution)/shard_map/ppermute | solution.py:542
  360.9 54.9 %collective-permute-start.49 = (bf16[56,3456]{1,0:T(8,128)(2,1)}, bf16[56,3456]{1,0:T(8,128)(2,1)}, u32[]{:S(2)}, u32[]{:S(2)}) collective-permute-start(bf16[56,3456]{1,0:T(8,128)(2,1)} %add_convert_fusion.11), channel_id=1, source_target_pairs={{2,0},{4,2},{6,4},{0,6},{3,1},{5,3},{7,5},{1,7},{10,8},{12,10},{14... | collective-permute-start | bytes 1161224 | tf_op jit(solution)/shard_map/ppermute | solution.py:52
  412.4 6.7 %collective-permute-start.30 = (bf16[112,1024]{0,1:T(8,128)(2,1)}, bf16[112,1024]{0,1:T(8,128)(2,1)}, u32[]{:S(2)}, u32[]{:S(2)}) collective-permute-start(bf16[112,1024]{0,1:T(8,128)(2,1)} %get-tuple-element.108), channel_id=1, source_target_pairs={{0,16},{8,24},{16,0},{24,8},{1,17},{9,25},{17,1},{25,9},{2,18},{10... | collective-permute-start | bytes 688136 | tf_op jit(solution)/shard_map/ppermute | solution.py:42
  412.4 6.7 %collective-permute-start.32 = (bf16[112,1024]{0,1:T(8,128)(2,1)}, bf16[112,1024]{0,1:T(8,128)(2,1)}, u32[]{:S(2)}, u32[]{:S(2)}) collective-permute-start(bf16[112,1024]{0,1:T(8,128)(2,1)} %get-tuple-element.111), channel_id=1, source_target_pairs={{0,8},{8,0},{16,24},{24,16},{1,9},{9,1},{17,25},{25,17},{2,10},{10... | collective-permute-start | bytes 688136 | tf_op jit(solution)/shard_map/ppermute | solution.py:38
  415.5 57.9 %collective-permute-start.29 = (bf16[1024,896]{1,0:T(8,128)(2,1)}, bf16[1024,896]{1,0:T(8,128)(2,1)}, u32[]{:S(2)}, u32[]{:S(2)}) collective-permute-start(bf16[1024,896]{1,0:T(8,128)(2,1)} %convolution_convert_fusion), channel_id=1, source_target_pairs={{0,1},{1,0},{2,3},{3,2},{4,5},{5,4},{6,7},{7,6},{8,9},{9,8},{10,11... | collective-permute-start | bytes 5505032 | tf_op jit(solution)/shard_map/ppermute | solution.py:29
  422.0 13.7 %collective-permute-start.31 = (bf16[224,1024]{0,1:T(8,128)(2,1)S(1)}, bf16[224,1024]{0,1:T(8,128)(2,1)S(1)}, u32[]{:S(2)}, u32[]{:S(2)}) collective-permute-start(bf16[224,1024]{0,1:T(8,128)(2,1)S(1)} %pad_maximum_fusion.14), channel_id=1, source_target_pairs={{0,8},{8,0},{16,24},{24,16},{1,9},{9,1},{17,25},{25,17},{2,10},{10... | collective-permute-start | bytes 1376264 | tf_op jit(solution)/shard_map/ppermute | solution.py:38
  423.4 14.4 %collective-permute-start.33 = (bf16[224,1024]{0,1:T(8,128)(2,1)S(1)}, bf16[224,1024]{0,1:T(8,128)(2,1)S(1)}, u32[]{:S(2)}, u32[]{:S(2)}) collective-permute-start(bf16[224,1024]{0,1:T(8,128)(2,1)S(1)} %pad_maximum_fusion.15), channel_id=1, source_target_pairs={{0,16},{8,24},{16,0},{24,8},{1,17},{9,25},{17,1},{25,9},{2,18},{10... | collective-permute-start | bytes 1376264 | tf_op jit(solution)/shard_map/ppermute | solution.py:42
  426.9 39.2 %collective-permute-start.40 = (bf16[56,7680]{1,0:T(8,128)(2,1)S(1)}, bf16[56,7680]{1,0:T(8,128)(2,1)S(1)}, u32[]{:S(2)}, u32[]{:S(2)}) collective-permute-start(bf16[56,7680]{1,0:T(8,128)(2,1)S(1)} %add_convert_fusion.6), channel_id=1, source_target_pairs={{2,0},{4,2},{6,4},{0,6},{3,1},{5,3},{7,5},{1,7},{10,8},{12,10},{14... | collective-permute-start | bytes 2580488 | tf_op jit(solution)/shard_map/ppermute | solution.py:52
  439.3 16.6 %collective-permute-start.34 = (bf16[56,1024]{0,1:T(8,128)(2,1)S(1)}, bf16[56,1024]{0,1:T(8,128)(2,1)S(1)}, u32[]{:S(2)}, u32[]{:S(2)}) collective-permute-start(bf16[56,1024]{0,1:T(8,128)(2,1)S(1)} %get-tuple-element.124), channel_id=1, source_target_pairs={{0,6},{2,0},{4,2},{6,4},{1,7},{3,1},{5,3},{7,5},{8,14},{10,8},{12,... | collective-permute-start | bytes 344072 | tf_op jit(solution)/shard_map/ppermute | solution.py:110
  439.4 26.6 %collective-permute-start.35 = (bf16[56,1024]{0,1:T(8,128)(2,1)S(1)}, bf16[56,1024]{0,1:T(8,128)(2,1)S(1)}, u32[]{:S(2)}, u32[]{:S(2)}) collective-permute-start(bf16[56,1024]{0,1:T(8,128)(2,1)S(1)} %get-tuple-element.126), channel_id=1, source_target_pairs={{0,4},{2,6},{4,0},{6,2},{1,5},{3,7},{5,1},{7,3},{8,12},{10,14},{12... | collective-permute-start | bytes 344072 | tf_op jit(solution)/shard_map/ppermute | solution.py:110
  439.4 26.5 %collective-permute-start.36 = (bf16[56,1024]{0,1:T(8,128)(2,1)S(1)}, bf16[56,1024]{0,1:T(8,128)(2,1)S(1)}, u32[]{:S(2)}, u32[]{:S(2)}) collective-permute-start(bf16[56,1024]{0,1:T(8,128)(2,1)S(1)} %get-tuple-element.125), channel_id=1, source_target_pairs={{0,2},{2,4},{4,6},{6,0},{1,3},{3,5},{5,7},{7,1},{8,10},{10,12},{12... | collective-permute-start | bytes 344072 | tf_op jit(solution)/shard_map/ppermute | solution.py:110
  467.2 24.1 %collective-permute-start.41 = (bf16[56,7680]{1,0:T(8,128)(2,1)}, bf16[56,7680]{1,0:T(8,128)(2,1)}, u32[]{:S(2)}, u32[]{:S(2)}) collective-permute-start(bf16[56,7680]{1,0:T(8,128)(2,1)} %add_convert_fusion.5), channel_id=1, source_target_pairs={{2,0},{4,2},{6,4},{0,6},{3,1},{5,3},{7,5},{1,7},{10,8},{12,10},{14... | collective-permute-start | bytes 2580488 | tf_op jit(solution)/shard_map/ppermute | solution.py:52
  479.8 21.6 %all-to-all-start = ((f32[16,1,2368]{2,1,0:T(1,128)}), f32[16,1,2368]{2,1,0:T(1,128)}, u32[]{:S(2)}, u32[]{:S(2)}) async-start(f32[16,1,2368]{2,1,0:T(1,128)} %broadcast_in_dim.16), calls=%async_computation | async-start | bytes 311296 | tf_op jit(solution)/shard_map/all_to_all | solution.py:62
  493.9 11.8 %collective-permute-start.42 = (bf16[56,3840]{1,0:T(8,128)(2,1)S(1)}, bf16[56,3840]{1,0:T(8,128)(2,1)S(1)}, u32[]{:S(2)}, u32[]{:S(2)}) collective-permute-start(bf16[56,3840]{1,0:T(8,128)(2,1)S(1)} %slice.500), channel_id=1, source_target_pairs={{0,24},{8,16},{16,8},{24,0},{1,25},{9,17},{17,9},{25,1},{2,26},{10... | collective-permute-start | bytes 1290248 | tf_op jit(solution)/shard_map/ppermute | solution.py:56
  (56 other events, 474.6 us)
